TPU v7x, 512 devices: a whole 4x8x8 slice. The times are simulated.
512 devices in a mesh: grp: 8 (over z), mem: 64 (over y, x, core).
Axes of the slice: x: 4, y: 8, z: 8, core: 2. Of those that a mesh axis runs over, the one named last changes fastest.
Arguments:
- phi_owned: float32 [8, 8, 8, 65536], P(None, None, None, ('grp', 'mem')), may hold values from -6 to 6
- band_counts: int32 [8, 64], P('grp'), may hold values from 1 to 128, 2048 in all within a row
- neighbours: int32 [8, 6, 2048], P('grp'), may hold values from -1 to 16383, as said below
Outputs:
- phi_new: float32 [8, 8, 8, 65536], P(None, None, None, ('grp', 'mem'))
Inputs may be any that keep to these rules, and one draw needn't show every extreme that they name: `band_counts`: in every group the counts sum to 2048, each is at least 1, and the largest is exactly 128. `neighbours`: tile k of a group lies at column k mod 64 and row k // 64 of the group's tile sheet. An entry is -1 (no neighbour) or the id of the tile across that face: tile k - 1, k + 1, k - 64, k + 64 of the same group for faces 0 to 3 (never across an edge of the sheet), tile k of group g - 1 or g + 1 for faces 4 and 5. Links are mutual.
All inputs are finite; a program needn't handle non-finite values.
Results may differ from a plain program's by a relative error of at most 0.0003.
Values sent between devices are 32-bit elements; how exact they have to be, the bound alone decides.
No kernel may reach another device: no remote copies, remote signals or barrier semaphores. Data moves between devices by JAX's collectives and lax.ppermute only.
A program may use at most 64 MiB of HBM per device.

v0:
```python
import jax
import jax.numpy as jnp
from jax import lax
from jax.sharding import PartitionSpec as P

STEPS = 4


TIME_STEP = 0.5
EPSILON = 1e-06


def with_halo(x, sides, width):
    for axis, dim in sides:
        devices, length = (lax.axis_size(axis), x.shape[dim])
        up = [(i, (i + 1) % devices) for i in range(devices - 1)]
        down = [(j, i) for i, j in up]
        last = lax.slice_in_dim(x, length - width, length, axis=dim)
        leading = lax.slice_in_dim(x, 0, width, axis=dim)
        before = lax.ppermute(last, axis, up)
        after = lax.ppermute(leading, axis, down)
        x = jnp.concatenate([before, x, after], axis=dim)
    return x


def upwind(backward, forward, positive):
    rising = jnp.maximum(
        jnp.square(jnp.maximum(backward, 0.0)), jnp.square(jnp.minimum(forward, 0.0))
    )
    falling = jnp.maximum(
        jnp.square(jnp.minimum(backward, 0.0)), jnp.square(jnp.maximum(forward, 0.0))
    )
    return jnp.where(positive, rising, falling)


def advance(level_set, sign_field, ghosts, present, slots):
    tile_edge = level_set.shape[0]
    positive = sign_field > 0
    wide_mask = [jnp.tile(present[face_index], tile_edge) for face_index in range(4)]
    below_x = jnp.where(wide_mask[0], ghosts[0], level_set[0])
    above_x = jnp.where(wide_mask[1], ghosts[1], level_set[tile_edge - 1])
    extended = jnp.concatenate([below_x[None], level_set, above_x[None]], axis=0)
    squares = upwind(level_set - extended[:tile_edge], extended[2:] - level_set, positive)
    below_y = jnp.where(wide_mask[2], ghosts[2], level_set[:, 0])
    above_y = jnp.where(wide_mask[3], ghosts[3], level_set[:, tile_edge - 1])
    extended = jnp.concatenate([below_y[:, None], level_set, above_y[:, None]], axis=1)
    squares = squares + upwind(
        level_set - extended[:, :tile_edge], extended[:, 2:] - level_set, positive
    )
    below_z = jnp.where(present[4], ghosts[4], level_set[:, :, :slots])
    above_z = jnp.where(present[5], ghosts[5], level_set[:, :, -slots:])
    backward = level_set - jnp.concatenate([below_z, level_set[:, :, :-slots]], axis=2)
    forward = jnp.concatenate([level_set[:, :, slots:], above_z], axis=2) - level_set
    squares = squares + upwind(backward, forward, positive)
    return level_set - TIME_STEP * sign_field * (jnp.sqrt(squares + EPSILON) - 1.0)


def outgoing(payload, first_tile, columns):
    leading = payload.shape[:-1]
    blocks = payload.reshape(leading + (payload.shape[-1] // columns, columns))
    return jnp.roll(blocks, first_tile % columns, axis=-1)


def incoming(returned, first_tile, columns):
    leading = returned.shape[:-2]
    blocks = jnp.roll(returned, -(first_tile % columns), axis=-1)
    return blocks.reshape(leading + (returned.shape[-2] * columns,))


def arrival(starts, column_index, columns, row_count):
    tile_ids = jnp.arange(row_count, dtype=jnp.int32) * columns + column_index
    owner_mask = (starts[None, :] <= tile_ids[:, None]).astype(jnp.int32)
    owner_of = jnp.sum(owner_mask, axis=1) - 1
    picked = (jnp.arange(columns, dtype=jnp.int32)[None, :] == owner_of[:, None]).astype(jnp.int32)
    first_tile = jnp.sum(picked * starts[None, :], axis=1)
    return (tile_ids - first_tile) // columns * columns + owner_of


def departure(starts, counts, column_index, columns, depth):
    offset = (column_index - starts[None, :]) % columns + jnp.arange(depth, dtype=jnp.int32)[
        :, None
    ] * columns
    sheet_row = (starts[None, :] + offset) // columns
    return jnp.where(offset < counts[None, :], sheet_row, 0).reshape(-1)


def on_device(phi_owned, band_counts, neighbours):
    tile_edge = phi_owned.shape[0]
    own_slots = phi_owned.shape[3]
    columns = lax.axis_size("mem")
    column_index = lax.axis_index("mem")
    depth = own_slots // columns
    tile_total = neighbours.shape[2]
    row_count = tile_total // columns
    counts = band_counts[0]
    starts = jnp.cumsum(counts) - counts
    first_tile = lax.dynamic_index_in_dim(starts, column_index, 0, keepdims=False)
    my_count = lax.dynamic_index_in_dim(counts, column_index, 0, keepdims=False)
    arrive = arrival(starts, column_index, columns, row_count)
    depart = departure(starts, counts, column_index, columns, depth)
    link_table = neighbours[0]
    held_links = (
        lax.dynamic_index_in_dim(
            link_table.reshape(6, row_count, columns), column_index, 2, keepdims=False
        )
        >= 0
    )
    received = lax.all_to_all(
        outgoing(phi_owned, first_tile, columns), "mem", split_axis=4, concat_axis=4, tiled=True
    )
    holder_tiles = jnp.take(
        received.reshape(tile_edge, tile_edge, tile_edge, own_slots), arrive, axis=3
    )
    level_set = holder_tiles.reshape(tile_edge, tile_edge, tile_edge * row_count)
    sign_field = level_set / jnp.sqrt(level_set * level_set + 1.0)
    for sweep in range(STEPS):
        padded_columns = with_halo(level_set, (("mem", 0),), 1)
        padded_groups = with_halo(level_set, (("grp", 2),), row_count)
        upper = level_set[:, tile_edge - 1].reshape(tile_edge, tile_edge, row_count)
        lower = level_set[:, 0].reshape(tile_edge, tile_edge, row_count)
        ghosts = (
            padded_columns[0],
            padded_columns[tile_edge + 1],
            jnp.roll(upper, 1, axis=2).reshape(tile_edge, -1),
            jnp.roll(lower, -1, axis=2).reshape(tile_edge, -1),
            padded_groups[:, :, :row_count],
            padded_groups[:, :, -row_count:],
        )
        level_set = advance(level_set, sign_field, ghosts, held_links, row_count)
    final_tiles = level_set.reshape(tile_edge, tile_edge, tile_edge, row_count)
    leaving = jnp.take(final_tiles, depart, axis=3).reshape(
        tile_edge, tile_edge, tile_edge, depth, columns
    )
    returned = lax.all_to_all(leaving, "mem", split_axis=4, concat_axis=4, tiled=True)
    result = incoming(returned, first_tile, columns)
    live = jnp.arange(own_slots, dtype=jnp.int32) < my_count
    return jnp.where(live, result, 0.0)


def solution(mesh):
    return jax.shard_map(
        on_device,
        mesh=mesh,
        in_specs=(P(None, None, None, ("grp", "mem")), P("grp", None), P("grp", None, None)),
        out_specs=P(None, None, None, ("grp", "mem")),
        check_vma=False,
    )
```

profile of v0, /device:TPU:193, one launch (start us, length us, event | category | flops | bytes accessed | tf_op | source)
XLA Modules:
  0.0 172.8 jit_solution(12509870855435636844)
XLA Ops:
  0.0 0.7 copy.47
  0.8 0.1 reduce
  0.9 0.7 bitcast_subtract_fusion.2
  1.6 0.6 dynamic_slice.15
  4.2 1.3 reshape.412
  5.5 1.2 dynamic-slice_maximum_fusion.1
  6.7 4.4 %copy.49 = f32[8,8,8,2,64]{2,1,3,0,4:T(8,128)} copy(f32[8,8,8,2,64]{4,3,2,1,0:T(2,128)S(1)} %dynamic-slice_maximum_fusion.1) | data formatting | bytes 524288 | tf_op jit(solution)/shard_map/jit(_roll_dynamic)/dynamic_slice | solution.py:61
  11.1 4.5 %reshape.452 = f32[64,1,1024]{2,1,0:T(1,128)} reshape(f32[64,8,2,8,8]{4,3,2,1,0:T(8,128)} %bitcast.66) | data formatting | bytes 524288
  15.6 10.8 %all-to-all-start = ((f32[64,1,1024]{2,1,0:T(1,128)}), f32[64,1,1024]{2,1,0:T(1,128)S(1)}, u32[]{:S(2)}, u32[]{:S(2)}) async-start(f32[64,1,1024]{2,1,0:T(1,128)} %reshape.452), calls=%async_computation | async-start | bytes 524288 | tf_op jit(solution)/shard_map/all_to_all | solution.py:108
  26.4 0.2 convert_reduce_fusion
  26.6 0.2 select_reduce_fusion
  26.8 0.1 reduce.2
  27.1 0.1 copy.60
  28.0 0.1 copy.48
  28.2 11.4 %all-to-all-done = f32[64,1,1024]{2,1,0:T(1,128)S(1)} async-done(((f32[64,1,1024]{2,1,0:T(1,128)}), f32[64,1,1024]{2,1,0:T(1,128)S(1)}, u32[]{:S(2)}, u32[]{:S(2)}) %all-to-all-start) | async-done | bytes 262176 | tf_op jit(solution)/shard_map/all_to_all | solution.py:108
  39.5 0.6 broadcast.461
  40.1 1.3 reduce.19
  41.4 3.6 %reshape.453 = f32[64,8,2,8,8]{4,3,2,1,0:T(8,128)} reshape(f32[64,1024]{1,0:T(8,128)S(1)} %reduce.19) | data formatting | bytes 524288
  45.0 4.6 %copy.50 = f32[8,8,8,2,64]{2,1,4,3,0:T(8,128)} copy(f32[8,8,8,2,64]{2,1,3,0,4:T(8,128)} %bitcast.67) | data formatting | bytes 524288 | tf_op jit(solution)/shard_map/all_to_all | solution.py:108
  49.6 2.9 %gather_fusion = f32[32,8,8,8]{3,2,1,0:T(8,128)S(1)} fusion(f32[8,8,8,128]{2,1,3,0:T(8,128)} %bitcast.71, s32[1024]{0:T(1024)S(1)} %pad_clamp_fusion.1), kind=kCustom, calls=%fused_computation | custom fusion | bytes 131200 | tf_op jit(solution)/shard_map/jit(_take)/gather | solution.py:111
  52.5 0.6 copy.51
  53.0 0.1 gather.13
  53.4 0.1 broadcast_select_fusion
  53.6 5.2 %collective-permute-start.2 = (f32[8,8,32]{2,1,0:T(8,128)S(1)}, f32[8,8,32]{2,1,0:T(8,128)S(1)}, u32[]{:S(2)}, u32[]{:S(2)}) collective-permute-start(f32[8,8,32]{2,1,0:T(8,128)S(1)} %get-tuple-element.59), channel_id=1, source_target_pairs={{0,64},{64,128},{128,192},{192,256},{256,320},{320,384},{384,448},... | collective-permute-start | bytes 24584 | tf_op jit(solution)/shard_map/ppermute | solution.py:20
  58.8 1.9 %collective-permute-start.3 = (f32[8,8,32]{2,1,0:T(8,128)S(1)}, f32[8,8,32]{2,1,0:T(8,128)S(1)}, u32[]{:S(2)}, u32[]{:S(2)}) collective-permute-start(f32[8,8,32]{2,1,0:T(8,128)S(1)} %get-tuple-element.60), channel_id=1, source_target_pairs={{64,0},{128,64},{192,128},{256,192},{320,256},{384,320},{448,384},... | collective-permute-start | bytes 24584 | tf_op jit(solution)/shard_map/ppermute | solution.py:21
  61.4 0.1 copy.54
  61.6 2.4 %collective-permute-start.1 = (f32[1,8,256]{2,1,0:T(8,128)S(1)}, f32[1,8,256]{2,1,0:T(8,128)S(1)}, u32[]{:S(2)}, u32[]{:S(2)}) collective-permute-start(f32[1,8,256]{2,1,0:T(8,128)S(1)} %squeeze.17), channel_id=1, source_target_pairs={{1,0},{2,1},{3,2},{4,3},{5,4},{6,5},{7,6},{8,7},{9,8},{10,9},{11,1... | collective-permute-start | bytes 24584 | tf_op jit(solution)/shard_map/ppermute | solution.py:21
  64.2 3.1 %collective-permute-start = (f32[1,8,256]{2,1,0:T(8,128)S(1)}, f32[1,8,256]{2,1,0:T(8,128)S(1)}, u32[]{:S(2)}, u32[]{:S(2)}) collective-permute-start(f32[1,8,256]{2,1,0:T(8,128)S(1)} %slice.284), channel_id=1, source_target_pairs={{0,1},{1,2},{2,3},{3,4},{4,5},{5,6},{6,7},{7,8},{8,9},{9,10},{10,1... | collective-permute-start | bytes 24584 | tf_op jit(solution)/shard_map/ppermute | solution.py:20
  67.4 0.7 collective-permute-done
  68.2 0.2 multiply_subtract_fusion.3
  68.6 4.6 %collective-permute-start.6 = (f32[8,8,32]{2,1,0:T(8,128)S(1)}, f32[8,8,32]{2,1,0:T(8,128)S(1)}, u32[]{:S(2)}, u32[]{:S(2)}) collective-permute-start(f32[8,8,32]{2,1,0:T(8,128)S(1)} %get-tuple-element.51), channel_id=1, source_target_pairs={{0,64},{64,128},{128,192},{192,256},{256,320},{320,384},{384,448},... | collective-permute-start | bytes 24584 | tf_op jit(solution)/shard_map/ppermute | solution.py:20
  73.1 1.9 %collective-permute-start.7 = (f32[8,8,32]{2,1,0:T(8,128)S(1)}, f32[8,8,32]{2,1,0:T(8,128)S(1)}, u32[]{:S(2)}, u32[]{:S(2)}) collective-permute-start(f32[8,8,32]{2,1,0:T(8,128)S(1)} %get-tuple-element.52), channel_id=1, source_target_pairs={{64,0},{128,64},{192,128},{256,192},{320,256},{384,320},{448,384},... | collective-permute-start | bytes 24584 | tf_op jit(solution)/shard_map/ppermute | solution.py:21
  75.7 4.5 %collective-permute-start.4 = (f32[1,8,256]{2,1,0:T(8,128)S(1)}, f32[1,8,256]{2,1,0:T(8,128)S(1)}, u32[]{:S(2)}, u32[]{:S(2)}) collective-permute-start(f32[1,8,256]{2,1,0:T(8,128)S(1)} %get-tuple-element.45), channel_id=1, source_target_pairs={{0,1},{1,2},{2,3},{3,4},{4,5},{5,6},{6,7},{7,8},{8,9},{9,10},{10,1... | collective-permute-start | bytes 24584 | tf_op jit(solution)/shard_map/ppermute | solution.py:20
  80.2 1.9 %collective-permute-start.5 = (f32[1,8,256]{2,1,0:T(8,128)S(1)}, f32[1,8,256]{2,1,0:T(8,128)S(1)}, u32[]{:S(2)}, u32[]{:S(2)}) collective-permute-start(f32[1,8,256]{2,1,0:T(8,128)S(1)} %get-tuple-element.46), channel_id=1, source_target_pairs={{1,0},{2,1},{3,2},{4,3},{5,4},{6,5},{7,6},{8,7},{9,8},{10,9},{11,1... | collective-permute-start | bytes 24584 | tf_op jit(solution)/shard_map/ppermute | solution.py:21
  82.3 2.9 %collective-permute-done.5 = f32[1,8,256]{2,1,0:T(8,128)S(1)} collective-permute-done((f32[1,8,256]{2,1,0:T(8,128)S(1)}, f32[1,8,256]{2,1,0:T(8,128)S(1)}, u32[]{:S(2)}, u32[]{:S(2)}) %collective-permute-start.5) | collective-permute-done | bytes 8224 | tf_op jit(solution)/shard_map/ppermute | solution.py:21
  85.2 0.2 multiply_subtract_fusion.2
  85.6 4.9 %collective-permute-start.10 = (f32[8,8,32]{2,1,0:T(8,128)S(1)}, f32[8,8,32]{2,1,0:T(8,128)S(1)}, u32[]{:S(2)}, u32[]{:S(2)}) collective-permute-start(f32[8,8,32]{2,1,0:T(8,128)S(1)} %get-tuple-element.39), channel_id=1, source_target_pairs={{0,64},{64,128},{128,192},{192,256},{256,320},{320,384},{384,448},... | collective-permute-start | bytes 24584 | tf_op jit(solution)/shard_map/ppermute | solution.py:20
  90.4 1.9 %collective-permute-start.11 = (f32[8,8,32]{2,1,0:T(8,128)S(1)}, f32[8,8,32]{2,1,0:T(8,128)S(1)}, u32[]{:S(2)}, u32[]{:S(2)}) collective-permute-start(f32[8,8,32]{2,1,0:T(8,128)S(1)} %get-tuple-element.40), channel_id=1, source_target_pairs={{64,0},{128,64},{192,128},{256,192},{320,256},{384,320},{448,384},... | collective-permute-start | bytes 24584 | tf_op jit(solution)/shard_map/ppermute | solution.py:21
  93.0 2.2 %collective-permute-start.8 = (f32[1,8,256]{2,1,0:T(8,128)S(1)}, f32[1,8,256]{2,1,0:T(8,128)S(1)}, u32[]{:S(2)}, u32[]{:S(2)}) collective-permute-start(f32[1,8,256]{2,1,0:T(8,128)S(1)} %get-tuple-element.33), channel_id=1, source_target_pairs={{0,1},{1,2},{2,3},{3,4},{4,5},{5,6},{6,7},{7,8},{8,9},{9,10},{10,1... | collective-permute-start | bytes 24584 | tf_op jit(solution)/shard_map/ppermute | solution.py:20
  95.3 2.1 %collective-permute-start.9 = (f32[1,8,256]{2,1,0:T(8,128)S(1)}, f32[1,8,256]{2,1,0:T(8,128)S(1)}, u32[]{:S(2)}, u32[]{:S(2)}) collective-permute-start(f32[1,8,256]{2,1,0:T(8,128)S(1)} %get-tuple-element.34), channel_id=1, source_target_pairs={{1,0},{2,1},{3,2},{4,3},{5,4},{6,5},{7,6},{8,7},{9,8},{10,9},{11,1... | collective-permute-start | bytes 24584 | tf_op jit(solution)/shard_map/ppermute | solution.py:21
  97.5 2.7 %collective-permute-done.9 = f32[1,8,256]{2,1,0:T(8,128)S(1)} collective-permute-done((f32[1,8,256]{2,1,0:T(8,128)S(1)}, f32[1,8,256]{2,1,0:T(8,128)S(1)}, u32[]{:S(2)}, u32[]{:S(2)}) %collective-permute-start.9) | collective-permute-done | bytes 8224 | tf_op jit(solution)/shard_map/ppermute | solution.py:21
  100.2 0.2 multiply_subtract_fusion.1
  100.6 4.9 %collective-permute-start.14 = (f32[8,8,32]{2,1,0:T(8,128)S(1)}, f32[8,8,32]{2,1,0:T(8,128)S(1)}, u32[]{:S(2)}, u32[]{:S(2)}) collective-permute-start(f32[8,8,32]{2,1,0:T(8,128)S(1)} %get-tuple-element.27), channel_id=1, source_target_pairs={{0,64},{64,128},{128,192},{192,256},{256,320},{320,384},{384,448},... | collective-permute-start | bytes 24584 | tf_op jit(solution)/shard_map/ppermute | solution.py:20
  105.5 1.9 %collective-permute-start.15 = (f32[8,8,32]{2,1,0:T(8,128)S(1)}, f32[8,8,32]{2,1,0:T(8,128)S(1)}, u32[]{:S(2)}, u32[]{:S(2)}) collective-permute-start(f32[8,8,32]{2,1,0:T(8,128)S(1)} %get-tuple-element.28), channel_id=1, source_target_pairs={{64,0},{128,64},{192,128},{256,192},{320,256},{384,320},{448,384},... | collective-permute-start | bytes 24584 | tf_op jit(solution)/shard_map/ppermute | solution.py:21
  108.1 2.2 %collective-permute-start.12 = (f32[1,8,256]{2,1,0:T(8,128)S(1)}, f32[1,8,256]{2,1,0:T(8,128)S(1)}, u32[]{:S(2)}, u32[]{:S(2)}) collective-permute-start(f32[1,8,256]{2,1,0:T(8,128)S(1)} %get-tuple-element.21), channel_id=1, source_target_pairs={{0,1},{1,2},{2,3},{3,4},{4,5},{5,6},{6,7},{7,8},{8,9},{9,10},{10,1... | collective-permute-start | bytes 24584 | tf_op jit(solution)/shard_map/ppermute | solution.py:20
  110.3 2.3 %collective-permute-start.13 = (f32[1,8,256]{2,1,0:T(8,128)S(1)}, f32[1,8,256]{2,1,0:T(8,128)S(1)}, u32[]{:S(2)}, u32[]{:S(2)}) collective-permute-start(f32[1,8,256]{2,1,0:T(8,128)S(1)} %get-tuple-element.22), channel_id=1, source_target_pairs={{1,0},{2,1},{3,2},{4,3},{5,4},{6,5},{7,6},{8,7},{9,8},{10,9},{11,1... | collective-permute-start | bytes 24584 | tf_op jit(solution)/shard_map/ppermute | solution.py:21
  112.7 2.6 %collective-permute-done.13 = f32[1,8,256]{2,1,0:T(8,128)S(1)} collective-permute-done((f32[1,8,256]{2,1,0:T(8,128)S(1)}, f32[1,8,256]{2,1,0:T(8,128)S(1)}, u32[]{:S(2)}, u32[]{:S(2)}) %collective-permute-start.13) | collective-permute-done | bytes 8224 | tf_op jit(solution)/shard_map/ppermute | solution.py:21
  115.3 0.2 multiply_subtract_fusion
  115.4 0.1 reshape.423
  115.6 0.4 copy.55
  116.0 3.0 %gather_fusion.1 = f32[128,8,8,8]{3,2,1,0:T(8,128)} fusion(f32[8,8,8,32]{2,1,3,0:T(8,128)S(1)} %copy.55, s32[1024]{0:T(1024)S(1)} %pad_clamp_fusion), kind=kCustom, calls=%fused_computation.1 | custom fusion | bytes 524800 | tf_op jit(solution)/shard_map/jit(_take)/gather | solution.py:131
  119.0 4.5 %fusion.34 = f32[64,2,8,8,8]{4,3,2,1,0:T(8,128)} fusion(f32[8,8,8,2,64]{2,1,0,4,3:T(8,128)} %bitcast.70, pred[2,64]{0,1:T(8,128)(4,1)S(1)} %copy.48), kind=kLoop, calls=%fused_computation.160 | loop fusion | flops 65536 | bytes 524416
  123.5 4.5 %reshape.454 = f32[64,1,1024]{2,1,0:T(1,128)} reshape(f32[64,2,8,8,8]{4,3,2,1,0:T(8,128)} %fusion.34) | data formatting | bytes 524288
  128.0 20.2 %all-to-all-start.1 = ((f32[64,1,1024]{2,1,0:T(1,128)}), f32[64,1,1024]{2,1,0:T(1,128)S(1)}, u32[]{:S(2)}, u32[]{:S(2)}) async-start(f32[64,1,1024]{2,1,0:T(1,128)} %reshape.454), calls=%async_computation.1 | async-start | bytes 524288 | tf_op jit(solution)/shard_map/all_to_all | solution.py:134
  148.2 0.6 constant_dynamic-slice_fusion.1
  148.8 0.6 iota_compare_fusion.1
  149.4 12.0 %all-to-all-done.1 = f32[64,1,1024]{2,1,0:T(1,128)S(1)} async-done(((f32[64,1,1024]{2,1,0:T(1,128)}), f32[64,1,1024]{2,1,0:T(1,128)S(1)}, u32[]{:S(2)}, u32[]{:S(2)}) %all-to-all-start.1) | async-done | bytes 262176 | tf_op jit(solution)/shard_map/all_to_all | solution.py:134
  161.4 1.3 reduce.20
  162.7 3.6 %reshape.455 = f32[64,2,8,8,8]{4,3,2,1,0:T(8,128)} reshape(f32[64,1024]{1,0:T(8,128)S(1)} %reduce.20) | data formatting | bytes 524288
  166.3 4.8 %copy.57 = f32[8,8,8,2,64]{4,2,3,1,0:T(8,128)S(1)} copy(f32[8,8,8,2,64]{2,1,0,3,4:T(8,128)} %bitcast.68) | data formatting | bytes 524288 | tf_op jit(solution)/shard_map/all_to_all | solution.py:134
  171.1 0.3 dynamic-slice_maximum_fusion
  171.5 0.3 copy.59
  171.8 0.3 reshape.424
  172.1 0.7 broadcast_select_fusion.1
  (108 shorter events, 5.2 us)
Async XLA Ops:
  6.6 19.7 %copy-start.1 = (s32[1,64]{1,0:T(1,128)S(1)}, s32[1,64]{1,0:T(1,128)}, u32[]{:S(2)}) copy-start(s32[1,64]{1,0:T(1,128)} %param.6) | copy-start | bytes 772
  6.6 20.2 %copy-start = (s32[1,6,2048]{2,0,1:T(1,128)S(1)}, s32[1,6,2048]{2,0,1:T(1,128)}, u32[]{:S(2)}) copy-start(s32[1,6,2048]{2,0,1:T(1,128)} %param.7) | copy-start | bytes 147460
  15.6 24.0 %all-to-all-start = ((f32[64,1,1024]{2,1,0:T(1,128)}), f32[64,1,1024]{2,1,0:T(1,128)S(1)}, u32[]{:S(2)}, u32[]{:S(2)}) async-start(f32[64,1,1024]{2,1,0:T(1,128)} %reshape.452), calls=%async_computation | async-start | bytes 524288 | tf_op jit(solution)/shard_map/all_to_all | solution.py:108
  53.6 14.5 %collective-permute-start.2 = (f32[8,8,32]{2,1,0:T(8,128)S(1)}, f32[8,8,32]{2,1,0:T(8,128)S(1)}, u32[]{:S(2)}, u32[]{:S(2)}) collective-permute-start(f32[8,8,32]{2,1,0:T(8,128)S(1)} %get-tuple-element.59), channel_id=1, source_target_pairs={{0,64},{64,128},{128,192},{192,256},{256,320},{320,384},{384,448},... | collective-permute-start | bytes 24584 | tf_op jit(solution)/shard_map/ppermute | solution.py:20
  58.8 9.3 %collective-permute-start.3 = (f32[8,8,32]{2,1,0:T(8,128)S(1)}, f32[8,8,32]{2,1,0:T(8,128)S(1)}, u32[]{:S(2)}, u32[]{:S(2)}) collective-permute-start(f32[8,8,32]{2,1,0:T(8,128)S(1)} %get-tuple-element.60), channel_id=1, source_target_pairs={{64,0},{128,64},{192,128},{256,192},{320,256},{384,320},{448,384},... | collective-permute-start | bytes 24584 | tf_op jit(solution)/shard_map/ppermute | solution.py:21
  61.6 5.8 %collective-permute-start.1 = (f32[1,8,256]{2,1,0:T(8,128)S(1)}, f32[1,8,256]{2,1,0:T(8,128)S(1)}, u32[]{:S(2)}, u32[]{:S(2)}) collective-permute-start(f32[1,8,256]{2,1,0:T(8,128)S(1)} %squeeze.17), channel_id=1, source_target_pairs={{1,0},{2,1},{3,2},{4,3},{5,4},{6,5},{7,6},{8,7},{9,8},{10,9},{11,1... | collective-permute-start | bytes 24584 | tf_op jit(solution)/shard_map/ppermute | solution.py:21
  64.2 3.9 %collective-permute-start = (f32[1,8,256]{2,1,0:T(8,128)S(1)}, f32[1,8,256]{2,1,0:T(8,128)S(1)}, u32[]{:S(2)}, u32[]{:S(2)}) collective-permute-start(f32[1,8,256]{2,1,0:T(8,128)S(1)} %slice.284), channel_id=1, source_target_pairs={{0,1},{1,2},{2,3},{3,4},{4,5},{5,6},{6,7},{7,8},{8,9},{9,10},{10,1... | collective-permute-start | bytes 24584 | tf_op jit(solution)/shard_map/ppermute | solution.py:20
  68.6 13.6 %collective-permute-start.6 = (f32[8,8,32]{2,1,0:T(8,128)S(1)}, f32[8,8,32]{2,1,0:T(8,128)S(1)}, u32[]{:S(2)}, u32[]{:S(2)}) collective-permute-start(f32[8,8,32]{2,1,0:T(8,128)S(1)} %get-tuple-element.51), channel_id=1, source_target_pairs={{0,64},{64,128},{128,192},{192,256},{256,320},{320,384},{384,448},... | collective-permute-start | bytes 24584 | tf_op jit(solution)/shard_map/ppermute | solution.py:20
  73.1 9.0 %collective-permute-start.7 = (f32[8,8,32]{2,1,0:T(8,128)S(1)}, f32[8,8,32]{2,1,0:T(8,128)S(1)}, u32[]{:S(2)}, u32[]{:S(2)}) collective-permute-start(f32[8,8,32]{2,1,0:T(8,128)S(1)} %get-tuple-element.52), channel_id=1, source_target_pairs={{64,0},{128,64},{192,128},{256,192},{320,256},{384,320},{448,384},... | collective-permute-start | bytes 24584 | tf_op jit(solution)/shard_map/ppermute | solution.py:21
  75.7 6.5 %collective-permute-start.4 = (f32[1,8,256]{2,1,0:T(8,128)S(1)}, f32[1,8,256]{2,1,0:T(8,128)S(1)}, u32[]{:S(2)}, u32[]{:S(2)}) collective-permute-start(f32[1,8,256]{2,1,0:T(8,128)S(1)} %get-tuple-element.45), channel_id=1, source_target_pairs={{0,1},{1,2},{2,3},{3,4},{4,5},{5,6},{6,7},{7,8},{8,9},{9,10},{10,1... | collective-permute-start | bytes 24584 | tf_op jit(solution)/shard_map/ppermute | solution.py:20
  80.2 5.0 %collective-permute-start.5 = (f32[1,8,256]{2,1,0:T(8,128)S(1)}, f32[1,8,256]{2,1,0:T(8,128)S(1)}, u32[]{:S(2)}, u32[]{:S(2)}) collective-permute-start(f32[1,8,256]{2,1,0:T(8,128)S(1)} %get-tuple-element.46), channel_id=1, source_target_pairs={{1,0},{2,1},{3,2},{4,3},{5,4},{6,5},{7,6},{8,7},{9,8},{10,9},{11,1... | collective-permute-start | bytes 24584 | tf_op jit(solution)/shard_map/ppermute | solution.py:21
  85.6 11.8 %collective-permute-start.10 = (f32[8,8,32]{2,1,0:T(8,128)S(1)}, f32[8,8,32]{2,1,0:T(8,128)S(1)}, u32[]{:S(2)}, u32[]{:S(2)}) collective-permute-start(f32[8,8,32]{2,1,0:T(8,128)S(1)} %get-tuple-element.39), channel_id=1, source_target_pairs={{0,64},{64,128},{128,192},{192,256},{256,320},{320,384},{384,448},... | collective-permute-start | bytes 24584 | tf_op jit(solution)/shard_map/ppermute | solution.py:20
  90.4 7.0 %collective-permute-start.11 = (f32[8,8,32]{2,1,0:T(8,128)S(1)}, f32[8,8,32]{2,1,0:T(8,128)S(1)}, u32[]{:S(2)}, u32[]{:S(2)}) collective-permute-start(f32[8,8,32]{2,1,0:T(8,128)S(1)} %get-tuple-element.40), channel_id=1, source_target_pairs={{64,0},{128,64},{192,128},{256,192},{320,256},{384,320},{448,384},... | collective-permute-start | bytes 24584 | tf_op jit(solution)/shard_map/ppermute | solution.py:21
  93.0 4.5 %collective-permute-start.8 = (f32[1,8,256]{2,1,0:T(8,128)S(1)}, f32[1,8,256]{2,1,0:T(8,128)S(1)}, u32[]{:S(2)}, u32[]{:S(2)}) collective-permute-start(f32[1,8,256]{2,1,0:T(8,128)S(1)} %get-tuple-element.33), channel_id=1, source_target_pairs={{0,1},{1,2},{2,3},{3,4},{4,5},{5,6},{6,7},{7,8},{8,9},{9,10},{10,1... | collective-permute-start | bytes 24584 | tf_op jit(solution)/shard_map/ppermute | solution.py:20
  95.3 5.0 %collective-permute-start.9 = (f32[1,8,256]{2,1,0:T(8,128)S(1)}, f32[1,8,256]{2,1,0:T(8,128)S(1)}, u32[]{:S(2)}, u32[]{:S(2)}) collective-permute-start(f32[1,8,256]{2,1,0:T(8,128)S(1)} %get-tuple-element.34), channel_id=1, source_target_pairs={{1,0},{2,1},{3,2},{4,3},{5,4},{6,5},{7,6},{8,7},{9,8},{10,9},{11,1... | collective-permute-start | bytes 24584 | tf_op jit(solution)/shard_map/ppermute | solution.py:21
  100.6 12.0 %collective-permute-start.14 = (f32[8,8,32]{2,1,0:T(8,128)S(1)}, f32[8,8,32]{2,1,0:T(8,128)S(1)}, u32[]{:S(2)}, u32[]{:S(2)}) collective-permute-start(f32[8,8,32]{2,1,0:T(8,128)S(1)} %get-tuple-element.27), channel_id=1, source_target_pairs={{0,64},{64,128},{128,192},{192,256},{256,320},{320,384},{384,448},... | collective-permute-start | bytes 24584 | tf_op jit(solution)/shard_map/ppermute | solution.py:20
  105.5 7.1 %collective-permute-start.15 = (f32[8,8,32]{2,1,0:T(8,128)S(1)}, f32[8,8,32]{2,1,0:T(8,128)S(1)}, u32[]{:S(2)}, u32[]{:S(2)}) collective-permute-start(f32[8,8,32]{2,1,0:T(8,128)S(1)} %get-tuple-element.28), channel_id=1, source_target_pairs={{64,0},{128,64},{192,128},{256,192},{320,256},{384,320},{448,384},... | collective-permute-start | bytes 24584 | tf_op jit(solution)/shard_map/ppermute | solution.py:21
  108.1 4.7 %collective-permute-start.12 = (f32[1,8,256]{2,1,0:T(8,128)S(1)}, f32[1,8,256]{2,1,0:T(8,128)S(1)}, u32[]{:S(2)}, u32[]{:S(2)}) collective-permute-start(f32[1,8,256]{2,1,0:T(8,128)S(1)} %get-tuple-element.21), channel_id=1, source_target_pairs={{0,1},{1,2},{2,3},{3,4},{4,5},{5,6},{6,7},{7,8},{8,9},{9,10},{10,1... | collective-permute-start | bytes 24584 | tf_op jit(solution)/shard_map/ppermute | solution.py:20
  110.3 5.0 %collective-permute-start.13 = (f32[1,8,256]{2,1,0:T(8,128)S(1)}, f32[1,8,256]{2,1,0:T(8,128)S(1)}, u32[]{:S(2)}, u32[]{:S(2)}) collective-permute-start(f32[1,8,256]{2,1,0:T(8,128)S(1)} %get-tuple-element.22), channel_id=1, source_target_pairs={{1,0},{2,1},{3,2},{4,3},{5,4},{6,5},{7,6},{8,7},{9,8},{10,9},{11,1... | collective-permute-start | bytes 24584 | tf_op jit(solution)/shard_map/ppermute | solution.py:21
  128.0 33.3 %all-to-all-start.1 = ((f32[64,1,1024]{2,1,0:T(1,128)}), f32[64,1,1024]{2,1,0:T(1,128)S(1)}, u32[]{:S(2)}, u32[]{:S(2)}) async-start(f32[64,1,1024]{2,1,0:T(1,128)} %reshape.454), calls=%async_computation.1 | async-start | bytes 524288 | tf_op jit(solution)/shard_map/all_to_all | solution.py:134
where the time goes:
time: 174 us; the launch traced here: 173 us
  starting transfers between devices  78.9 us (45%)
  local copies, waits for them, and re-layouts  45.6 us (26%)
  waiting for transfers between devices  32.3 us (19%)
  other arithmetic  13.3 us (8%)
  between operations  2.64 us (2%)
    ppermute x8, starting transfers between devices, with_halo(): before = lax.ppermute(last, axis, up)  31.5 us
    all_to_all x1, starting transfers between devices, on_device(): lax.all_to_all(leaving, 'mem', split_axis=4, concat_axis=4, tiled=True)  20.2 us
    ppermute x8, starting transfers between devices, with_halo(): after = lax.ppermute(leading, axis, down)  16.4 us
    unnamed x9, local copies, waits for them, and re-layouts  16.3 us
    all_to_all x1, waiting for transfers between devices, on_device(): lax.all_to_all(leaving, 'mem', split_axis=4, concat_axis=4, tiled=True)  12 us
    all_to_all x1, waiting for transfers between devices, on_device(): lax.all_to_all(outgoing(phi_owned, first_tile, columns), 'mem', split_axi...  11.4 us
    all_to_all x1, starting transfers between devices, on_device(): lax.all_to_all(outgoing(phi_owned, first_tile, columns), 'mem', split_axi...  10.8 us
    ppermute x8, waiting for transfers between devices, with_halo(): after = lax.ppermute(leading, axis, down)  8.2 us
  transfers between devices with their start and end apart: 18, of which 6 were waited for; matrix products, arithmetic and copies ran while one was open for 4% of the time, Pallas kernels for 0%

commit v1 on v0

v1 whole, which is shorter than its diff:
```python
import functools

import jax
import jax.numpy as jnp
from jax import lax
from jax.experimental import pallas as pl
from jax.experimental.pallas import tpu as pltpu
from jax.sharding import PartitionSpec as P

STEPS = 4
TIME_STEP = 0.5
EPSILON = 1e-06

TILE = 8
ROWS = 32
COLUMNS = 64
SLOTS = 128
CELLS = TILE**3
DEPTH = SLOTS // COLUMNS
WIDE = 16
TABLE = 40

F32 = jnp.float32
I32 = jnp.int32


def shift(x, amount, axis):
    return pltpu.roll(x, amount % x.shape[axis] if isinstance(amount, int) else amount, axis)


def iota(shape, axis):
    return lax.broadcasted_iota(I32, shape, axis)


def own_start(counts_ref, me):
    total = jnp.int32(0)
    for owner in range(COLUMNS - 1):
        total = total + jnp.where(owner < me, counts_ref[0, owner], 0)
    return total


def pack_kernel(where_am_i, *refs):
    counts_ref, phi_ref, out_ref = refs[-3:]
    turn = own_start(counts_ref, where_am_i(refs)) & (COLUMNS - 1)
    low_half = iota((TILE, SLOTS), 0) < TILE // 2
    for z in range(TILE):
        blocks = []
        for y in range(TILE):
            tiles = phi_ref[pl.ds(y * TILE + z, TILE, stride=TILE * TILE), :]
            here = pltpu.roll(tiles, turn, 1)
            left = shift(here, 1, 1)
            right = shift(here, -1, 1)
            blocks.append(shift(jnp.where(low_half, here, left), 4, 0))
            blocks.append(shift(jnp.where(low_half, right, here), 4, 0))
        turned = jnp.concatenate(blocks, axis=0).T
        for d in range(DEPTH):
            out_ref[pl.ds(d * TILE + z, COLUMNS, stride=DEPTH * TILE), :] = turned[
                d * COLUMNS : (d + 1) * COLUMNS
            ]


def mask_kernel(where_am_i, *refs):
    links_ref, out_ref, lhs_ref, found_ref = refs[-4:]
    me = where_am_i(refs)
    pairs = ROWS // 2
    for v in range(pairs):
        lhs_ref[v * 8 : v * 8 + 6, :] = jnp.where(
            links_ref[0, :, v * 128 : (v + 1) * 128] >= 0, 1.0, 0.0
        )
        lhs_ref[v * 8 + 6 : v * 8 + 8, :] = jnp.zeros((2, 128), F32)
    source = iota((128, 256), 0)
    target = iota((128, 256), 1)
    x16 = target % WIDE
    column = me + jnp.where(x16 < 4, -1, jnp.where(x16 >= 12, 1, 0))
    pick = (source % COLUMNS == column) & (source // COLUMNS == target // 128)
    found = jnp.dot(
        lhs_ref[...].astype(jnp.bfloat16),
        jnp.where(pick, 1.0, 0.0).astype(jnp.bfloat16),
        preferred_element_type=F32,
    )
    for v in range(pairs):
        for half in range(2):
            found_ref[pl.ds(2 * v + half, 8, stride=ROWS), :] = found[
                v * 8 : v * 8 + 8, half * 128 : (half + 1) * 128
            ]
    lane = iota((ROWS, 128), 1)
    x16 = lane % WIDE
    out_ref[0] = jnp.where((x16 == 3) | (x16 == 11), found_ref[ROWS : 2 * ROWS, :], 1.0)
    out_ref[1] = jnp.where(lane >= 112, found_ref[3 * ROWS : 4 * ROWS, :], 1.0)
    out_ref[2] = found_ref[4 * ROWS : 5 * ROWS, :]
    out_ref[3] = found_ref[5 * ROWS : 6 * ROWS, :]


def fill_table(counts_ref, table_ref, column):
    for entry in range(3):
        table_ref[entry, 1] = jnp.int32(0)
        table_ref[entry, ROWS] = jnp.int32(0)

    def body(owner, start):
        turn = start & (COLUMNS - 1)
        for entry in range(3):
            delta = entry - 1
            first = (column + delta - turn) & (COLUMNS - 1)
            row = (start + first - delta) >> 6
            slot = ((first + turn - delta) & (SLOTS - 1)) >> 6
            table_ref[entry, row + 1] = owner * DEPTH + slot
            table_ref[entry, row + 2] = owner * DEPTH + (1 - slot)
        return start + counts_ref[0, owner]

    lax.fori_loop(0, COLUMNS, body, jnp.int32(0), unroll=8)


def unpack_kernel(where_am_i, *refs):
    counts_ref, received_ref, masks_ref, low_ref, high_ref, table_out_ref, table_ref, tiles_ref = refs[-8:]
    fill_table(counts_ref, table_ref, where_am_i(refs))
    x16 = iota((TILE, 128), 1) % WIDE
    for r in range(ROWS):
        left = received_ref[table_ref[0, r + 1]]
        here = received_ref[table_ref[1, r + 1]]
        right = received_ref[table_ref[2, r + 1]]
        tile = jnp.where(x16 < 4, left, jnp.where(x16 >= 12, right, here))
        tiles_ref[pl.ds(r, TILE, stride=ROWS), :] = tile
        table_out_ref[0, r] = table_ref[1, r + 1]
    half = TILE // 2
    for z in range(half):
        low_ref[z] = tiles_ref[z * ROWS : (z + 1) * ROWS, :]
        high_ref[z] = tiles_ref[(z + half) * ROWS : (z + half + 1) * ROWS, :]
    for i in range(2):
        low_ref[half + i] = masks_ref[i]
        high_ref[half + i] = masks_ref[i]


def march_kernel(*refs):
    (
        table_ref,
        below_ref,
        low_ref,
        high_ref,
        above_ref,
        masks_ref,
        out_ref,
        even_ref,
        odd_ref,
        sign_ref,
        done_ref,
    ) = refs
    half = TILE // 2
    lane = iota((ROWS, 128), 1)
    first_y = lane < WIDE
    last_y = lane >= 128 - WIDE
    sources = (below_ref, low_ref, high_ref, above_ref)
    for z in range(1, 2 * TILE - 1):
        level = sources[z // half][z % half]
        sign_ref[z] = level / jnp.sqrt(level * level + 1.0)

    def load(step, z):
        if step == 0:
            return sources[z // half][z % half]
        return (odd_ref if step % 2 else even_ref)[z]

    for step in range(STEPS):
        target_ref = even_ref if step % 2 else odd_ref
        level = load(step, step)
        after = load(step, step + 1)
        ahead_z = after - level
        if step == 3:
            ahead_z = ahead_z * masks_ref[2]
        for z in range(step + 1, 2 * TILE - 1 - step):
            back_z = ahead_z
            level = after
            after = load(step, z + 1)
            ahead_z = after - level
            if z == 3:
                ahead_z = ahead_z * masks_ref[2]
            if z == 11:
                ahead_z = ahead_z * masks_ref[3]
            links = (below_ref, low_ref, low_ref, above_ref)[z // half]
            sign_field = sign_ref[z]
            up = jnp.where(sign_field > 0, 1.0, -1.0)
            down = -up
            squares = None
            ahead = (shift(level, -1, 1) - level) * links[half]
            back = shift(ahead, 1, 1)
            squares = jnp.square(jnp.maximum(jnp.maximum(up * back, down * ahead), 0.0))
            beyond = jnp.where(first_y, shift(level, -1, 0), level)
            ahead = (shift(beyond, -WIDE, 1) - level) * links[half + 1]
            back = shift(jnp.where(last_y, shift(ahead, 1, 0), ahead), WIDE, 1)
            squares = squares + jnp.square(
                jnp.maximum(jnp.maximum(up * back, down * ahead), 0.0)
            )
            squares = squares + jnp.square(
                jnp.maximum(jnp.maximum(up * back_z, down * ahead_z), 0.0)
            )
            target_ref[z] = level - TIME_STEP * sign_field * (jnp.sqrt(squares + EPSILON) - 1.0)
    final_ref = even_ref
    left_half = lane % WIDE < TILE
    for q in range(half):
        done_ref[q * ROWS : (q + 1) * ROWS, :] = jnp.where(
            left_half, shift(final_ref[half + q], -4, 1), shift(final_ref[2 * half + q], 4, 1)
        )
    for r in range(ROWS):
        out_ref[table_ref[0, r]] = done_ref[pl.ds(r, half, stride=ROWS), :]


def deliver_kernel(where_am_i, *refs):
    counts_ref, returned_ref, out_ref = refs[-3:]
    me = where_am_i(refs)
    turn = own_start(counts_ref, me) & (COLUMNS - 1)
    live = iota((SLOTS, SLOTS), 1) < counts_ref[0, me]
    half = TILE // 2
    for q in range(half):
        rows = [
            returned_ref[pl.ds(d * half + q, COLUMNS, stride=DEPTH * half), :] for d in range(DEPTH)
        ]
        turned = jnp.concatenate(rows, axis=0).T
        turned = pltpu.roll(turned, (SLOTS - turn) & (SLOTS - 1), 1)
        turned = jnp.where(live, turned, 0.0)
        for y in range(TILE):
            for upper in range(2):
                row = y * WIDE + upper * TILE
                out_ref[pl.ds(y * TILE + q + upper * half, TILE, stride=TILE * TILE), :] = turned[
                    row : row + TILE
                ]


def spec(space=pltpu.VMEM):
    return pl.BlockSpec(memory_space=space)


def run(kernel, operands, shapes, scratch, me=None, spaces=None, out_spaces=None, cost=(0, 0)):
    spaces = spaces or [pltpu.VMEM] * len(operands)
    out_spaces = out_spaces or [pltpu.VMEM] * len(shapes)
    if me is not None:
        operands = (me, *operands)
        spaces = [pltpu.SMEM, *spaces]
    out = pl.pallas_call(
        kernel,
        out_shape=[jax.ShapeDtypeStruct(s, t) for s, t in shapes],
        in_specs=[spec(s) for s in spaces],
        out_specs=[spec(s) for s in out_spaces],
        scratch_shapes=scratch,
        compiler_params=pltpu.CompilerParams(vmem_limit_bytes=32 << 20),
        cost_estimate=pl.CostEstimate(flops=cost[0], bytes_accessed=cost[1], transcendentals=0),
        name=getattr(kernel, "func", kernel).__name__,
    )(*operands)
    return out


def position(refs):
    return lax.axis_index("mem")


def given(refs):
    return refs[0][0]


def bind(kernel, me):
    return functools.partial(kernel, position if me is None else given)


def pack(counts, phi, me=None):
    (out,) = run(
        bind(pack_kernel, me),
        (counts, phi.reshape(CELLS, SLOTS)),
        [((COLUMNS * DEPTH * TILE, 128), F32)],
        [],
        me,
        [pltpu.SMEM, pltpu.VMEM],
    )
    return out.reshape(COLUMNS, DEPTH * TILE, 128)


def masks_of(neighbours, me=None):
    (out,) = run(
        bind(mask_kernel, me),
        (neighbours,),
        [((4, ROWS, 128), F32)],
        [pltpu.VMEM((128, 128), F32), pltpu.VMEM((8 * ROWS, 128), F32)],
        me,
        cost=(1 << 22, 1 << 17),
    )
    return out


def unpack(counts, received, masks, me=None):
    half = TILE // 2
    return run(
        bind(unpack_kernel, me),
        (counts, received.reshape(COLUMNS * DEPTH, TILE, 128), masks),
        [((half + 2, ROWS, 128), F32), ((half + 2, ROWS, 128), F32), ((1, ROWS), I32)],
        [pltpu.SMEM((3, TABLE), I32), pltpu.VMEM((TILE * ROWS, 128), F32)],
        me,
        [pltpu.SMEM, pltpu.VMEM, pltpu.VMEM],
        [pltpu.VMEM, pltpu.VMEM, pltpu.SMEM],
    )


def march(table, below, low, high, above, masks):
    half = TILE // 2
    (out,) = run(
        march_kernel,
        (table, below, low, high, above, masks),
        [((COLUMNS * DEPTH, half, 128), F32)],
        [pltpu.VMEM((2 * TILE, ROWS, 128), F32)] * 3 + [pltpu.VMEM((half * ROWS, 128), F32)],
        None,
        [pltpu.SMEM] + [pltpu.VMEM] * 5,
    )
    return out.reshape(COLUMNS, DEPTH * half, 128)


def deliver(counts, returned, me=None):
    (out,) = run(
        bind(deliver_kernel, me),
        (counts, returned.reshape(COLUMNS * TILE, 128)),
        [((CELLS, SLOTS), F32)],
        [],
        me,
        [pltpu.SMEM, pltpu.VMEM],
    )
    return out.reshape(TILE, TILE, TILE, SLOTS)


def exchange(x):
    return lax.all_to_all(x, "mem", split_axis=0, concat_axis=0, tiled=True)


def on_device(phi_owned, band_counts, neighbours):
    received = exchange(pack(band_counts, phi_owned))
    masks = masks_of(neighbours)
    low, high, table = unpack(band_counts, received, masks)
    groups = lax.axis_size("grp")
    rising = [(g, g + 1) for g in range(groups - 1)]
    falling = [(g + 1, g) for g in range(groups - 1)]
    below = lax.ppermute(high, "grp", rising)
    above = lax.ppermute(low, "grp", falling)
    returned = exchange(march(table, below, low, high, above, masks))
    return deliver(band_counts, returned)


def solution(mesh):
    return jax.shard_map(
        on_device,
        mesh=mesh,
        in_specs=(P(None, None, None, ("grp", "mem")), P("grp", None), P("grp", None, None)),
        out_specs=P(None, None, None, ("grp", "mem")),
        check_vma=False,
    )
```

time: 174 us -> 75.4 us (0.43)
  starting transfers between devices: 78.9 us -> 18.1 us
  local copies, waits for them, and re-layouts: 45.6 us -> 1.63 us
  blocking collectives: 0 us -> 20.1 us
  other arithmetic: 13.3 us -> 0 us
  Pallas kernels: 0 us -> 13.1 us
  waiting for transfers between devices: 32.3 us -> 22.1 us
  between operations: 2.64 us -> 0.07 us
    ppermute x16 -> x2, starting transfers between devices: 48 us -> 7.13 us  [the longest x1 5.21 us: on_device(): below = lax.ppermute(high, 'grp', rising)]
    all_to_all x0 -> x1, blocking collectives: none -> 20.1 us  [exchange(): return lax.all_to_all(x, 'mem', split_axis=0, concat_axis=0, tiled=True)]
    all_to_all x2 -> x1, starting transfers between devices: 31 us -> 10.9 us  [exchange(): return lax.all_to_all(x, 'mem', split_axis=0, concat_axis=0, tiled=True)]
    unnamed x9 -> x7, local copies, waits for them, and re-layouts: 16.3 us -> 1.63 us
    pallas_call x0 -> x5, Pallas kernels: none -> 13.1 us  [run(): pl.pallas_call(kernel, out_shape=[jax.ShapeDtypeStruct(s, t) for s, t in...]
    all_to_all x3 -> x0, local copies, waits for them, and re-layouts: 10 us -> none  [the longest x2 5.17 us: on_device(): lax.all_to_all(outgoing(phi_owned, first_tile, columns), 'mem', split_axi...]
    gather x4 -> x0, local copies, waits for them, and re-layouts: 6.61 us -> none  [the longest x3 3.56 us: on_device(): jnp.take(received.reshape(tile_edge, tile_edge, tile_edge, own_slots), ar...]
    dynamic_slice x5 -> x0, local copies, waits for them, and re-layouts: 5.94 us -> none  [the longest x1 4.42 us: outgoing(): return jnp.roll(blocks, first_tile % columns, axis=-1)]
  transfers between devices with their start and end apart: 18 -> 3, of which waited for: 6 -> 2; matrix products, arithmetic and copies ran while one was open for 4% -> 0% of each run, Pallas kernels for 0% -> 0%
where the time goes in v1:
time: 75.4 us; the launch traced here: 75.1 us
  waiting for transfers between devices  22.1 us (29%)
  blocking collectives  20.1 us (27%)
  starting transfers between devices  18.1 us (24%)
  Pallas kernels  13.1 us (17%)
  local copies, waits for them, and re-layouts  1.63 us (2%)
    all_to_all x1, blocking collectives, exchange(): return lax.all_to_all(x, 'mem', split_axis=0, concat_axis=0, tiled=True)  20.1 us
    all_to_all x1, waiting for transfers between devices, exchange(): return lax.all_to_all(x, 'mem', split_axis=0, concat_axis=0, tiled=True)  17.5 us
    pallas_call x5, Pallas kernels, run(): pl.pallas_call(kernel, out_shape=[jax.ShapeDtypeStruct(s, t) for s, t in...  13.1 us
    all_to_all x1, starting transfers between devices, exchange(): return lax.all_to_all(x, 'mem', split_axis=0, concat_axis=0, tiled=True)  10.9 us
    ppermute x1, starting transfers between devices, on_device(): below = lax.ppermute(high, 'grp', rising)  5.21 us
    ppermute x1, waiting for transfers between devices, on_device(): above = lax.ppermute(low, 'grp', falling)  4.63 us
    ppermute x1, starting transfers between devices, on_device(): above = lax.ppermute(low, 'grp', falling)  1.92 us
    unnamed x7, local copies, waits for them, and re-layouts  1.63 us
  transfers between devices with their start and end apart: 3, of which 2 were waited for; matrix products, arithmetic and copies ran while one was open for 0% of the time, Pallas kernels for 0%

profile of v1, /device:TPU:193, one launch (start us, length us, event | category | flops | bytes accessed | tf_op | source)
XLA Modules:
  0.0 75.1 jit_solution(8872818988487336132)
XLA Ops:
  0.0 0.0 copy-start.1
  0.0 0.7 copy-done.1
  0.7 0.0 copy-start
  0.7 0.9 %copy-done = f32[8,8,8,128]{3,2,1,0:T(8,128)S(1)} copy-done((f32[8,8,8,128]{3,2,1,0:T(8,128)S(1)}, f32[8,8,8,128]{3,2,1,0:T(8,128)}, u32[]{:S(2)}) %copy-start) | copy-done | bytes 262168
  1.6 3.2 %pack_kernel.1 = f32[1024,128]{1,0:T(8,128)} custom-call(s32[1,64]{1,0:T(1,128)S(1)} %copy-done.1, f32[512,128]{1,0:T(8,128)S(1)} %bitcast.9), custom_call_target="tpu_custom_call" | custom-call | tf_op jit(solution)/shard_map/pack_kernel/pallas_call | solution.py:236
  4.8 0.0 copy-start.2
  4.8 10.9 %all-to-all-start = ((f32[64,16,128]{2,1,0:T(8,128)}), f32[64,16,128]{2,1,0:T(8,128)S(1)}, u32[]{:S(2)}, u32[]{:S(2)}) async-start(f32[64,16,128]{2,1,0:T(8,128)} %bitcast.1), calls=%async_computation | async-start | bytes 1048576 | tf_op jit(solution)/shard_map/all_to_all | solution.py:324
  15.7 0.0 copy-done.2
  15.8 0.2 mask_kernel.1.refs_2_.refs_5_
  16.0 17.5 %all-to-all-done = f32[64,16,128]{2,1,0:T(8,128)S(1)} async-done(((f32[64,16,128]{2,1,0:T(8,128)}), f32[64,16,128]{2,1,0:T(8,128)S(1)}, u32[]{:S(2)}, u32[]{:S(2)}) %all-to-all-start) | async-done | bytes 524320 | tf_op jit(solution)/shard_map/all_to_all | solution.py:324
  33.4 2.7 %unpack_kernel.1 = (f32[6,32,128]{2,1,0:T(8,128)S(1)}, f32[6,32,128]{2,1,0:T(8,128)S(1)}, s32[1,32]{1,0:T(1,128)S(1)}) custom-call(s32[1,64]{1,0:T(1,128)S(1)} %copy-done.1, f32[128,8,128]{2,1,0:T(8,128)S(1)} %bitcast.6, f32[4,32,128]{2,1,0:T(8,128)S(1)} %mask_kernel.1.refs_2_.refs_5_), custom_call_target="tpu_custom_call" | custom-call | tf_op jit(solution)/shard_map/unpack_kernel/pallas_call | solution.py:236
  36.1 5.2 %collective-permute-start = (f32[6,32,128]{2,1,0:T(8,128)S(1)}, f32[6,32,128]{2,1,0:T(8,128)S(1)}, u32[]{:S(2)}, u32[]{:S(2)}) collective-permute-start(f32[6,32,128]{2,1,0:T(8,128)S(1)} %get-tuple-element.9.refs_3_), channel_id=1, source_target_pairs={{0,64},{64,128},{128,192},{192,256},{256,320},{320,384},{384,448},... | collective-permute-start | bytes 294920 | tf_op jit(solution)/shard_map/ppermute | solution.py:334
  41.3 1.9 %collective-permute-start.1 = (f32[6,32,128]{2,1,0:T(8,128)S(1)}, f32[6,32,128]{2,1,0:T(8,128)S(1)}, u32[]{:S(2)}, u32[]{:S(2)}) collective-permute-start(f32[6,32,128]{2,1,0:T(8,128)S(1)} %get-tuple-element.10.refs_2_), channel_id=1, source_target_pairs={{64,0},{128,64},{192,128},{256,192},{320,256},{384,320},{448,384},... | collective-permute-start | bytes 294920 | tf_op jit(solution)/shard_map/ppermute | solution.py:335
  43.2 0.0 collective-permute-done.refs_1_
  43.3 4.6 %collective-permute-done.1.refs_4_ = f32[6,32,128]{2,1,0:T(8,128)S(1)} collective-permute-done((f32[6,32,128]{2,1,0:T(8,128)S(1)}, f32[6,32,128]{2,1,0:T(8,128)S(1)}, u32[]{:S(2)}, u32[]{:S(2)}) %collective-permute-start.1) | collective-permute-done | bytes 98336 | tf_op jit(solution)/shard_map/ppermute | solution.py:335
  47.9 5.5 %march_kernel.1 = f32[128,4,128]{2,1,0:T(4,128)S(1)} custom-call(s32[1,32]{1,0:T(1,128)S(1)} %get-tuple-element.8.refs_0_, f32[6,32,128]{2,1,0:T(8,128)S(1)} %collective-permute-done.refs_1_, f32[6,32,128]{2,1,0:T(8,128)S(1)} %get-tuple-element.10.refs_2_, f32[6,32,128]{2,1,0:T(8,128)S(1)} %get-tuple-element.9.refs_3_, ...), custom_call_target="tpu_custom_call" | custom-call | tf_op jit(solution)/shard_map/march_kernel/pallas_call | solution.py:236
  53.4 20.1 %all_to_all.10 = f32[64,8,128]{2,1,0:T(8,128)S(1)} all-to-all(f32[64,8,128]{2,1,0:T(8,128)S(1)} %bitcast.8), channel_id=1, replica_groups=mesh['grp'=8,'mem'=64] {'mem'}, dimensions={0} | all-to-all | bytes 524288 | tf_op jit(solution)/shard_map/all_to_all | solution.py:324
  73.5 1.6 %deliver_kernel.1 = f32[512,128]{1,0:T(8,128)} custom-call(s32[1,64]{1,0:T(1,128)S(1)} %copy-done.1, f32[512,128]{1,0:T(8,128)S(1)} %bitcast.7), custom_call_target="tpu_custom_call" | custom-call | tf_op jit(solution)/shard_map/deliver_kernel/pallas_call | solution.py:236
  (1 shorter events, 0.0 us)
Async XLA Ops:
  0.0 0.7 copy-start.1
  0.7 0.9 %copy-start = (f32[8,8,8,128]{3,2,1,0:T(8,128)S(1)}, f32[8,8,8,128]{3,2,1,0:T(8,128)}, u32[]{:S(2)}) copy-start(f32[8,8,8,128]{3,2,1,0:T(8,128)} %param.3) | copy-start | bytes 786436
  4.8 10.9 %copy-start.2 = (s32[1,6,2048]{2,0,1:T(1,128)S(1)}, s32[1,6,2048]{2,0,1:T(1,128)}, u32[]{:S(2)}) copy-start(s32[1,6,2048]{2,0,1:T(1,128)} %param.5) | copy-start | bytes 147460
  4.8 28.6 %all-to-all-start = ((f32[64,16,128]{2,1,0:T(8,128)}), f32[64,16,128]{2,1,0:T(8,128)S(1)}, u32[]{:S(2)}, u32[]{:S(2)}) async-start(f32[64,16,128]{2,1,0:T(8,128)} %bitcast.1), calls=%async_computation | async-start | bytes 1048576 | tf_op jit(solution)/shard_map/all_to_all | solution.py:324
  36.1 7.1 %collective-permute-start = (f32[6,32,128]{2,1,0:T(8,128)S(1)}, f32[6,32,128]{2,1,0:T(8,128)S(1)}, u32[]{:S(2)}, u32[]{:S(2)}) collective-permute-start(f32[6,32,128]{2,1,0:T(8,128)S(1)} %get-tuple-element.9.refs_3_), channel_id=1, source_target_pairs={{0,64},{64,128},{128,192},{192,256},{256,320},{320,384},{384,448},... | collective-permute-start | bytes 294920 | tf_op jit(solution)/shard_map/ppermute | solution.py:334
  41.3 6.6 %collective-permute-start.1 = (f32[6,32,128]{2,1,0:T(8,128)S(1)}, f32[6,32,128]{2,1,0:T(8,128)S(1)}, u32[]{:S(2)}, u32[]{:S(2)}) collective-permute-start(f32[6,32,128]{2,1,0:T(8,128)S(1)} %get-tuple-element.10.refs_2_), channel_id=1, source_target_pairs={{64,0},{128,64},{192,128},{256,192},{320,256},{384,320},{448,384},... | collective-permute-start | bytes 294920 | tf_op jit(solution)/shard_map/ppermute | solution.py:335

commit v2 on v1

--- a/solution.py
+++ b/solution.py
@@ -40,18 +40,30 @@
 
 
 def pack_kernel(where_am_i, *refs):
-    counts_ref, phi_ref, out_ref = refs[-3:]
+    counts_hbm, phi_hbm, out_ref, counts_ref, phi_ref, sems = refs[-6:]
+    half = TILE // 2
+    copies = [
+        pltpu.make_async_copy(counts_hbm, counts_ref, sems.at[0]),
+        pltpu.make_async_copy(phi_hbm.at[pl.ds(half, half)], phi_ref.at[pl.ds(0, half)], sems.at[1]),
+        pltpu.make_async_copy(phi_hbm.at[pl.ds(0, half)], phi_ref.at[pl.ds(half, half)], sems.at[2]),
+    ]
+    for copy in copies:
+        copy.start()
+    copies[0].wait()
     turn = own_start(counts_ref, where_am_i(refs)) & (COLUMNS - 1)
-    low_half = iota((TILE, SLOTS), 0) < TILE // 2
+    copies[1].wait()
+    copies[2].wait()
+    layers = phi_ref.reshape(CELLS, SLOTS)
+    low_half = iota((TILE, SLOTS), 0) < half
     for z in range(TILE):
         blocks = []
         for y in range(TILE):
-            tiles = phi_ref[pl.ds(y * TILE + z, TILE, stride=TILE * TILE), :]
+            tiles = layers[pl.ds(y * TILE + z, TILE, stride=TILE * TILE), :]
             here = pltpu.roll(tiles, turn, 1)
             left = shift(here, 1, 1)
             right = shift(here, -1, 1)
-            blocks.append(shift(jnp.where(low_half, here, left), 4, 0))
-            blocks.append(shift(jnp.where(low_half, right, here), 4, 0))
+            blocks.append(jnp.where(low_half, left, here))
+            blocks.append(jnp.where(low_half, here, right))
         turned = jnp.concatenate(blocks, axis=0).T
         for d in range(DEPTH):
             out_ref[pl.ds(d * TILE + z, COLUMNS, stride=DEPTH * TILE), :] = turned[
@@ -60,8 +72,9 @@
 
 
 def mask_kernel(where_am_i, *refs):
-    links_ref, out_ref, lhs_ref, found_ref = refs[-4:]
+    counts_ref, links_ref, out_ref, table_ref, lhs_ref, found_ref = refs[-6:]
     me = where_am_i(refs)
+    fill_table(counts_ref, table_ref, me)
     pairs = ROWS // 2
     for v in range(pairs):
         lhs_ref[v * 8 : v * 8 + 6, :] = jnp.where(
@@ -110,9 +123,8 @@
     lax.fori_loop(0, COLUMNS, body, jnp.int32(0), unroll=8)
 
 
-def unpack_kernel(where_am_i, *refs):
-    counts_ref, received_ref, masks_ref, low_ref, high_ref, table_out_ref, table_ref, tiles_ref = refs[-8:]
-    fill_table(counts_ref, table_ref, where_am_i(refs))
+def unpack_kernel(*refs):
+    table_ref, received_ref, masks_ref, low_ref, high_ref, tiles_ref = refs
     x16 = iota((TILE, 128), 1) % WIDE
     for r in range(ROWS):
         left = received_ref[table_ref[0, r + 1]]
@@ -120,7 +132,6 @@
         right = received_ref[table_ref[2, r + 1]]
         tile = jnp.where(x16 < 4, left, jnp.where(x16 >= 12, right, here))
         tiles_ref[pl.ds(r, TILE, stride=ROWS), :] = tile
-        table_out_ref[0, r] = table_ref[1, r + 1]
     half = TILE // 2
     for z in range(half):
         low_ref[z] = tiles_ref[z * ROWS : (z + 1) * ROWS, :]
@@ -199,7 +210,7 @@
             left_half, shift(final_ref[half + q], -4, 1), shift(final_ref[2 * half + q], 4, 1)
         )
     for r in range(ROWS):
-        out_ref[table_ref[0, r]] = done_ref[pl.ds(r, half, stride=ROWS), :]
+        out_ref[table_ref[1, r + 1]] = done_ref[pl.ds(r, half, stride=ROWS), :]
 
 
 def deliver_kernel(where_am_i, *refs):
@@ -227,7 +238,9 @@
     return pl.BlockSpec(memory_space=space)
 
 
-def run(kernel, operands, shapes, scratch, me=None, spaces=None, out_spaces=None, cost=(0, 0)):
+def run(
+    kernel, operands, shapes, scratch, me=None, spaces=None, out_spaces=None, cost=(0, 0), grant=32
+):
     spaces = spaces or [pltpu.VMEM] * len(operands)
     out_spaces = out_spaces or [pltpu.VMEM] * len(shapes)
     if me is not None:
@@ -239,7 +252,7 @@
         in_specs=[spec(s) for s in spaces],
         out_specs=[spec(s) for s in out_spaces],
         scratch_shapes=scratch,
-        compiler_params=pltpu.CompilerParams(vmem_limit_bytes=32 << 20),
+        compiler_params=pltpu.CompilerParams(vmem_limit_bytes=grant << 20),
         cost_estimate=pl.CostEstimate(flops=cost[0], bytes_accessed=cost[1], transcendentals=0),
         name=getattr(kernel, "func", kernel).__name__,
     )(*operands)
@@ -259,39 +272,45 @@
 
 
 def pack(counts, phi, me=None):
+    layers = (TILE, TILE * TILE, SLOTS)
     (out,) = run(
         bind(pack_kernel, me),
-        (counts, phi.reshape(CELLS, SLOTS)),
+        (counts, phi.reshape(layers)),
         [((COLUMNS * DEPTH * TILE, 128), F32)],
-        [],
+        [
+            pltpu.SMEM((1, COLUMNS), I32),
+            pltpu.VMEM(layers, F32),
+            pltpu.SemaphoreType.DMA((3,)),
+        ],
+        me,
+        [pltpu.HBM, pltpu.HBM],
+        grant=62,
+    )
+    return out.reshape(COLUMNS, DEPTH * TILE, 128)
+
+
+def masks_of(counts, neighbours, me=None):
+    return run(
+        bind(mask_kernel, me),
+        (counts, neighbours),
+        [((4, ROWS, 128), F32), ((3, TABLE), I32)],
+        [pltpu.VMEM((128, 128), F32), pltpu.VMEM((8 * ROWS, 128), F32)],
         me,
         [pltpu.SMEM, pltpu.VMEM],
-    )
-    return out.reshape(COLUMNS, DEPTH * TILE, 128)
-
-
-def masks_of(neighbours, me=None):
-    (out,) = run(
-        bind(mask_kernel, me),
-        (neighbours,),
-        [((4, ROWS, 128), F32)],
-        [pltpu.VMEM((128, 128), F32), pltpu.VMEM((8 * ROWS, 128), F32)],
-        me,
+        [pltpu.VMEM, pltpu.SMEM],
         cost=(1 << 22, 1 << 17),
     )
-    return out
-
-
-def unpack(counts, received, masks, me=None):
+
+
+def unpack(table, received, masks):
     half = TILE // 2
     return run(
-        bind(unpack_kernel, me),
-        (counts, received.reshape(COLUMNS * DEPTH, TILE, 128), masks),
-        [((half + 2, ROWS, 128), F32), ((half + 2, ROWS, 128), F32), ((1, ROWS), I32)],
-        [pltpu.SMEM((3, TABLE), I32), pltpu.VMEM((TILE * ROWS, 128), F32)],
-        me,
+        unpack_kernel,
+        (table, received.reshape(COLUMNS * DEPTH, TILE, 128), masks),
+        [((half + 2, ROWS, 128), F32), ((half + 2, ROWS, 128), F32)],
+        [pltpu.VMEM((TILE * ROWS, 128), F32)],
+        None,
         [pltpu.SMEM, pltpu.VMEM, pltpu.VMEM],
-        [pltpu.VMEM, pltpu.VMEM, pltpu.SMEM],
     )
 
 
@@ -326,8 +345,8 @@
 
 def on_device(phi_owned, band_counts, neighbours):
     received = exchange(pack(band_counts, phi_owned))
-    masks = masks_of(neighbours)
-    low, high, table = unpack(band_counts, received, masks)
+    masks, table = masks_of(band_counts, neighbours)
+    low, high = unpack(table, received, masks)
     groups = lax.axis_size("grp")
     rising = [(g, g + 1) for g in range(groups - 1)]
     falling = [(g + 1, g) for g in range(groups - 1)]

time: 75.4 us -> 72.6 us (0.963)
  waiting for transfers between devices: 22.1 us -> 19.2 us
  Pallas kernels: 13.1 us -> 14.2 us
  local copies, waits for them, and re-layouts: 1.63 us -> 0.65 us
    all_to_all x1, waiting for transfers between devices: 17.5 us -> 14.5 us  [exchange(): return lax.all_to_all(x, 'mem', split_axis=0, concat_axis=0, tiled=True)]
    pallas_call x5, Pallas kernels: 13.1 us -> 14.2 us  [run(): pl.pallas_call(kernel, out_shape=[jax.ShapeDtypeStruct(s, t) for s, t in...]
    unnamed x7 -> x5, local copies, waits for them, and re-layouts: 1.63 us -> 0.65 us
  transfers between devices with their start and end apart: 3 -> 3, of which waited for: 2 -> 2; matrix products, arithmetic and copies ran while one was open for 0% -> 0% of each run, Pallas kernels for 0% -> 3%
where the time goes in v2:
time: 72.6 us; the launch traced here: 72.3 us
  blocking collectives  20.1 us (28%)
  waiting for transfers between devices  19.2 us (26%)
  starting transfers between devices  18.1 us (25%)
  Pallas kernels  14.2 us (20%)
    all_to_all x1, blocking collectives, exchange(): return lax.all_to_all(x, 'mem', split_axis=0, concat_axis=0, tiled=True)  20.1 us
    all_to_all x1, waiting for transfers between devices, exchange(): return lax.all_to_all(x, 'mem', split_axis=0, concat_axis=0, tiled=True)  14.5 us
    pallas_call x5, Pallas kernels, run(): pl.pallas_call(kernel, out_shape=[jax.ShapeDtypeStruct(s, t) for s, t in...  14.2 us
    all_to_all x1, starting transfers between devices, exchange(): return lax.all_to_all(x, 'mem', split_axis=0, concat_axis=0, tiled=True)  10.9 us
    ppermute x1, starting transfers between devices, on_device(): below = lax.ppermute(high, 'grp', rising)  5.21 us
    ppermute x1, waiting for transfers between devices, on_device(): above = lax.ppermute(low, 'grp', falling)  4.63 us
    ppermute x1, starting transfers between devices, on_device(): above = lax.ppermute(low, 'grp', falling)  1.92 us
  transfers between devices with their start and end apart: 3, of which 2 were waited for; matrix products, arithmetic and copies ran while one was open for 0% of the time, Pallas kernels for 3%

profile of v2, /device:TPU:193, one launch (start us, length us, event | category | flops | bytes accessed | tf_op | source)
XLA Modules:
  0.0 72.3 jit_solution(11956365775922339211)
XLA Ops:
  0.0 3.8 %pack_kernel.1 = f32[1024,128]{1,0:T(8,128)} custom-call(s32[1,64]{1,0:T(1,128)} %refs_0_.5, f32[8,64,128]{2,1,0:T(8,128)} %bitcast.10), custom_call_target="tpu_custom_call" | custom-call | tf_op jit(solution)/shard_map/pack_kernel/pallas_call | solution.py:249
  3.9 0.0 copy-start.1
  3.9 10.9 %all-to-all-start = ((f32[64,16,128]{2,1,0:T(8,128)}), f32[64,16,128]{2,1,0:T(8,128)S(1)}, u32[]{:S(2)}, u32[]{:S(2)}) async-start(f32[64,16,128]{2,1,0:T(8,128)} %bitcast.9), calls=%async_computation | async-start | bytes 1048576 | tf_op jit(solution)/shard_map/all_to_all | solution.py:343
  14.8 0.0 copy-done.1
  14.8 0.0 copy-start
  14.9 0.6 copy-done
  15.5 2.5 %mask_kernel.1 = (f32[4,32,128]{2,1,0:T(8,128)S(1)}, s32[3,40]{1,0:T(4,128)S(1)}) custom-call(s32[1,64]{1,0:T(1,128)S(1)} %copy-done, s32[1,6,2048]{2,1,0:T(8,128)S(1)} %copy.4.refs_1_), custom_call_target="tpu_custom_call" | custom-call | flops 4194304 | bytes 131072 | tf_op jit(solution)/shard_map/mask_kernel/pallas_call | solution.py:249
  18.0 14.5 %all-to-all-done = f32[64,16,128]{2,1,0:T(8,128)S(1)} async-done(((f32[64,16,128]{2,1,0:T(8,128)}), f32[64,16,128]{2,1,0:T(8,128)S(1)}, u32[]{:S(2)}, u32[]{:S(2)}) %all-to-all-start) | async-done | bytes 524320 | tf_op jit(solution)/shard_map/all_to_all | solution.py:343
  32.5 0.7 unpack_kernel.1
  33.2 5.2 %collective-permute-start = (f32[6,32,128]{2,1,0:T(8,128)S(1)}, f32[6,32,128]{2,1,0:T(8,128)S(1)}, u32[]{:S(2)}, u32[]{:S(2)}) collective-permute-start(f32[6,32,128]{2,1,0:T(8,128)S(1)} %get-tuple-element.11.refs_3_), channel_id=1, source_target_pairs={{0,64},{64,128},{128,192},{192,256},{256,320},{320,384},{384,448},... | collective-permute-start | bytes 294920 | tf_op jit(solution)/shard_map/ppermute | solution.py:353
  38.5 1.9 %collective-permute-start.1 = (f32[6,32,128]{2,1,0:T(8,128)S(1)}, f32[6,32,128]{2,1,0:T(8,128)S(1)}, u32[]{:S(2)}, u32[]{:S(2)}) collective-permute-start(f32[6,32,128]{2,1,0:T(8,128)S(1)} %get-tuple-element.12.refs_2_), channel_id=1, source_target_pairs={{64,0},{128,64},{192,128},{256,192},{320,256},{384,320},{448,384},... | collective-permute-start | bytes 294920 | tf_op jit(solution)/shard_map/ppermute | solution.py:354
  40.4 0.0 collective-permute-done.refs_1_
  40.4 4.6 %collective-permute-done.1.refs_4_ = f32[6,32,128]{2,1,0:T(8,128)S(1)} collective-permute-done((f32[6,32,128]{2,1,0:T(8,128)S(1)}, f32[6,32,128]{2,1,0:T(8,128)S(1)}, u32[]{:S(2)}, u32[]{:S(2)}) %collective-permute-start.1) | collective-permute-done | bytes 98336 | tf_op jit(solution)/shard_map/ppermute | solution.py:354
  45.0 5.5 %march_kernel.1 = f32[128,4,128]{2,1,0:T(4,128)S(1)} custom-call(s32[3,40]{1,0:T(4,128)S(1)} %get-tuple-element.9.refs_0_, f32[6,32,128]{2,1,0:T(8,128)S(1)} %collective-permute-done.refs_1_, f32[6,32,128]{2,1,0:T(8,128)S(1)} %get-tuple-element.12.refs_2_, f32[6,32,128]{2,1,0:T(8,128)S(1)} %get-tuple-element.11.refs_3_, ...), custom_call_target="tpu_custom_call" | custom-call | tf_op jit(solution)/shard_map/march_kernel/pallas_call | solution.py:249
  50.6 20.1 %all_to_all.10 = f32[64,8,128]{2,1,0:T(8,128)S(1)} all-to-all(f32[64,8,128]{2,1,0:T(8,128)S(1)} %bitcast.8), channel_id=1, replica_groups=mesh['grp'=8,'mem'=64] {'mem'}, dimensions={0} | all-to-all | bytes 524288 | tf_op jit(solution)/shard_map/all_to_all | solution.py:343
  70.7 1.6 %deliver_kernel.1 = f32[512,128]{1,0:T(8,128)} custom-call(s32[1,64]{1,0:T(1,128)S(1)} %copy-done, f32[512,128]{1,0:T(8,128)S(1)} %bitcast.7), custom_call_target="tpu_custom_call" | custom-call | tf_op jit(solution)/shard_map/deliver_kernel/pallas_call | solution.py:249
  (1 shorter events, 0.0 us)
Async XLA Ops:
  3.9 11.0 %copy-start.1 = (s32[1,6,2048]{2,0,1:T(1,128)S(1)}, s32[1,6,2048]{2,0,1:T(1,128)}, u32[]{:S(2)}) copy-start(s32[1,6,2048]{2,0,1:T(1,128)} %param.5) | copy-start | bytes 147460
  3.9 28.7 %all-to-all-start = ((f32[64,16,128]{2,1,0:T(8,128)}), f32[64,16,128]{2,1,0:T(8,128)S(1)}, u32[]{:S(2)}, u32[]{:S(2)}) async-start(f32[64,16,128]{2,1,0:T(8,128)} %bitcast.9), calls=%async_computation | async-start | bytes 1048576 | tf_op jit(solution)/shard_map/all_to_all | solution.py:343
  14.8 0.7 copy-start
  33.2 7.1 %collective-permute-start = (f32[6,32,128]{2,1,0:T(8,128)S(1)}, f32[6,32,128]{2,1,0:T(8,128)S(1)}, u32[]{:S(2)}, u32[]{:S(2)}) collective-permute-start(f32[6,32,128]{2,1,0:T(8,128)S(1)} %get-tuple-element.11.refs_3_), channel_id=1, source_target_pairs={{0,64},{64,128},{128,192},{192,256},{256,320},{320,384},{384,448},... | collective-permute-start | bytes 294920 | tf_op jit(solution)/shard_map/ppermute | solution.py:353
  38.5 6.6 %collective-permute-start.1 = (f32[6,32,128]{2,1,0:T(8,128)S(1)}, f32[6,32,128]{2,1,0:T(8,128)S(1)}, u32[]{:S(2)}, u32[]{:S(2)}) collective-permute-start(f32[6,32,128]{2,1,0:T(8,128)S(1)} %get-tuple-element.12.refs_2_), channel_id=1, source_target_pairs={{64,0},{128,64},{192,128},{256,192},{320,256},{384,320},{448,384},... | collective-permute-start | bytes 294920 | tf_op jit(solution)/shard_map/ppermute | solution.py:354

commit v3 on v2

--- a/solution.py
+++ b/solution.py
@@ -162,21 +162,23 @@
     sources = (below_ref, low_ref, high_ref, above_ref)
     for z in range(1, 2 * TILE - 1):
         level = sources[z // half][z % half]
-        sign_ref[z] = level / jnp.sqrt(level * level + 1.0)
+        sign_ref[z] = level * lax.rsqrt(level * level + 1.0)
 
     def load(step, z):
         if step == 0:
             return sources[z // half][z % half]
         return (odd_ref if step % 2 else even_ref)[z]
 
-    for step in range(STEPS):
+    def one_step(step, lo, hi):
         target_ref = even_ref if step % 2 else odd_ref
-        level = load(step, step)
-        after = load(step, step + 1)
+        level = load(step, lo - 1)
+        after = load(step, lo)
         ahead_z = after - level
-        if step == 3:
+        if lo == 4:
             ahead_z = ahead_z * masks_ref[2]
-        for z in range(step + 1, 2 * TILE - 1 - step):
+        if lo == 12:
+            ahead_z = ahead_z * masks_ref[3]
+        for z in range(lo, hi):
             back_z = ahead_z
             level = after
             after = load(step, z + 1)
@@ -202,7 +204,14 @@
             squares = squares + jnp.square(
                 jnp.maximum(jnp.maximum(up * back_z, down * ahead_z), 0.0)
             )
-            target_ref[z] = level - TIME_STEP * sign_field * (jnp.sqrt(squares + EPSILON) - 1.0)
+            length = squares + EPSILON
+            target_ref[z] = level - TIME_STEP * sign_field * (length * lax.rsqrt(length) - 1.0)
+
+    first, last = 1, 2 * TILE - 1
+    for step in range(STEPS):
+        middle = TILE
+        for lo, hi in ((first + step, middle), (middle, last - step)):
+            pl.when(table_ref[1, 1] >= 0)(functools.partial(one_step, step, lo, hi))
     final_ref = even_ref
     left_half = lane % WIDE < TILE
     for q in range(half):

time: 72.6 us -> 69.6 us (0.959)
  Pallas kernels: 14.2 us -> 11.2 us
    pallas_call x5, Pallas kernels: 14.2 us -> 11.2 us  [run(): pl.pallas_call(kernel, out_shape=[jax.ShapeDtypeStruct(s, t) for s, t in...]
  transfers between devices with their start and end apart: 3 -> 3, of which waited for: 2 -> 2; matrix products, arithmetic and copies ran while one was open for 0% -> 0% of each run, Pallas kernels for 3% -> 4%
where the time goes in v3:
time: 69.6 us; the launch traced here: 69.3 us
  blocking collectives  20.1 us (29%)
  waiting for transfers between devices  19.2 us (28%)
  starting transfers between devices  18.1 us (26%)
  Pallas kernels  11.2 us (16%)
    all_to_all x1, blocking collectives, exchange(): return lax.all_to_all(x, 'mem', split_axis=0, concat_axis=0, tiled=True)  20.1 us
    all_to_all x1, waiting for transfers between devices, exchange(): return lax.all_to_all(x, 'mem', split_axis=0, concat_axis=0, tiled=True)  14.5 us
    pallas_call x5, Pallas kernels, run(): pl.pallas_call(kernel, out_shape=[jax.ShapeDtypeStruct(s, t) for s, t in...  11.2 us
    all_to_all x1, starting transfers between devices, exchange(): return lax.all_to_all(x, 'mem', split_axis=0, concat_axis=0, tiled=True)  10.9 us
    ppermute x1, starting transfers between devices, on_device(): below = lax.ppermute(high, 'grp', rising)  5.21 us
    ppermute x1, waiting for transfers between devices, on_device(): above = lax.ppermute(low, 'grp', falling)  4.63 us
    ppermute x1, starting transfers between devices, on_device(): above = lax.ppermute(low, 'grp', falling)  1.92 us
  transfers between devices with their start and end apart: 3, of which 2 were waited for; matrix products, arithmetic and copies ran while one was open for 0% of the time, Pallas kernels for 4%

profile of v3, /device:TPU:193, one launch (start us, length us, event | category | flops | bytes accessed | tf_op | source)
XLA Modules:
  0.0 69.3 jit_solution(14061015021281749767)
XLA Ops:
  0.0 3.8 %pack_kernel.1 = f32[1024,128]{1,0:T(8,128)} custom-call(s32[1,64]{1,0:T(1,128)} %refs_0_.5, f32[8,64,128]{2,1,0:T(8,128)} %bitcast.10), custom_call_target="tpu_custom_call" | custom-call | tf_op jit(solution)/shard_map/pack_kernel/pallas_call | solution.py:258
  3.9 0.0 copy-start.1
  3.9 10.9 %all-to-all-start = ((f32[64,16,128]{2,1,0:T(8,128)}), f32[64,16,128]{2,1,0:T(8,128)S(1)}, u32[]{:S(2)}, u32[]{:S(2)}) async-start(f32[64,16,128]{2,1,0:T(8,128)} %bitcast.9), calls=%async_computation | async-start | bytes 1048576 | tf_op jit(solution)/shard_map/all_to_all | solution.py:352
  14.8 0.0 copy-done.1
  14.8 0.0 copy-start
  14.9 0.6 copy-done
  15.5 2.5 %mask_kernel.1 = (f32[4,32,128]{2,1,0:T(8,128)S(1)}, s32[3,40]{1,0:T(4,128)S(1)}) custom-call(s32[1,64]{1,0:T(1,128)S(1)} %copy-done, s32[1,6,2048]{2,1,0:T(8,128)S(1)} %copy.4.refs_1_), custom_call_target="tpu_custom_call" | custom-call | flops 4194304 | bytes 131072 | tf_op jit(solution)/shard_map/mask_kernel/pallas_call | solution.py:258
  18.0 14.5 %all-to-all-done = f32[64,16,128]{2,1,0:T(8,128)S(1)} async-done(((f32[64,16,128]{2,1,0:T(8,128)}), f32[64,16,128]{2,1,0:T(8,128)S(1)}, u32[]{:S(2)}, u32[]{:S(2)}) %all-to-all-start) | async-done | bytes 524320 | tf_op jit(solution)/shard_map/all_to_all | solution.py:352
  32.5 0.7 %unpack_kernel.1 = (f32[6,32,128]{2,1,0:T(8,128)S(1)}, f32[6,32,128]{2,1,0:T(8,128)S(1)}) custom-call(s32[3,40]{1,0:T(4,128)S(1)} %get-tuple-element.9.refs_0_, f32[128,8,128]{2,1,0:T(8,128)S(1)} %bitcast.6, f32[4,32,128]{2,1,0:T(8,128)S(1)} %get-tuple-element.10.refs_2_.refs_5_), custom_call_target="tpu_custom_call" | custom-call | tf_op jit(solution)/shard_map/unpack_kernel/pallas_call | solution.py:258
  33.2 5.2 %collective-permute-start = (f32[6,32,128]{2,1,0:T(8,128)S(1)}, f32[6,32,128]{2,1,0:T(8,128)S(1)}, u32[]{:S(2)}, u32[]{:S(2)}) collective-permute-start(f32[6,32,128]{2,1,0:T(8,128)S(1)} %get-tuple-element.11.refs_3_), channel_id=1, source_target_pairs={{0,64},{64,128},{128,192},{192,256},{256,320},{320,384},{384,448},... | collective-permute-start | bytes 294920 | tf_op jit(solution)/shard_map/ppermute | solution.py:362
  38.5 1.9 %collective-permute-start.1 = (f32[6,32,128]{2,1,0:T(8,128)S(1)}, f32[6,32,128]{2,1,0:T(8,128)S(1)}, u32[]{:S(2)}, u32[]{:S(2)}) collective-permute-start(f32[6,32,128]{2,1,0:T(8,128)S(1)} %get-tuple-element.12.refs_2_), channel_id=1, source_target_pairs={{64,0},{128,64},{192,128},{256,192},{320,256},{384,320},{448,384},... | collective-permute-start | bytes 294920 | tf_op jit(solution)/shard_map/ppermute | solution.py:363
  40.4 0.0 collective-permute-done.refs_1_
  40.4 4.6 %collective-permute-done.1.refs_4_ = f32[6,32,128]{2,1,0:T(8,128)S(1)} collective-permute-done((f32[6,32,128]{2,1,0:T(8,128)S(1)}, f32[6,32,128]{2,1,0:T(8,128)S(1)}, u32[]{:S(2)}, u32[]{:S(2)}) %collective-permute-start.1) | collective-permute-done | bytes 98336 | tf_op jit(solution)/shard_map/ppermute | solution.py:363
  45.0 2.5 %march_kernel.1 = f32[128,4,128]{2,1,0:T(4,128)S(1)} custom-call(s32[3,40]{1,0:T(4,128)S(1)} %get-tuple-element.9.refs_0_, f32[6,32,128]{2,1,0:T(8,128)S(1)} %collective-permute-done.refs_1_, f32[6,32,128]{2,1,0:T(8,128)S(1)} %get-tuple-element.12.refs_2_, f32[6,32,128]{2,1,0:T(8,128)S(1)} %get-tuple-element.11.refs_3_, ...), custom_call_target="tpu_custom_call" | custom-call | tf_op jit(solution)/shard_map/march_kernel/pallas_call | solution.py:258
  47.6 20.1 %all_to_all.10 = f32[64,8,128]{2,1,0:T(8,128)S(1)} all-to-all(f32[64,8,128]{2,1,0:T(8,128)S(1)} %bitcast.8), channel_id=1, replica_groups=mesh['grp'=8,'mem'=64] {'mem'}, dimensions={0} | all-to-all | bytes 524288 | tf_op jit(solution)/shard_map/all_to_all | solution.py:352
  67.7 1.6 %deliver_kernel.1 = f32[512,128]{1,0:T(8,128)} custom-call(s32[1,64]{1,0:T(1,128)S(1)} %copy-done, f32[512,128]{1,0:T(8,128)S(1)} %bitcast.7), custom_call_target="tpu_custom_call" | custom-call | tf_op jit(solution)/shard_map/deliver_kernel/pallas_call | solution.py:258
  (1 shorter events, 0.0 us)
Async XLA Ops:
  3.9 11.0 %copy-start.1 = (s32[1,6,2048]{2,0,1:T(1,128)S(1)}, s32[1,6,2048]{2,0,1:T(1,128)}, u32[]{:S(2)}) copy-start(s32[1,6,2048]{2,0,1:T(1,128)} %param.5) | copy-start | bytes 147460
  3.9 28.7 %all-to-all-start = ((f32[64,16,128]{2,1,0:T(8,128)}), f32[64,16,128]{2,1,0:T(8,128)S(1)}, u32[]{:S(2)}, u32[]{:S(2)}) async-start(f32[64,16,128]{2,1,0:T(8,128)} %bitcast.9), calls=%async_computation | async-start | bytes 1048576 | tf_op jit(solution)/shard_map/all_to_all | solution.py:352
  14.8 0.7 copy-start
  33.2 7.2 %collective-permute-start = (f32[6,32,128]{2,1,0:T(8,128)S(1)}, f32[6,32,128]{2,1,0:T(8,128)S(1)}, u32[]{:S(2)}, u32[]{:S(2)}) collective-permute-start(f32[6,32,128]{2,1,0:T(8,128)S(1)} %get-tuple-element.11.refs_3_), channel_id=1, source_target_pairs={{0,64},{64,128},{128,192},{192,256},{256,320},{320,384},{384,448},... | collective-permute-start | bytes 294920 | tf_op jit(solution)/shard_map/ppermute | solution.py:362
  38.5 6.6 %collective-permute-start.1 = (f32[6,32,128]{2,1,0:T(8,128)S(1)}, f32[6,32,128]{2,1,0:T(8,128)S(1)}, u32[]{:S(2)}, u32[]{:S(2)}) collective-permute-start(f32[6,32,128]{2,1,0:T(8,128)S(1)} %get-tuple-element.12.refs_2_), channel_id=1, source_target_pairs={{64,0},{128,64},{192,128},{256,192},{320,256},{384,320},{448,384},... | collective-permute-start | bytes 294920 | tf_op jit(solution)/shard_map/ppermute | solution.py:363

commit v4 on v2

v4 whole, which is shorter than its diff:
```python
import functools

import jax
import jax.numpy as jnp
from jax import lax
from jax.experimental import pallas as pl
from jax.experimental.pallas import tpu as pltpu
from jax.sharding import PartitionSpec as P

STEPS = 4
TIME_STEP = 0.5
EPSILON = 1e-06

TILE = 8
ROWS = 32
COLUMNS = 64
SLOTS = 128
CELLS = TILE**3
DEPTH = SLOTS // COLUMNS
WIDE = 16
TABLE = 40
HALF = TILE // 2
PAIRS = HALF // 2
SENT = 3 * DEPTH * PAIRS
BACK = 2 * DEPTH * PAIRS

F32 = jnp.float32
I32 = jnp.int32


def shift(x, amount, axis):
    return pltpu.roll(x, amount % x.shape[axis] if isinstance(amount, int) else amount, axis)


def iota(shape, axis):
    return lax.broadcasted_iota(I32, shape, axis)


def own_start(counts_ref, me):
    total = jnp.int32(0)
    for owner in range(COLUMNS - 1):
        total = total + jnp.where(owner < me, counts_ref[0, owner], 0)
    return total


def plane_of(core, pair, upper):
    w = pair + PAIRS * upper
    return TILE - 1 - w if core else w


def pack_kernel(where_am_i, *refs):
    counts_hbm, phi_hbm, out_ref, counts_ref, phi_ref, turned_ref, sems = refs[-7:]
    copies = [
        pltpu.make_async_copy(counts_hbm, counts_ref, sems.at[0]),
        pltpu.make_async_copy(phi_hbm, phi_ref, sems.at[1]),
    ]
    for copy in copies:
        copy.start()
    copies[0].wait()
    turn = own_start(counts_ref, where_am_i(refs)) & (COLUMNS - 1)
    copies[1].wait()
    chips = COLUMNS // 2
    upper_x = iota((chips, 128), 1) % TILE >= HALF
    for core in range(2):
        for pair in range(PAIRS):
            blocks = []
            for y in range(TILE):
                for upper in range(2):
                    z = plane_of(core, pair, upper)
                    tiles = phi_ref[pl.ds(y * TILE + z, TILE, stride=TILE * TILE), :]
                    blocks.append(pltpu.roll(tiles, turn, 1))
            turned = jnp.concatenate(blocks, axis=0).T
            held_ref = turned_ref.at[core * PAIRS + pair]
            held_ref[8 : 8 + SLOTS, :] = turned
            held_ref[7:8, :] = turned[SLOTS - 1 :]
            held_ref[8 + SLOTS : 9 + SLOTS, :] = turned[:1]
            for d in range(DEPTH):
                first = 8 + d * COLUMNS
                base = core * SENT + d * PAIRS + pair
                for column in range(2):
                    out_ref[
                        pl.ds(base + column * DEPTH * PAIRS, chips, stride=2 * SENT), :
                    ] = held_ref[pl.ds(first + column, chips, stride=2), :]
                left = held_ref[pl.ds(first - 1, chips, stride=2), :]
                right = held_ref[pl.ds(first + 2, chips, stride=2), :]
                out_ref[pl.ds(base + 2 * DEPTH * PAIRS, chips, stride=2 * SENT), :] = jnp.where(
                    upper_x, left, right
                )


def fill_table(counts_ref, table_ref, column):
    for entry in range(6):
        table_ref[entry, 1] = jnp.int32(0)
        table_ref[entry, ROWS] = jnp.int32(0)

    def body(owner, start):
        turn = start & (COLUMNS - 1)
        for entry, delta in enumerate((0, 1, -1, 2)):
            first = (column + delta - turn) & (COLUMNS - 1)
            row = (start + first - delta) >> 6
            slot = ((first + turn - delta) & (SLOTS - 1)) >> 6
            base = owner * (3 * DEPTH) + min(entry, 2) * DEPTH
            table_ref[entry, row + 1] = base + slot
            table_ref[entry, row + 2] = base + (1 - slot)
            if entry < 2:
                base = owner * (2 * DEPTH) + entry * DEPTH
                table_ref[4 + entry, row + 1] = base + slot
                table_ref[4 + entry, row + 2] = base + (1 - slot)
        return start + counts_ref[0, owner]

    lax.fori_loop(0, COLUMNS, body, jnp.int32(0), unroll=8)


def mask_kernel(where_am_i, *refs):
    counts_ref, links_ref, flat_ref, outer_ref, table_ref, lhs_ref, found_ref = refs[-7:]
    me = where_am_i(refs)
    chip, core = me >> 1, me & 1
    fill_table(counts_ref, table_ref, 2 * chip)
    blocks = ROWS // 2
    for v in range(blocks):
        lhs_ref[v * 8 : v * 8 + 6, :] = jnp.where(
            links_ref[0, :, v * 128 : (v + 1) * 128] >= 0, 1.0, 0.0
        )
        lhs_ref[v * 8 + 6 : v * 8 + 8, :] = jnp.zeros((2, 128), F32)
    source = iota((128, 256), 0)
    target = iota((128, 256), 1)
    x16 = target % WIDE
    lane = iota((ROWS, 128), 1)
    for column in range(2):
        wanted = 2 * chip + column + jnp.where(x16 < 4, -1, jnp.where(x16 >= 12, 1, 0))
        pick = (source % COLUMNS == wanted) & (source // COLUMNS == target // 128)
        found = jnp.dot(
            lhs_ref[...].astype(jnp.bfloat16),
            jnp.where(pick, 1.0, 0.0).astype(jnp.bfloat16),
            preferred_element_type=F32,
        )
        for v in range(blocks):
            for odd in range(2):
                found_ref[pl.ds(2 * v + odd, 8, stride=ROWS), :] = found[
                    v * 8 : v * 8 + 8, odd * 128 : (odd + 1) * 128
                ]
        edge = (lane % WIDE == 3) | (lane % WIDE == 11)
        flat_ref[column] = jnp.where(edge, found_ref[ROWS : 2 * ROWS, :], 1.0)
        flat_ref[2 + column] = jnp.where(lane >= 112, found_ref[3 * ROWS : 4 * ROWS, :], 1.0)
        outer_ref[column] = jnp.where(
            core == 0, found_ref[4 * ROWS : 5 * ROWS, :], found_ref[5 * ROWS : 6 * ROWS, :]
        )


def unpack_kernel(table_ref, received_ref, planes_ref, packed_ref):
    for r in range(ROWS):
        for entry in range(4):
            packed_ref[pl.ds(entry * PAIRS * ROWS + r, PAIRS, stride=ROWS), :] = received_ref[
                table_ref[entry, r + 1]
            ]
    lane = iota((ROWS, 128), 1)
    x16 = lane % WIDE
    for pair in range(PAIRS):
        first, second, left, right = (
            packed_ref[(entry * PAIRS + pair) * ROWS : (entry * PAIRS + pair + 1) * ROWS, :]
            for entry in range(4)
        )
        outside = jnp.where(lane % TILE >= HALF, left, right)

        def join(left, here, right):
            return jnp.where(x16 < 4, left, jnp.where(x16 >= 12, right, here))

        second_4 = shift(second, 4, 1)
        first_m4 = shift(first, -4, 1)
        planes_ref[pair] = join(shift(outside, -4, 1), shift(first, 4, 1), shift(second, 12, 1))
        planes_ref[PAIRS + pair] = join(shift(outside, -12, 1), first_m4, second_4)
        planes_ref[HALF + pair] = join(first_m4, second_4, shift(outside, 12, 1))
        planes_ref[HALF + PAIRS + pair] = join(
            shift(first, -12, 1), shift(second, -4, 1), shift(outside, 4, 1)
        )


def march_kernel(*refs):
    (
        table_ref,
        outer_ref,
        own_ref,
        inner_ref,
        far_ref,
        near_ref,
        faces_ref,
        out_ref,
        even_ref,
        odd_ref,
        sign_ref,
        done_ref,
    ) = refs
    depth = 3 * HALF
    lane = iota((ROWS, 128), 1)
    first_y = lane < WIDE
    last_y = lane >= 128 - WIDE

    def start(column, p):
        base = column * HALF
        if p < HALF:
            return outer_ref[base + HALF - 1 - p]
        if p < 2 * HALF:
            return own_ref[base + p - HALF]
        return inner_ref[base + depth - 1 - p]

    def load(step, column, p):
        if step == 0:
            return start(column, p)
        return (odd_ref if step % 2 else even_ref)[column * depth + p]

    def one_step(step, column, lo, hi):
        target_ref = even_ref if step % 2 else odd_ref
        level = load(step, column, lo - 1)
        after = load(step, column, lo)
        ahead_z = after - level
        if lo == HALF:
            ahead_z = ahead_z * faces_ref[column]
        for p in range(lo, hi):
            back_z = ahead_z
            level = after
            after = load(step, column, p + 1)
            ahead_z = after - level
            if p == HALF - 1:
                ahead_z = ahead_z * faces_ref[column]
            links = far_ref if p < HALF else near_ref
            if step == 0:
                sign_field = level * lax.rsqrt(level * level + 1.0)
                sign_ref[column * depth + p] = sign_field
            else:
                sign_field = sign_ref[column * depth + p]
            up = jnp.where(sign_field > 0, 1.0, -1.0)
            down = -up
            ahead = (shift(level, -1, 1) - level) * links[column]
            back = shift(ahead, 1, 1)
            squares = jnp.square(jnp.maximum(jnp.maximum(up * back, down * ahead), 0.0))
            beyond = jnp.where(first_y, shift(level, -1, 0), level)
            ahead = (shift(beyond, -WIDE, 1) - level) * links[2 + column]
            back = shift(jnp.where(last_y, shift(ahead, 1, 0), ahead), WIDE, 1)
            squares = squares + jnp.square(
                jnp.maximum(jnp.maximum(up * back, down * ahead), 0.0)
            )
            squares = squares + jnp.square(
                jnp.maximum(jnp.maximum(up * back_z, down * ahead_z), 0.0)
            )
            length = squares + EPSILON
            target_ref[column * depth + p] = level - TIME_STEP * sign_field * (
                length * lax.rsqrt(length) - 1.0
            )

    for step, cuts in enumerate(((1, 6, 11), (2, 6, 10), (3, 9), (4, 8))):
        for column in range(2):
            for lo, hi in zip(cuts[:-1], cuts[1:]):
                pl.when(table_ref[0, 1] >= 0)(
                    functools.partial(one_step, step, column, lo, hi)
                )
    lower = lane % WIDE < TILE
    for column in range(2):
        for pair in range(PAIRS):
            p = column * depth + HALF + pair
            row = (column * PAIRS + pair) * ROWS
            done_ref[row : row + ROWS, :] = jnp.where(
                lower, shift(even_ref[p], -4, 1), shift(even_ref[p + PAIRS], 4, 1)
            )
    for r in range(ROWS):
        for column in range(2):
            out_ref[table_ref[4 + column, r + 1]] = done_ref[
                pl.ds(column * PAIRS * ROWS + r, PAIRS, stride=ROWS), :
            ]


def deliver_kernel(where_am_i, *refs):
    counts_ref, returned_ref, out_ref, turned_ref = refs[-4:]
    me = where_am_i(refs)
    turn = own_start(counts_ref, me) & (COLUMNS - 1)
    live = iota((SLOTS, SLOTS), 1) < counts_ref[0, me]
    chips = COLUMNS // 2
    for core in range(2):
        for pair in range(PAIRS):
            held_ref = turned_ref.at[core * PAIRS + pair]
            for d in range(DEPTH):
                for column in range(2):
                    row = core * BACK + (column * DEPTH + d) * PAIRS + pair
                    held_ref[pl.ds(d * COLUMNS + column, chips, stride=2), :] = returned_ref[
                        pl.ds(row, chips, stride=2 * BACK), :
                    ]
            turned = pltpu.roll(held_ref[...].T, (SLOTS - turn) & (SLOTS - 1), 1)
            turned = jnp.where(live, turned, 0.0)
            for y in range(TILE):
                for upper in range(2):
                    row = y * WIDE + upper * TILE
                    z = plane_of(core, pair, upper)
                    out_ref[pl.ds(y * TILE + z, TILE, stride=TILE * TILE), :] = turned[
                        row : row + TILE
                    ]


def spec(space=pltpu.VMEM):
    return pl.BlockSpec(memory_space=space)


def run(
    kernel, operands, shapes, scratch, me=None, spaces=None, out_spaces=None, cost=(0, 0), grant=32
):
    spaces = spaces or [pltpu.VMEM] * len(operands)
    out_spaces = out_spaces or [pltpu.VMEM] * len(shapes)
    if me is not None:
        operands = (me, *operands)
        spaces = [pltpu.SMEM, *spaces]
    out = pl.pallas_call(
        kernel,
        out_shape=[jax.ShapeDtypeStruct(s, t) for s, t in shapes],
        in_specs=[spec(s) for s in spaces],
        out_specs=[spec(s) for s in out_spaces],
        scratch_shapes=scratch,
        compiler_params=pltpu.CompilerParams(vmem_limit_bytes=grant << 20),
        cost_estimate=pl.CostEstimate(flops=cost[0], bytes_accessed=cost[1], transcendentals=0),
        name=getattr(kernel, "func", kernel).__name__,
    )(*operands)
    return out


def position(refs):
    return lax.axis_index("mem")


def given(refs):
    return refs[0][0]


def bind(kernel, me):
    return functools.partial(kernel, position if me is None else given)


def pack(counts, phi, me=None):
    (out,) = run(
        bind(pack_kernel, me),
        (counts, phi.reshape(CELLS, SLOTS)),
        [((COLUMNS * SENT, 128), F32)],
        [
            pltpu.SMEM((1, COLUMNS), I32),
            pltpu.VMEM((CELLS, SLOTS), F32),
            pltpu.VMEM((2 * PAIRS, SLOTS + 16, 128), F32),
            pltpu.SemaphoreType.DMA((2,)),
        ],
        me,
        [pltpu.HBM, pltpu.HBM],
        grant=62,
    )
    return out.reshape(COLUMNS * SENT // 4, 4, 128)


def masks_of(counts, neighbours, me=None):
    return run(
        bind(mask_kernel, me),
        (counts, neighbours),
        [((4, ROWS, 128), F32), ((2, ROWS, 128), F32), ((6, TABLE), I32)],
        [pltpu.VMEM((128, 128), F32), pltpu.VMEM((8 * ROWS, 128), F32)],
        me,
        [pltpu.SMEM, pltpu.VMEM],
        [pltpu.VMEM, pltpu.VMEM, pltpu.SMEM],
        cost=(1 << 22, 1 << 17),
    )


def unpack(table, received):
    (out,) = run(
        unpack_kernel,
        (table, received.reshape(COLUMNS * SENT // PAIRS, PAIRS, 128)),
        [((TILE, ROWS, 128), F32)],
        [pltpu.VMEM((4 * PAIRS * ROWS, 128), F32)],
        None,
        [pltpu.SMEM, pltpu.VMEM],
    )
    return out


def march(table, outer, own, inner, far, near, faces):
    (out,) = run(
        march_kernel,
        (table, outer, own, inner, far, near, faces),
        [((COLUMNS * BACK // PAIRS, PAIRS, 128), F32)],
        [pltpu.VMEM((6 * HALF, ROWS, 128), F32)] * 3 + [pltpu.VMEM((TILE // 2 * ROWS, 128), F32)],
        None,
        [pltpu.SMEM] + [pltpu.VMEM] * 6,
    )
    return out.reshape(COLUMNS, BACK, 128)


def deliver(counts, returned, me=None):
    (out,) = run(
        bind(deliver_kernel, me),
        (counts, returned.reshape(COLUMNS * BACK, 128)),
        [((CELLS, SLOTS), F32)],
        [pltpu.VMEM((2 * PAIRS, SLOTS, 128), F32)],
        me,
        [pltpu.SMEM, pltpu.VMEM],
    )
    return out.reshape(TILE, TILE, TILE, SLOTS)


def exchange(x):
    return lax.all_to_all(x, "mem", split_axis=0, concat_axis=0, tiled=True)


def on_device(phi_owned, band_counts, neighbours):
    groups, members = lax.axis_size("grp"), lax.axis_size("mem")
    mates = [(m, m ^ 1) for m in range(members)]
    across = []
    for g in range(groups - 1):
        for m in range(0, members, 2):
            low, high = g * members + m + 1, (g + 1) * members + m
            across += [(low, high), (high, low)]
    received = exchange(pack(band_counts, phi_owned))
    near, faces, table = masks_of(band_counts, neighbours)
    far = lax.ppermute(near, ("grp", "mem"), across)
    received, far = lax.optimization_barrier((received, far))
    own = unpack(table, received)
    outer = lax.ppermute(own, ("grp", "mem"), across)
    inner = lax.ppermute(own, "mem", mates)
    returned = exchange(march(table, outer, own, inner, far, near, faces))
    return deliver(band_counts, returned)


def solution(mesh):
    return jax.shard_map(
        on_device,
        mesh=mesh,
        in_specs=(P(None, None, None, ("grp", "mem")), P("grp", None), P("grp", None, None)),
        out_specs=P(None, None, None, ("grp", "mem")),
        check_vma=False,
    )
```

time: 72.6 us -> 62 us (0.85)
  waiting for transfers between devices: 19.2 us -> 6.57 us
  starting transfers between devices: 18.1 us -> 23.8 us
  Pallas kernels: 14.2 us -> 11.5 us
  blocking collectives: 20.1 us -> 19.1 us
    all_to_all x1, waiting for transfers between devices: 14.5 us -> 3.03 us  [exchange(): return lax.all_to_all(x, 'mem', split_axis=0, concat_axis=0, tiled=True)]
    ppermute x2 -> x3, starting transfers between devices: 7.13 us -> 12.8 us  [the longest x1 5.55 us: on_device(): far = lax.ppermute(near, ('grp', 'mem'), across)]
    pallas_call x5, Pallas kernels: 14.2 us -> 11.5 us  [run(): pl.pallas_call(kernel, out_shape=[jax.ShapeDtypeStruct(s, t) for s, t in...]
    ppermute x2 -> x3, waiting for transfers between devices: 4.64 us -> 3.54 us  [the longest x1 2.23 us: on_device(): far = lax.ppermute(near, ('grp', 'mem'), across)]
    all_to_all x1, blocking collectives: 20.1 us -> 19.1 us  [exchange(): return lax.all_to_all(x, 'mem', split_axis=0, concat_axis=0, tiled=True)]
  transfers between devices with their start and end apart: 3 -> 4, of which waited for: 2 -> 4; matrix products, arithmetic and copies ran while one was open for 0% -> 0% of each run, Pallas kernels for 3% -> 6%
where the time goes in v4:
time: 62 us; the launch traced here: 61.7 us
  starting transfers between devices  23.8 us (38%)
  blocking collectives  19.1 us (31%)
  Pallas kernels  11.5 us (19%)
  waiting for transfers between devices  6.57 us (11%)
  local copies, waits for them, and re-layouts  0.65 us (1%)
    all_to_all x1, blocking collectives, exchange(): return lax.all_to_all(x, 'mem', split_axis=0, concat_axis=0, tiled=True)  19.1 us
    pallas_call x5, Pallas kernels, run(): pl.pallas_call(kernel, out_shape=[jax.ShapeDtypeStruct(s, t) for s, t in...  11.5 us
    all_to_all x1, starting transfers between devices, exchange(): return lax.all_to_all(x, 'mem', split_axis=0, concat_axis=0, tiled=True)  10.9 us
    ppermute x1, starting transfers between devices, on_device(): far = lax.ppermute(near, ('grp', 'mem'), across)  5.55 us
    ppermute x1, starting transfers between devices, on_device(): outer = lax.ppermute(own, ('grp', 'mem'), across)  5.37 us
    all_to_all x1, waiting for transfers between devices, exchange(): return lax.all_to_all(x, 'mem', split_axis=0, concat_axis=0, tiled=True)  3.03 us
    ppermute x1, waiting for transfers between devices, on_device(): far = lax.ppermute(near, ('grp', 'mem'), across)  2.23 us
    ppermute x1, starting transfers between devices, on_device(): inner = lax.ppermute(own, 'mem', mates)  1.92 us
  transfers between devices with their start and end apart: 4, of which 4 were waited for; matrix products, arithmetic and copies ran while one was open for 0% of the time, Pallas kernels for 6%

profile of v4, /device:TPU:193, one launch (start us, length us, event | category | flops | bytes accessed | tf_op | source)
XLA Modules:
  0.0 61.7 jit_solution(17985304070043647695)
XLA Ops:
  0.0 2.0 %pack_kernel.1 = f32[768,128]{1,0:T(8,128)} custom-call(s32[1,64]{1,0:T(1,128)} %refs_0_.5, f32[512,128]{1,0:T(8,128)} %bitcast.10), custom_call_target="tpu_custom_call" | custom-call | tf_op jit(solution)/shard_map/pack_kernel/pallas_call | solution.py:309
  2.0 0.0 copy-start.1
  2.1 10.9 %all-to-all-start = ((f32[192,4,128]{2,1,0:T(4,128)}), f32[192,4,128]{2,1,0:T(4,128)S(1)}, u32[]{:S(2)}, u32[]{:S(2)}) async-start(f32[192,4,128]{2,1,0:T(4,128)} %bitcast.9), calls=%async_computation | async-start | bytes 786432 | tf_op jit(solution)/shard_map/all_to_all | solution.py:402
  13.0 0.0 copy-done.1
  13.0 0.0 copy-start
  13.0 0.6 %copy-done = s32[1,64]{1,0:T(1,128)S(1)} copy-done((s32[1,64]{1,0:T(1,128)S(1)}, s32[1,64]{1,0:T(1,128)}, u32[]{:S(2)}) %copy-start) | copy-done | bytes 280
  13.7 3.6 %mask_kernel.1 = (f32[4,32,128]{2,1,0:T(8,128)S(1)}, f32[2,32,128]{2,1,0:T(8,128)S(1)}, s32[6,40]{1,0:T(8,128)S(1)}) custom-call(s32[1,64]{1,0:T(1,128)S(1)} %copy-done, s32[1,6,2048]{2,1,0:T(8,128)S(1)} %copy.4.refs_1_), custom_call_target="tpu_custom_call" | custom-call | flops 4194304 | bytes 131072 | tf_op jit(solution)/shard_map/mask_kernel/pallas_call | solution.py:309
  17.2 5.6 %collective-permute-start = (f32[4,32,128]{2,1,0:T(8,128)S(1)}, f32[4,32,128]{2,1,0:T(8,128)S(1)}, u32[]{:S(2)}, u32[]{:S(2)}) collective-permute-start(f32[4,32,128]{2,1,0:T(8,128)S(1)} %get-tuple-element.11.refs_5_), channel_id=1, source_target_pairs={{1,64},{64,1},{3,66},{66,3},{5,68},{68,5},{7,70},{70,7},{9,72},{72... | collective-permute-start | bytes 196616 | tf_op jit(solution)/shard_map/ppermute | solution.py:415
  22.8 2.2 %collective-permute-done.refs_4_ = f32[4,32,128]{2,1,0:T(8,128)S(1)} collective-permute-done((f32[4,32,128]{2,1,0:T(8,128)S(1)}, f32[4,32,128]{2,1,0:T(8,128)S(1)}, u32[]{:S(2)}, u32[]{:S(2)}) %collective-permute-start) | collective-permute-done | bytes 65568 | tf_op jit(solution)/shard_map/ppermute | solution.py:415
  25.0 3.0 %all-to-all-done = f32[192,4,128]{2,1,0:T(4,128)S(1)} async-done(((f32[192,4,128]{2,1,0:T(4,128)}), f32[192,4,128]{2,1,0:T(4,128)S(1)}, u32[]{:S(2)}, u32[]{:S(2)}) %all-to-all-start) | async-done | bytes 393248 | tf_op jit(solution)/shard_map/all_to_all | solution.py:402
  28.1 0.9 %unpack_kernel.1.refs_2_ = f32[8,32,128]{2,1,0:T(8,128)S(1)} custom-call(s32[6,40]{1,0:T(8,128)S(1)} %get-tuple-element.10.table_ref.refs_0_, f32[384,2,128]{2,1,0:T(2,128)S(1)} %bitcast.6), custom_call_target="tpu_custom_call" | custom-call | tf_op jit(solution)/shard_map/unpack_kernel/pallas_call | solution.py:309
  28.9 5.4 %collective-permute-start.1 = (f32[8,32,128]{2,1,0:T(8,128)S(1)}, f32[8,32,128]{2,1,0:T(8,128)S(1)}, u32[]{:S(2)}, u32[]{:S(2)}) collective-permute-start(f32[8,32,128]{2,1,0:T(8,128)S(1)} %unpack_kernel.1.refs_2_), channel_id=1, source_target_pairs={{1,64},{64,1},{3,66},{66,3},{5,68},{68,5},{7,70},{70,7},{9,72},{72... | collective-permute-start | bytes 393224 | tf_op jit(solution)/shard_map/ppermute | solution.py:418
  34.3 1.9 %collective-permute-start.2 = (f32[8,32,128]{2,1,0:T(8,128)S(1)}, f32[8,32,128]{2,1,0:T(8,128)S(1)}, u32[]{:S(2)}, u32[]{:S(2)}) collective-permute-start(f32[8,32,128]{2,1,0:T(8,128)S(1)} %unpack_kernel.1.refs_2_), channel_id=1, source_target_pairs={{0,1},{1,0},{2,3},{3,2},{4,5},{5,4},{6,7},{7,6},{8,9},{9,8},{10,11... | collective-permute-start | bytes 393224 | tf_op jit(solution)/shard_map/ppermute | solution.py:419
  36.2 0.7 %collective-permute-done.1.refs_1_ = f32[8,32,128]{2,1,0:T(8,128)S(1)} collective-permute-done((f32[8,32,128]{2,1,0:T(8,128)S(1)}, f32[8,32,128]{2,1,0:T(8,128)S(1)}, u32[]{:S(2)}, u32[]{:S(2)}) %collective-permute-start.1) | collective-permute-done | bytes 131104 | tf_op jit(solution)/shard_map/ppermute | solution.py:418
  37.0 0.6 collective-permute-done.2.refs_3_
  37.6 3.4 %march_kernel.1 = f32[256,2,128]{2,1,0:T(2,128)S(1)} custom-call(s32[6,40]{1,0:T(8,128)S(1)} %get-tuple-element.10.table_ref.refs_0_, f32[8,32,128]{2,1,0:T(8,128)S(1)} %collective-permute-done.1.refs_1_, f32[8,32,128]{2,1,0:T(8,128)S(1)} %unpack_kernel.1.refs_2_, f32[8,32,128]{2,1,0:T(8,128)S(1)} %collective-permute-done.2.refs_3_, ...), custom_call_target="tpu_custom_call" | custom-call | tf_op jit(solution)/shard_map/march_kernel/pallas_call | solution.py:309
  40.9 19.1 %all_to_all.10 = f32[64,8,128]{2,1,0:T(8,128)S(1)} all-to-all(f32[64,8,128]{2,1,0:T(8,128)S(1)} %bitcast.7), channel_id=1, replica_groups=mesh['grp'=8,'mem'=64] {'mem'}, dimensions={0} | all-to-all | bytes 524288 | tf_op jit(solution)/shard_map/all_to_all | solution.py:402
  60.1 1.6 %deliver_kernel.1 = f32[512,128]{1,0:T(8,128)} custom-call(s32[1,64]{1,0:T(1,128)S(1)} %copy-done, f32[512,128]{1,0:T(8,128)S(1)} %bitcast.8), custom_call_target="tpu_custom_call" | custom-call | tf_op jit(solution)/shard_map/deliver_kernel/pallas_call | solution.py:309
  (1 shorter events, 0.0 us)
Async XLA Ops:
  2.0 11.0 %copy-start.1 = (s32[1,6,2048]{2,0,1:T(1,128)S(1)}, s32[1,6,2048]{2,0,1:T(1,128)}, u32[]{:S(2)}) copy-start(s32[1,6,2048]{2,0,1:T(1,128)} %param.5) | copy-start | bytes 147460
  2.1 26.0 %all-to-all-start = ((f32[192,4,128]{2,1,0:T(4,128)}), f32[192,4,128]{2,1,0:T(4,128)S(1)}, u32[]{:S(2)}, u32[]{:S(2)}) async-start(f32[192,4,128]{2,1,0:T(4,128)} %bitcast.9), calls=%async_computation | async-start | bytes 786432 | tf_op jit(solution)/shard_map/all_to_all | solution.py:402
  13.0 0.7 %copy-start = (s32[1,64]{1,0:T(1,128)S(1)}, s32[1,64]{1,0:T(1,128)}, u32[]{:S(2)}) copy-start(s32[1,64]{1,0:T(1,128)} %refs_0_.5) | copy-start | bytes 772
  17.2 7.8 %collective-permute-start = (f32[4,32,128]{2,1,0:T(8,128)S(1)}, f32[4,32,128]{2,1,0:T(8,128)S(1)}, u32[]{:S(2)}, u32[]{:S(2)}) collective-permute-start(f32[4,32,128]{2,1,0:T(8,128)S(1)} %get-tuple-element.11.refs_5_), channel_id=1, source_target_pairs={{1,64},{64,1},{3,66},{66,3},{5,68},{68,5},{7,70},{70,7},{9,72},{72... | collective-permute-start | bytes 196616 | tf_op jit(solution)/shard_map/ppermute | solution.py:415
  28.9 8.0 %collective-permute-start.1 = (f32[8,32,128]{2,1,0:T(8,128)S(1)}, f32[8,32,128]{2,1,0:T(8,128)S(1)}, u32[]{:S(2)}, u32[]{:S(2)}) collective-permute-start(f32[8,32,128]{2,1,0:T(8,128)S(1)} %unpack_kernel.1.refs_2_), channel_id=1, source_target_pairs={{1,64},{64,1},{3,66},{66,3},{5,68},{68,5},{7,70},{70,7},{9,72},{72... | collective-permute-start | bytes 393224 | tf_op jit(solution)/shard_map/ppermute | solution.py:418
  34.3 3.2 %collective-permute-start.2 = (f32[8,32,128]{2,1,0:T(8,128)S(1)}, f32[8,32,128]{2,1,0:T(8,128)S(1)}, u32[]{:S(2)}, u32[]{:S(2)}) collective-permute-start(f32[8,32,128]{2,1,0:T(8,128)S(1)} %unpack_kernel.1.refs_2_), channel_id=1, source_target_pairs={{0,1},{1,0},{2,3},{3,2},{4,5},{5,4},{6,7},{7,6},{8,9},{9,8},{10,11... | collective-permute-start | bytes 393224 | tf_op jit(solution)/shard_map/ppermute | solution.py:419

commit v5 on v4

--- a/solution.py
+++ b/solution.py
@@ -175,9 +175,9 @@
         )
 
 
-def march_kernel(*refs):
+def march_kernel(where_am_i, *refs):
     (
-        table_ref,
+        table_vmem,
         outer_ref,
         own_ref,
         inner_ref,
@@ -187,9 +187,15 @@
         out_ref,
         even_ref,
         odd_ref,
-        sign_ref,
+        pull_ref,
+        side_ref,
         done_ref,
-    ) = refs
+        table_ref,
+        sem,
+    ) = refs[-15:]
+    here = where_am_i(refs)
+    fetch = pltpu.make_async_copy(table_vmem, table_ref, sem)
+    fetch.start()
     depth = 3 * HALF
     lane = iota((ROWS, 128), 1)
     first_y = lane < WIDE
@@ -225,10 +231,13 @@
             links = far_ref if p < HALF else near_ref
             if step == 0:
                 sign_field = level * lax.rsqrt(level * level + 1.0)
-                sign_ref[column * depth + p] = sign_field
+                pull = TIME_STEP * sign_field
+                up = jnp.where(sign_field > 0, 1.0, -1.0)
+                pull_ref[column * depth + p] = pull
+                side_ref[column * depth + p] = up
             else:
-                sign_field = sign_ref[column * depth + p]
-            up = jnp.where(sign_field > 0, 1.0, -1.0)
+                pull = pull_ref[column * depth + p]
+                up = side_ref[column * depth + p]
             down = -up
             ahead = (shift(level, -1, 1) - level) * links[column]
             back = shift(ahead, 1, 1)
@@ -243,16 +252,19 @@
                 jnp.maximum(jnp.maximum(up * back_z, down * ahead_z), 0.0)
             )
             length = squares + EPSILON
-            target_ref[column * depth + p] = level - TIME_STEP * sign_field * (
+            target_ref[column * depth + p] = level - pull * (
                 length * lax.rsqrt(length) - 1.0
             )
 
-    for step, cuts in enumerate(((1, 6, 11), (2, 6, 10), (3, 9), (4, 8))):
-        for column in range(2):
-            for lo, hi in zip(cuts[:-1], cuts[1:]):
-                pl.when(table_ref[0, 1] >= 0)(
-                    functools.partial(one_step, step, column, lo, hi)
-                )
+    spans = ((1, 11), (2, 10), (3, 9), (4, 8))
+
+    def several(steps, columns):
+        for step in steps:
+            for column in columns:
+                one_step(step, column, *spans[step])
+
+    for block, (steps, columns) in enumerate((((0,), (0,)), ((0,), (1,)), ((1,), (0,)), ((1,), (1,)), ((2,), (0,)), ((2,), (1,)), ((3,), (0, 1)))):
+        pl.when(here > -1 - block)(functools.partial(several, steps, columns))
     lower = lane % WIDE < TILE
     for column in range(2):
         for pair in range(PAIRS):
@@ -261,6 +273,7 @@
             done_ref[row : row + ROWS, :] = jnp.where(
                 lower, shift(even_ref[p], -4, 1), shift(even_ref[p + PAIRS], 4, 1)
             )
+    fetch.wait()
     for r in range(ROWS):
         for column in range(2):
             out_ref[table_ref[4 + column, r + 1]] = done_ref[
@@ -271,8 +284,10 @@
 def deliver_kernel(where_am_i, *refs):
     counts_ref, returned_ref, out_ref, turned_ref = refs[-4:]
     me = where_am_i(refs)
-    turn = own_start(counts_ref, me) & (COLUMNS - 1)
-    live = iota((SLOTS, SLOTS), 1) < counts_ref[0, me]
+    counts = counts_ref[...]
+    owner = iota((1, COLUMNS), 1)
+    turn = jnp.sum(jnp.where(owner < me, counts, 0)) & (COLUMNS - 1)
+    live = iota((SLOTS, SLOTS), 1) < jnp.sum(jnp.where(owner == me, counts, 0))
     chips = COLUMNS // 2
     for core in range(2):
         for pair in range(PAIRS):
@@ -374,14 +389,18 @@
     return out
 
 
-def march(table, outer, own, inner, far, near, faces):
+def march(table, outer, own, inner, far, near, faces, me=None):
     (out,) = run(
-        march_kernel,
+        bind(march_kernel, me),
         (table, outer, own, inner, far, near, faces),
         [((COLUMNS * BACK // PAIRS, PAIRS, 128), F32)],
-        [pltpu.VMEM((6 * HALF, ROWS, 128), F32)] * 3 + [pltpu.VMEM((TILE // 2 * ROWS, 128), F32)],
-        None,
-        [pltpu.SMEM] + [pltpu.VMEM] * 6,
+        [pltpu.VMEM((6 * HALF, ROWS, 128), F32)] * 4
+        + [
+            pltpu.VMEM((2 * PAIRS * ROWS, 128), F32),
+            pltpu.SMEM((6, TABLE), I32),
+            pltpu.SemaphoreType.DMA,
+        ],
+        me,
     )
     return out.reshape(COLUMNS, BACK, 128)
 
@@ -393,7 +412,6 @@
         [((CELLS, SLOTS), F32)],
         [pltpu.VMEM((2 * PAIRS, SLOTS, 128), F32)],
         me,
-        [pltpu.SMEM, pltpu.VMEM],
     )
     return out.reshape(TILE, TILE, TILE, SLOTS)
 

time: 62 us -> 60.4 us (0.974)
  Pallas kernels: 11.5 us -> 9.85 us
    pallas_call x5, Pallas kernels: 11.5 us -> 9.85 us  [run(): pl.pallas_call(kernel, out_shape=[jax.ShapeDtypeStruct(s, t) for s, t in...]
where the time goes in v5:
time: 60.4 us; the launch traced here: 60.1 us
  starting transfers between devices  23.8 us (39%)
  blocking collectives  19.1 us (32%)
  Pallas kernels  9.85 us (16%)
  waiting for transfers between devices  6.57 us (11%)
  local copies, waits for them, and re-layouts  0.65 us (1%)
    all_to_all x1, blocking collectives, exchange(): return lax.all_to_all(x, 'mem', split_axis=0, concat_axis=0, tiled=True)  19.1 us
    all_to_all x1, starting transfers between devices, exchange(): return lax.all_to_all(x, 'mem', split_axis=0, concat_axis=0, tiled=True)  10.9 us
    pallas_call x5, Pallas kernels, run(): pl.pallas_call(kernel, out_shape=[jax.ShapeDtypeStruct(s, t) for s, t in...  9.85 us
    ppermute x1, starting transfers between devices, on_device(): far = lax.ppermute(near, ('grp', 'mem'), across)  5.55 us
    ppermute x1, starting transfers between devices, on_device(): outer = lax.ppermute(own, ('grp', 'mem'), across)  5.37 us
    all_to_all x1, waiting for transfers between devices, exchange(): return lax.all_to_all(x, 'mem', split_axis=0, concat_axis=0, tiled=True)  3.03 us
    ppermute x1, waiting for transfers between devices, on_device(): far = lax.ppermute(near, ('grp', 'mem'), across)  2.23 us
    ppermute x1, starting transfers between devices, on_device(): inner = lax.ppermute(own, 'mem', mates)  1.92 us
  transfers between devices with their start and end apart: 4, of which 4 were waited for; matrix products, arithmetic and copies ran while one was open for 0% of the time, Pallas kernels for 6%

profile of v5, /device:TPU:193, one launch (start us, length us, event | category | flops | bytes accessed | tf_op | source)
XLA Modules:
  0.0 60.1 jit_solution(1302890617765035063)
XLA Ops:
  0.0 2.0 %pack_kernel.1 = f32[768,128]{1,0:T(8,128)} custom-call(s32[1,64]{1,0:T(1,128)} %refs_0_.5, f32[512,128]{1,0:T(8,128)} %bitcast.10), custom_call_target="tpu_custom_call" | custom-call | tf_op jit(solution)/shard_map/pack_kernel/pallas_call | solution.py:324
  2.0 0.0 copy-start.1
  2.1 10.9 %all-to-all-start = ((f32[192,4,128]{2,1,0:T(4,128)}), f32[192,4,128]{2,1,0:T(4,128)S(1)}, u32[]{:S(2)}, u32[]{:S(2)}) async-start(f32[192,4,128]{2,1,0:T(4,128)} %bitcast.9), calls=%async_computation | async-start | bytes 786432 | tf_op jit(solution)/shard_map/all_to_all | solution.py:420
  13.0 0.0 copy-done.1
  13.0 0.0 copy-start
  13.0 0.6 %copy-done = s32[1,64]{1,0:T(1,128)S(1)} copy-done((s32[1,64]{1,0:T(1,128)S(1)}, s32[1,64]{1,0:T(1,128)}, u32[]{:S(2)}) %copy-start) | copy-done | bytes 280
  13.7 3.6 %mask_kernel.1 = (f32[4,32,128]{2,1,0:T(8,128)S(1)}, f32[2,32,128]{2,1,0:T(8,128)S(1)}, s32[6,40]{1,0:T(8,128)S(1)}) custom-call(s32[1,64]{1,0:T(1,128)S(1)} %copy-done, s32[1,6,2048]{2,1,0:T(8,128)S(1)} %copy.4.refs_1_), custom_call_target="tpu_custom_call" | custom-call | flops 4194304 | bytes 131072 | tf_op jit(solution)/shard_map/mask_kernel/pallas_call | solution.py:324
  17.2 5.6 %collective-permute-start = (f32[4,32,128]{2,1,0:T(8,128)S(1)}, f32[4,32,128]{2,1,0:T(8,128)S(1)}, u32[]{:S(2)}, u32[]{:S(2)}) collective-permute-start(f32[4,32,128]{2,1,0:T(8,128)S(1)} %get-tuple-element.11.refs_5_), channel_id=1, source_target_pairs={{1,64},{64,1},{3,66},{66,3},{5,68},{68,5},{7,70},{70,7},{9,72},{72... | collective-permute-start | bytes 196616 | tf_op jit(solution)/shard_map/ppermute | solution.py:433
  22.8 2.2 %collective-permute-done.refs_4_ = f32[4,32,128]{2,1,0:T(8,128)S(1)} collective-permute-done((f32[4,32,128]{2,1,0:T(8,128)S(1)}, f32[4,32,128]{2,1,0:T(8,128)S(1)}, u32[]{:S(2)}, u32[]{:S(2)}) %collective-permute-start) | collective-permute-done | bytes 65568 | tf_op jit(solution)/shard_map/ppermute | solution.py:433
  25.0 3.0 %all-to-all-done = f32[192,4,128]{2,1,0:T(4,128)S(1)} async-done(((f32[192,4,128]{2,1,0:T(4,128)}), f32[192,4,128]{2,1,0:T(4,128)S(1)}, u32[]{:S(2)}, u32[]{:S(2)}) %all-to-all-start) | async-done | bytes 393248 | tf_op jit(solution)/shard_map/all_to_all | solution.py:420
  28.1 0.9 %unpack_kernel.1.refs_2_ = f32[8,32,128]{2,1,0:T(8,128)S(1)} custom-call(s32[6,40]{1,0:T(8,128)S(1)} %get-tuple-element.10.table_ref.refs_0_, f32[384,2,128]{2,1,0:T(2,128)S(1)} %bitcast.6), custom_call_target="tpu_custom_call" | custom-call | tf_op jit(solution)/shard_map/unpack_kernel/pallas_call | solution.py:324
  28.9 5.4 %collective-permute-start.1 = (f32[8,32,128]{2,1,0:T(8,128)S(1)}, f32[8,32,128]{2,1,0:T(8,128)S(1)}, u32[]{:S(2)}, u32[]{:S(2)}) collective-permute-start(f32[8,32,128]{2,1,0:T(8,128)S(1)} %unpack_kernel.1.refs_2_), channel_id=1, source_target_pairs={{1,64},{64,1},{3,66},{66,3},{5,68},{68,5},{7,70},{70,7},{9,72},{72... | collective-permute-start | bytes 393224 | tf_op jit(solution)/shard_map/ppermute | solution.py:436
  34.3 1.9 %collective-permute-start.2 = (f32[8,32,128]{2,1,0:T(8,128)S(1)}, f32[8,32,128]{2,1,0:T(8,128)S(1)}, u32[]{:S(2)}, u32[]{:S(2)}) collective-permute-start(f32[8,32,128]{2,1,0:T(8,128)S(1)} %unpack_kernel.1.refs_2_), channel_id=1, source_target_pairs={{0,1},{1,0},{2,3},{3,2},{4,5},{5,4},{6,7},{7,6},{8,9},{9,8},{10,11... | collective-permute-start | bytes 393224 | tf_op jit(solution)/shard_map/ppermute | solution.py:437
  36.2 0.7 %collective-permute-done.1.refs_1_ = f32[8,32,128]{2,1,0:T(8,128)S(1)} collective-permute-done((f32[8,32,128]{2,1,0:T(8,128)S(1)}, f32[8,32,128]{2,1,0:T(8,128)S(1)}, u32[]{:S(2)}, u32[]{:S(2)}) %collective-permute-start.1) | collective-permute-done | bytes 131104 | tf_op jit(solution)/shard_map/ppermute | solution.py:436
  37.0 0.6 %collective-permute-done.2.refs_3_ = f32[8,32,128]{2,1,0:T(8,128)S(1)} collective-permute-done((f32[8,32,128]{2,1,0:T(8,128)S(1)}, f32[8,32,128]{2,1,0:T(8,128)S(1)}, u32[]{:S(2)}, u32[]{:S(2)}) %collective-permute-start.2) | collective-permute-done | bytes 131104 | tf_op jit(solution)/shard_map/ppermute | solution.py:437
  37.6 2.2 %march_kernel.1 = f32[256,2,128]{2,1,0:T(2,128)S(1)} custom-call(s32[6,40]{1,0:T(8,128)S(1)} %get-tuple-element.10.table_ref.refs_0_, f32[8,32,128]{2,1,0:T(8,128)S(1)} %collective-permute-done.1.refs_1_, f32[8,32,128]{2,1,0:T(8,128)S(1)} %unpack_kernel.1.refs_2_, f32[8,32,128]{2,1,0:T(8,128)S(1)} %collective-permute-done.2.refs_3_, ...), custom_call_target="tpu_custom_call" | custom-call | tf_op jit(solution)/shard_map/march_kernel/pallas_call | solution.py:324
  39.8 19.1 %all_to_all.10 = f32[64,8,128]{2,1,0:T(8,128)S(1)} all-to-all(f32[64,8,128]{2,1,0:T(8,128)S(1)} %bitcast.7), channel_id=1, replica_groups=mesh['grp'=8,'mem'=64] {'mem'}, dimensions={0} | all-to-all | bytes 524288 | tf_op jit(solution)/shard_map/all_to_all | solution.py:420
  58.9 1.2 %deliver_kernel.1 = f32[512,128]{1,0:T(8,128)} custom-call(s32[1,64]{1,0:T(1,128)S(1)} %copy-done, f32[512,128]{1,0:T(8,128)S(1)} %bitcast.8), custom_call_target="tpu_custom_call" | custom-call | tf_op jit(solution)/shard_map/deliver_kernel/pallas_call | solution.py:324
  (1 shorter events, 0.0 us)
Async XLA Ops:
  2.0 11.0 %copy-start.1 = (s32[1,6,2048]{2,0,1:T(1,128)S(1)}, s32[1,6,2048]{2,0,1:T(1,128)}, u32[]{:S(2)}) copy-start(s32[1,6,2048]{2,0,1:T(1,128)} %param.5) | copy-start | bytes 147460
  2.1 26.0 %all-to-all-start = ((f32[192,4,128]{2,1,0:T(4,128)}), f32[192,4,128]{2,1,0:T(4,128)S(1)}, u32[]{:S(2)}, u32[]{:S(2)}) async-start(f32[192,4,128]{2,1,0:T(4,128)} %bitcast.9), calls=%async_computation | async-start | bytes 786432 | tf_op jit(solution)/shard_map/all_to_all | solution.py:420
  13.0 0.7 %copy-start = (s32[1,64]{1,0:T(1,128)S(1)}, s32[1,64]{1,0:T(1,128)}, u32[]{:S(2)}) copy-start(s32[1,64]{1,0:T(1,128)} %refs_0_.5) | copy-start | bytes 772
  17.2 7.8 %collective-permute-start = (f32[4,32,128]{2,1,0:T(8,128)S(1)}, f32[4,32,128]{2,1,0:T(8,128)S(1)}, u32[]{:S(2)}, u32[]{:S(2)}) collective-permute-start(f32[4,32,128]{2,1,0:T(8,128)S(1)} %get-tuple-element.11.refs_5_), channel_id=1, source_target_pairs={{1,64},{64,1},{3,66},{66,3},{5,68},{68,5},{7,70},{70,7},{9,72},{72... | collective-permute-start | bytes 196616 | tf_op jit(solution)/shard_map/ppermute | solution.py:433
  28.9 8.0 %collective-permute-start.1 = (f32[8,32,128]{2,1,0:T(8,128)S(1)}, f32[8,32,128]{2,1,0:T(8,128)S(1)}, u32[]{:S(2)}, u32[]{:S(2)}) collective-permute-start(f32[8,32,128]{2,1,0:T(8,128)S(1)} %unpack_kernel.1.refs_2_), channel_id=1, source_target_pairs={{1,64},{64,1},{3,66},{66,3},{5,68},{68,5},{7,70},{70,7},{9,72},{72... | collective-permute-start | bytes 393224 | tf_op jit(solution)/shard_map/ppermute | solution.py:436
  34.3 3.2 %collective-permute-start.2 = (f32[8,32,128]{2,1,0:T(8,128)S(1)}, f32[8,32,128]{2,1,0:T(8,128)S(1)}, u32[]{:S(2)}, u32[]{:S(2)}) collective-permute-start(f32[8,32,128]{2,1,0:T(8,128)S(1)} %unpack_kernel.1.refs_2_), channel_id=1, source_target_pairs={{0,1},{1,0},{2,3},{3,2},{4,5},{5,4},{6,7},{7,6},{8,9},{9,8},{10,11... | collective-permute-start | bytes 393224 | tf_op jit(solution)/shard_map/ppermute | solution.py:437

commit v6 on v5

--- a/solution.py
+++ b/solution.py
@@ -49,7 +49,8 @@
 
 
 def pack_kernel(where_am_i, *refs):
-    counts_hbm, phi_hbm, out_ref, counts_ref, phi_ref, turned_ref, sems = refs[-7:]
+    counts_hbm, phi_hbm, blocks_ref, counts_ref, phi_ref, turned_ref, sems = refs[-7:]
+    out_ref = blocks_ref.reshape(COLUMNS * SENT, 128)
     copies = [
         pltpu.make_async_copy(counts_hbm, counts_ref, sems.at[0]),
         pltpu.make_async_copy(phi_hbm, phi_ref, sems.at[1]),
@@ -314,7 +315,7 @@
 
 
 def run(
-    kernel, operands, shapes, scratch, me=None, spaces=None, out_spaces=None, cost=(0, 0), grant=32
+    kernel, operands, shapes, scratch, me=None, spaces=None, out_spaces=None, cost=(0, 0), grant=32, kinds=None
 ):
     spaces = spaces or [pltpu.VMEM] * len(operands)
     out_spaces = out_spaces or [pltpu.VMEM] * len(shapes)
@@ -323,7 +324,7 @@
         spaces = [pltpu.SMEM, *spaces]
     out = pl.pallas_call(
         kernel,
-        out_shape=[jax.ShapeDtypeStruct(s, t) for s, t in shapes],
+        out_shape=[o(s, t) for (s, t), o in zip(shapes, kinds or [jax.ShapeDtypeStruct] * len(shapes))],
         in_specs=[spec(s) for s in spaces],
         out_specs=[spec(s) for s in out_spaces],
         scratch_shapes=scratch,
@@ -349,8 +350,11 @@
 def pack(counts, phi, me=None):
     (out,) = run(
         bind(pack_kernel, me),
-        (counts, phi.reshape(CELLS, SLOTS)),
-        [((COLUMNS * SENT, 128), F32)],
+        (
+            pltpu.with_memory_space_constraint(counts, pltpu.HBM),
+            pltpu.with_memory_space_constraint(phi.reshape(CELLS, SLOTS), pltpu.HBM),
+        ),
+        [((COLUMNS * SENT // 4, 4, 128), F32)],
         [
             pltpu.SMEM((1, COLUMNS), I32),
             pltpu.VMEM((CELLS, SLOTS), F32),
@@ -359,9 +363,10 @@
         ],
         me,
         [pltpu.HBM, pltpu.HBM],
-        grant=62,
-    )
-    return out.reshape(COLUMNS * SENT // 4, 4, 128)
+        grant=32,
+        kinds=[pltpu.VMEM],
+    )
+    return out
 
 
 def masks_of(counts, neighbours, me=None):

time: 60.4 us -> 60.4 us (level)
  no operation moved by 1% of the time
where the time goes in v6:
time: 60.4 us; the launch traced here: 60.1 us
  starting transfers between devices  23.8 us (39%)
  blocking collectives  19.1 us (32%)
  Pallas kernels  9.85 us (16%)
  waiting for transfers between devices  6.57 us (11%)
  local copies, waits for them, and re-layouts  0.65 us (1%)
    all_to_all x1, blocking collectives, exchange(): return lax.all_to_all(x, 'mem', split_axis=0, concat_axis=0, tiled=True)  19.1 us
    all_to_all x1, starting transfers between devices, exchange(): return lax.all_to_all(x, 'mem', split_axis=0, concat_axis=0, tiled=True)  10.9 us
    pallas_call x5, Pallas kernels, run(): pl.pallas_call(kernel, out_shape=[o(s, t) for (s, t), o in zip(shapes, ki...  9.85 us
    ppermute x1, starting transfers between devices, on_device(): far = lax.ppermute(near, ('grp', 'mem'), across)  5.55 us
    ppermute x1, starting transfers between devices, on_device(): outer = lax.ppermute(own, ('grp', 'mem'), across)  5.37 us
    all_to_all x1, waiting for transfers between devices, exchange(): return lax.all_to_all(x, 'mem', split_axis=0, concat_axis=0, tiled=True)  3.03 us
    ppermute x1, waiting for transfers between devices, on_device(): far = lax.ppermute(near, ('grp', 'mem'), across)  2.23 us
    ppermute x1, starting transfers between devices, on_device(): inner = lax.ppermute(own, 'mem', mates)  1.92 us
  transfers between devices with their start and end apart: 4, of which 4 were waited for; matrix products, arithmetic and copies ran while one was open for 0% of the time, Pallas kernels for 6%

profile of v6, /device:TPU:193, one launch (start us, length us, event | category | flops | bytes accessed | tf_op | source)
XLA Modules:
  0.0 60.1 jit_solution(14691601745060402196)
XLA Ops:
  0.0 2.0 %pack_kernel.1 = f32[192,4,128]{2,1,0:T(4,128)} custom-call(s32[1,64]{1,0:T(1,128)} %refs_0_.5, f32[512,128]{1,0:T(8,128)} %bitcast.8), custom_call_target="tpu_custom_call" | custom-call | tf_op jit(solution)/shard_map/pack_kernel/pallas_call | solution.py:325
  2.0 0.0 copy-start.1
  2.1 10.9 %all-to-all-start = ((f32[192,4,128]{2,1,0:T(4,128)}), f32[192,4,128]{2,1,0:T(4,128)S(1)}, u32[]{:S(2)}, u32[]{:S(2)}) async-start(f32[192,4,128]{2,1,0:T(4,128)} %pack_kernel.1), calls=%async_computation | async-start | bytes 786432 | tf_op jit(solution)/shard_map/all_to_all | solution.py:425
  13.0 0.0 copy-done.1
  13.0 0.0 copy-start
  13.0 0.6 %copy-done = s32[1,64]{1,0:T(1,128)S(1)} copy-done((s32[1,64]{1,0:T(1,128)S(1)}, s32[1,64]{1,0:T(1,128)}, u32[]{:S(2)}) %copy-start) | copy-done | bytes 280
  13.7 3.6 %mask_kernel.1 = (f32[4,32,128]{2,1,0:T(8,128)S(1)}, f32[2,32,128]{2,1,0:T(8,128)S(1)}, s32[6,40]{1,0:T(8,128)S(1)}) custom-call(s32[1,64]{1,0:T(1,128)S(1)} %copy-done, s32[1,6,2048]{2,1,0:T(8,128)S(1)} %copy.4.refs_1_), custom_call_target="tpu_custom_call" | custom-call | flops 4194304 | bytes 131072 | tf_op jit(solution)/shard_map/mask_kernel/pallas_call | solution.py:325
  17.2 5.6 %collective-permute-start = (f32[4,32,128]{2,1,0:T(8,128)S(1)}, f32[4,32,128]{2,1,0:T(8,128)S(1)}, u32[]{:S(2)}, u32[]{:S(2)}) collective-permute-start(f32[4,32,128]{2,1,0:T(8,128)S(1)} %get-tuple-element.11.refs_5_), channel_id=1, source_target_pairs={{1,64},{64,1},{3,66},{66,3},{5,68},{68,5},{7,70},{70,7},{9,72},{72... | collective-permute-start | bytes 196616 | tf_op jit(solution)/shard_map/ppermute | solution.py:438
  22.8 2.2 %collective-permute-done.refs_4_ = f32[4,32,128]{2,1,0:T(8,128)S(1)} collective-permute-done((f32[4,32,128]{2,1,0:T(8,128)S(1)}, f32[4,32,128]{2,1,0:T(8,128)S(1)}, u32[]{:S(2)}, u32[]{:S(2)}) %collective-permute-start) | collective-permute-done | bytes 65568 | tf_op jit(solution)/shard_map/ppermute | solution.py:438
  25.0 3.0 %all-to-all-done = f32[192,4,128]{2,1,0:T(4,128)S(1)} async-done(((f32[192,4,128]{2,1,0:T(4,128)}), f32[192,4,128]{2,1,0:T(4,128)S(1)}, u32[]{:S(2)}, u32[]{:S(2)}) %all-to-all-start) | async-done | bytes 393248 | tf_op jit(solution)/shard_map/all_to_all | solution.py:425
  28.1 0.9 %unpack_kernel.1.refs_2_ = f32[8,32,128]{2,1,0:T(8,128)S(1)} custom-call(s32[6,40]{1,0:T(8,128)S(1)} %get-tuple-element.10.table_ref.refs_0_, f32[384,2,128]{2,1,0:T(2,128)S(1)} %bitcast.5), custom_call_target="tpu_custom_call" | custom-call | tf_op jit(solution)/shard_map/unpack_kernel/pallas_call | solution.py:325
  28.9 5.4 %collective-permute-start.1 = (f32[8,32,128]{2,1,0:T(8,128)S(1)}, f32[8,32,128]{2,1,0:T(8,128)S(1)}, u32[]{:S(2)}, u32[]{:S(2)}) collective-permute-start(f32[8,32,128]{2,1,0:T(8,128)S(1)} %unpack_kernel.1.refs_2_), channel_id=1, source_target_pairs={{1,64},{64,1},{3,66},{66,3},{5,68},{68,5},{7,70},{70,7},{9,72},{72... | collective-permute-start | bytes 393224 | tf_op jit(solution)/shard_map/ppermute | solution.py:441
  34.3 1.9 %collective-permute-start.2 = (f32[8,32,128]{2,1,0:T(8,128)S(1)}, f32[8,32,128]{2,1,0:T(8,128)S(1)}, u32[]{:S(2)}, u32[]{:S(2)}) collective-permute-start(f32[8,32,128]{2,1,0:T(8,128)S(1)} %unpack_kernel.1.refs_2_), channel_id=1, source_target_pairs={{0,1},{1,0},{2,3},{3,2},{4,5},{5,4},{6,7},{7,6},{8,9},{9,8},{10,11... | collective-permute-start | bytes 393224 | tf_op jit(solution)/shard_map/ppermute | solution.py:442
  36.2 0.7 %collective-permute-done.1.refs_1_ = f32[8,32,128]{2,1,0:T(8,128)S(1)} collective-permute-done((f32[8,32,128]{2,1,0:T(8,128)S(1)}, f32[8,32,128]{2,1,0:T(8,128)S(1)}, u32[]{:S(2)}, u32[]{:S(2)}) %collective-permute-start.1) | collective-permute-done | bytes 131104 | tf_op jit(solution)/shard_map/ppermute | solution.py:441
  37.0 0.6 %collective-permute-done.2.refs_3_ = f32[8,32,128]{2,1,0:T(8,128)S(1)} collective-permute-done((f32[8,32,128]{2,1,0:T(8,128)S(1)}, f32[8,32,128]{2,1,0:T(8,128)S(1)}, u32[]{:S(2)}, u32[]{:S(2)}) %collective-permute-start.2) | collective-permute-done | bytes 131104 | tf_op jit(solution)/shard_map/ppermute | solution.py:442
  37.6 2.2 %march_kernel.1 = f32[256,2,128]{2,1,0:T(2,128)S(1)} custom-call(s32[6,40]{1,0:T(8,128)S(1)} %get-tuple-element.10.table_ref.refs_0_, f32[8,32,128]{2,1,0:T(8,128)S(1)} %collective-permute-done.1.refs_1_, f32[8,32,128]{2,1,0:T(8,128)S(1)} %unpack_kernel.1.refs_2_, f32[8,32,128]{2,1,0:T(8,128)S(1)} %collective-permute-done.2.refs_3_, ...), custom_call_target="tpu_custom_call" | custom-call | tf_op jit(solution)/shard_map/march_kernel/pallas_call | solution.py:325
  39.8 19.1 %all_to_all.10 = f32[64,8,128]{2,1,0:T(8,128)S(1)} all-to-all(f32[64,8,128]{2,1,0:T(8,128)S(1)} %bitcast.6), channel_id=1, replica_groups=mesh['grp'=8,'mem'=64] {'mem'}, dimensions={0} | all-to-all | bytes 524288 | tf_op jit(solution)/shard_map/all_to_all | solution.py:425
  58.9 1.2 %deliver_kernel.1 = f32[512,128]{1,0:T(8,128)} custom-call(s32[1,64]{1,0:T(1,128)S(1)} %copy-done, f32[512,128]{1,0:T(8,128)S(1)} %bitcast.7), custom_call_target="tpu_custom_call" | custom-call | tf_op jit(solution)/shard_map/deliver_kernel/pallas_call | solution.py:325
  (1 shorter events, 0.0 us)
Async XLA Ops:
  2.0 11.0 %copy-start.1 = (s32[1,6,2048]{2,0,1:T(1,128)S(1)}, s32[1,6,2048]{2,0,1:T(1,128)}, u32[]{:S(2)}) copy-start(s32[1,6,2048]{2,0,1:T(1,128)} %param.5) | copy-start | bytes 147460
  2.1 26.0 %all-to-all-start = ((f32[192,4,128]{2,1,0:T(4,128)}), f32[192,4,128]{2,1,0:T(4,128)S(1)}, u32[]{:S(2)}, u32[]{:S(2)}) async-start(f32[192,4,128]{2,1,0:T(4,128)} %pack_kernel.1), calls=%async_computation | async-start | bytes 786432 | tf_op jit(solution)/shard_map/all_to_all | solution.py:425
  13.0 0.7 %copy-start = (s32[1,64]{1,0:T(1,128)S(1)}, s32[1,64]{1,0:T(1,128)}, u32[]{:S(2)}) copy-start(s32[1,64]{1,0:T(1,128)} %refs_0_.5) | copy-start | bytes 772
  17.2 7.8 %collective-permute-start = (f32[4,32,128]{2,1,0:T(8,128)S(1)}, f32[4,32,128]{2,1,0:T(8,128)S(1)}, u32[]{:S(2)}, u32[]{:S(2)}) collective-permute-start(f32[4,32,128]{2,1,0:T(8,128)S(1)} %get-tuple-element.11.refs_5_), channel_id=1, source_target_pairs={{1,64},{64,1},{3,66},{66,3},{5,68},{68,5},{7,70},{70,7},{9,72},{72... | collective-permute-start | bytes 196616 | tf_op jit(solution)/shard_map/ppermute | solution.py:438
  28.9 8.0 %collective-permute-start.1 = (f32[8,32,128]{2,1,0:T(8,128)S(1)}, f32[8,32,128]{2,1,0:T(8,128)S(1)}, u32[]{:S(2)}, u32[]{:S(2)}) collective-permute-start(f32[8,32,128]{2,1,0:T(8,128)S(1)} %unpack_kernel.1.refs_2_), channel_id=1, source_target_pairs={{1,64},{64,1},{3,66},{66,3},{5,68},{68,5},{7,70},{70,7},{9,72},{72... | collective-permute-start | bytes 393224 | tf_op jit(solution)/shard_map/ppermute | solution.py:441
  34.3 3.2 %collective-permute-start.2 = (f32[8,32,128]{2,1,0:T(8,128)S(1)}, f32[8,32,128]{2,1,0:T(8,128)S(1)}, u32[]{:S(2)}, u32[]{:S(2)}) collective-permute-start(f32[8,32,128]{2,1,0:T(8,128)S(1)} %unpack_kernel.1.refs_2_), channel_id=1, source_target_pairs={{0,1},{1,0},{2,3},{3,2},{4,5},{5,4},{6,7},{7,6},{8,9},{9,8},{10,11... | collective-permute-start | bytes 393224 | tf_op jit(solution)/shard_map/ppermute | solution.py:442

commit v7 on v5

--- a/solution.py
+++ b/solution.py
@@ -177,7 +177,7 @@
 
 def march_kernel(where_am_i, *refs):
     (
-        table_vmem,
+        table_ref,
         outer_ref,
         own_ref,
         inner_ref,
@@ -190,12 +190,8 @@
         pull_ref,
         side_ref,
         done_ref,
-        table_ref,
-        sem,
-    ) = refs[-15:]
+    ) = refs[-13:]
     here = where_am_i(refs)
-    fetch = pltpu.make_async_copy(table_vmem, table_ref, sem)
-    fetch.start()
     depth = 3 * HALF
     lane = iota((ROWS, 128), 1)
     first_y = lane < WIDE
@@ -273,7 +269,6 @@
             done_ref[row : row + ROWS, :] = jnp.where(
                 lower, shift(even_ref[p], -4, 1), shift(even_ref[p + PAIRS], 4, 1)
             )
-    fetch.wait()
     for r in range(ROWS):
         for column in range(2):
             out_ref[table_ref[4 + column, r + 1]] = done_ref[
@@ -323,7 +318,10 @@
         spaces = [pltpu.SMEM, *spaces]
     out = pl.pallas_call(
         kernel,
-        out_shape=[jax.ShapeDtypeStruct(s, t) for s, t in shapes],
+        out_shape=[
+            (pltpu.SMEM if space == pltpu.SMEM else jax.ShapeDtypeStruct)(*shape)
+            for shape, space in zip(shapes, out_spaces)
+        ],
         in_specs=[spec(s) for s in spaces],
         out_specs=[spec(s) for s in out_spaces],
         scratch_shapes=scratch,
@@ -380,7 +378,7 @@
 def unpack(table, received):
     (out,) = run(
         unpack_kernel,
-        (table, received.reshape(COLUMNS * SENT // PAIRS, PAIRS, 128)),
+        (pltpu.with_memory_space_constraint(table, pltpu.SMEM), received.reshape(COLUMNS * SENT // PAIRS, PAIRS, 128)),
         [((TILE, ROWS, 128), F32)],
         [pltpu.VMEM((4 * PAIRS * ROWS, 128), F32)],
         None,
@@ -392,15 +390,14 @@
 def march(table, outer, own, inner, far, near, faces, me=None):
     (out,) = run(
         bind(march_kernel, me),
-        (table, outer, own, inner, far, near, faces),
+        (pltpu.with_memory_space_constraint(table, pltpu.SMEM), outer, own, inner, far, near, faces),
         [((COLUMNS * BACK // PAIRS, PAIRS, 128), F32)],
         [pltpu.VMEM((6 * HALF, ROWS, 128), F32)] * 4
         + [
             pltpu.VMEM((2 * PAIRS * ROWS, 128), F32),
-            pltpu.SMEM((6, TABLE), I32),
-            pltpu.SemaphoreType.DMA,
         ],
         me,
+        [pltpu.SMEM] + [pltpu.VMEM] * 6,
     )
     return out.reshape(COLUMNS, BACK, 128)
 

time: 60.4 us -> 59.4 us (0.983)
  Pallas kernels: 9.85 us -> 8.86 us
    pallas_call x5, Pallas kernels: 9.85 us -> 8.86 us  [run(): pl.pallas_call(kernel, out_shape=[(pltpu.SMEM if space == pltpu.SMEM else...]
  transfers between devices with their start and end apart: 4 -> 4, of which waited for: 4 -> 4; matrix products, arithmetic and copies ran while one was open for 0% -> 0% of each run, Pallas kernels for 6% -> 5%
where the time goes in v7:
time: 59.4 us; the launch traced here: 59.1 us
  starting transfers between devices  23.8 us (40%)
  blocking collectives  18.8 us (32%)
  Pallas kernels  8.86 us (15%)
  waiting for transfers between devices  6.95 us (12%)
  local copies, waits for them, and re-layouts  0.65 us (1%)
    all_to_all x1, blocking collectives, exchange(): return lax.all_to_all(x, 'mem', split_axis=0, concat_axis=0, tiled=True)  18.8 us
    all_to_all x1, starting transfers between devices, exchange(): return lax.all_to_all(x, 'mem', split_axis=0, concat_axis=0, tiled=True)  10.9 us
    pallas_call x5, Pallas kernels, run(): pl.pallas_call(kernel, out_shape=[(pltpu.SMEM if space == pltpu.SMEM else...  8.86 us
    ppermute x1, starting transfers between devices, on_device(): far = lax.ppermute(near, ('grp', 'mem'), across)  5.55 us
    ppermute x1, starting transfers between devices, on_device(): outer = lax.ppermute(own, ('grp', 'mem'), across)  5.37 us
    all_to_all x1, waiting for transfers between devices, exchange(): return lax.all_to_all(x, 'mem', split_axis=0, concat_axis=0, tiled=True)  3.41 us
    ppermute x1, waiting for transfers between devices, on_device(): far = lax.ppermute(near, ('grp', 'mem'), across)  2.23 us
    ppermute x1, starting transfers between devices, on_device(): inner = lax.ppermute(own, 'mem', mates)  1.92 us
  transfers between devices with their start and end apart: 4, of which 4 were waited for; matrix products, arithmetic and copies ran while one was open for 0% of the time, Pallas kernels for 5%

profile of v7, /device:TPU:193, one launch (start us, length us, event | category | flops | bytes accessed | tf_op | source)
XLA Modules:
  0.0 59.1 jit_solution(6346758422574524894)
XLA Ops:
  0.0 2.0 %pack_kernel.1 = f32[768,128]{1,0:T(8,128)} custom-call(s32[1,64]{1,0:T(1,128)} %refs_0_.5, f32[512,128]{1,0:T(8,128)} %bitcast.10), custom_call_target="tpu_custom_call" | custom-call | tf_op jit(solution)/shard_map/pack_kernel/pallas_call | solution.py:319
  2.0 0.0 copy-start.1
  2.1 10.9 %all-to-all-start = ((f32[192,4,128]{2,1,0:T(4,128)}), f32[192,4,128]{2,1,0:T(4,128)S(1)}, u32[]{:S(2)}, u32[]{:S(2)}) async-start(f32[192,4,128]{2,1,0:T(4,128)} %bitcast.9), calls=%async_computation | async-start | bytes 786432 | tf_op jit(solution)/shard_map/all_to_all | solution.py:417
  13.0 0.0 copy-done.1
  13.0 0.0 copy-start
  13.0 0.6 %copy-done = s32[1,64]{1,0:T(1,128)S(1)} copy-done((s32[1,64]{1,0:T(1,128)S(1)}, s32[1,64]{1,0:T(1,128)}, u32[]{:S(2)}) %copy-start) | copy-done | bytes 280
  13.7 3.2 %mask_kernel.1 = (f32[4,32,128]{2,1,0:T(8,128)S(1)}, f32[2,32,128]{2,1,0:T(8,128)S(1)}, s32[6,40]{1,0:T(8,128)S(4)}) custom-call(s32[1,64]{1,0:T(1,128)S(1)} %copy-done, s32[1,6,2048]{2,1,0:T(8,128)S(1)} %copy.4.refs_1_), custom_call_target="tpu_custom_call" | custom-call | flops 4194304 | bytes 131072 | tf_op jit(solution)/shard_map/mask_kernel/pallas_call | solution.py:319
  16.9 5.6 %collective-permute-start = (f32[4,32,128]{2,1,0:T(8,128)S(1)}, f32[4,32,128]{2,1,0:T(8,128)S(1)}, u32[]{:S(2)}, u32[]{:S(2)}) collective-permute-start(f32[4,32,128]{2,1,0:T(8,128)S(1)} %get-tuple-element.11.refs_5_), channel_id=1, source_target_pairs={{1,64},{64,1},{3,66},{66,3},{5,68},{68,5},{7,70},{70,7},{9,72},{72... | collective-permute-start | bytes 196616 | tf_op jit(solution)/shard_map/ppermute | solution.py:430
  22.4 2.2 %collective-permute-done.refs_4_ = f32[4,32,128]{2,1,0:T(8,128)S(1)} collective-permute-done((f32[4,32,128]{2,1,0:T(8,128)S(1)}, f32[4,32,128]{2,1,0:T(8,128)S(1)}, u32[]{:S(2)}, u32[]{:S(2)}) %collective-permute-start) | collective-permute-done | bytes 65568 | tf_op jit(solution)/shard_map/ppermute | solution.py:430
  24.6 3.4 %all-to-all-done = f32[192,4,128]{2,1,0:T(4,128)S(1)} async-done(((f32[192,4,128]{2,1,0:T(4,128)}), f32[192,4,128]{2,1,0:T(4,128)S(1)}, u32[]{:S(2)}, u32[]{:S(2)}) %all-to-all-start) | async-done | bytes 393248 | tf_op jit(solution)/shard_map/all_to_all | solution.py:417
  28.1 0.3 unpack_kernel.1.refs_2_
  28.4 5.4 %collective-permute-start.1 = (f32[8,32,128]{2,1,0:T(8,128)S(1)}, f32[8,32,128]{2,1,0:T(8,128)S(1)}, u32[]{:S(2)}, u32[]{:S(2)}) collective-permute-start(f32[8,32,128]{2,1,0:T(8,128)S(1)} %unpack_kernel.1.refs_2_), channel_id=1, source_target_pairs={{1,64},{64,1},{3,66},{66,3},{5,68},{68,5},{7,70},{70,7},{9,72},{72... | collective-permute-start | bytes 393224 | tf_op jit(solution)/shard_map/ppermute | solution.py:433
  33.7 1.9 %collective-permute-start.2 = (f32[8,32,128]{2,1,0:T(8,128)S(1)}, f32[8,32,128]{2,1,0:T(8,128)S(1)}, u32[]{:S(2)}, u32[]{:S(2)}) collective-permute-start(f32[8,32,128]{2,1,0:T(8,128)S(1)} %unpack_kernel.1.refs_2_), channel_id=1, source_target_pairs={{0,1},{1,0},{2,3},{3,2},{4,5},{5,4},{6,7},{7,6},{8,9},{9,8},{10,11... | collective-permute-start | bytes 393224 | tf_op jit(solution)/shard_map/ppermute | solution.py:434
  35.7 0.7 %collective-permute-done.1.refs_1_ = f32[8,32,128]{2,1,0:T(8,128)S(1)} collective-permute-done((f32[8,32,128]{2,1,0:T(8,128)S(1)}, f32[8,32,128]{2,1,0:T(8,128)S(1)}, u32[]{:S(2)}, u32[]{:S(2)}) %collective-permute-start.1) | collective-permute-done | bytes 131104 | tf_op jit(solution)/shard_map/ppermute | solution.py:433
  36.4 0.6 %collective-permute-done.2.refs_3_ = f32[8,32,128]{2,1,0:T(8,128)S(1)} collective-permute-done((f32[8,32,128]{2,1,0:T(8,128)S(1)}, f32[8,32,128]{2,1,0:T(8,128)S(1)}, u32[]{:S(2)}, u32[]{:S(2)}) %collective-permute-start.2) | collective-permute-done | bytes 131104 | tf_op jit(solution)/shard_map/ppermute | solution.py:434
  37.0 2.2 %march_kernel.1 = f32[256,2,128]{2,1,0:T(2,128)S(1)} custom-call(s32[6,40]{1,0:T(8,128)S(4)} %get-tuple-element.10.table_ref.refs_0_, f32[8,32,128]{2,1,0:T(8,128)S(1)} %collective-permute-done.1.refs_1_, f32[8,32,128]{2,1,0:T(8,128)S(1)} %unpack_kernel.1.refs_2_, f32[8,32,128]{2,1,0:T(8,128)S(1)} %collective-permute-done.2.refs_3_, ...), custom_call_target="tpu_custom_call" | custom-call | tf_op jit(solution)/shard_map/march_kernel/pallas_call | solution.py:319
  39.2 18.8 %all_to_all.10 = f32[64,8,128]{2,1,0:T(8,128)S(1)} all-to-all(f32[64,8,128]{2,1,0:T(8,128)S(1)} %bitcast.7), channel_id=1, replica_groups=mesh['grp'=8,'mem'=64] {'mem'}, dimensions={0} | all-to-all | bytes 524288 | tf_op jit(solution)/shard_map/all_to_all | solution.py:417
  57.9 1.2 %deliver_kernel.1 = f32[512,128]{1,0:T(8,128)} custom-call(s32[1,64]{1,0:T(1,128)S(1)} %copy-done, f32[512,128]{1,0:T(8,128)S(1)} %bitcast.8), custom_call_target="tpu_custom_call" | custom-call | tf_op jit(solution)/shard_map/deliver_kernel/pallas_call | solution.py:319
  (1 shorter events, 0.0 us)
Async XLA Ops:
  2.0 11.0 %copy-start.1 = (s32[1,6,2048]{2,0,1:T(1,128)S(1)}, s32[1,6,2048]{2,0,1:T(1,128)}, u32[]{:S(2)}) copy-start(s32[1,6,2048]{2,0,1:T(1,128)} %param.5) | copy-start | bytes 147460
  2.1 26.0 %all-to-all-start = ((f32[192,4,128]{2,1,0:T(4,128)}), f32[192,4,128]{2,1,0:T(4,128)S(1)}, u32[]{:S(2)}, u32[]{:S(2)}) async-start(f32[192,4,128]{2,1,0:T(4,128)} %bitcast.9), calls=%async_computation | async-start | bytes 786432 | tf_op jit(solution)/shard_map/all_to_all | solution.py:417
  13.0 0.7 %copy-start = (s32[1,64]{1,0:T(1,128)S(1)}, s32[1,64]{1,0:T(1,128)}, u32[]{:S(2)}) copy-start(s32[1,64]{1,0:T(1,128)} %refs_0_.5) | copy-start | bytes 772
  16.9 7.8 %collective-permute-start = (f32[4,32,128]{2,1,0:T(8,128)S(1)}, f32[4,32,128]{2,1,0:T(8,128)S(1)}, u32[]{:S(2)}, u32[]{:S(2)}) collective-permute-start(f32[4,32,128]{2,1,0:T(8,128)S(1)} %get-tuple-element.11.refs_5_), channel_id=1, source_target_pairs={{1,64},{64,1},{3,66},{66,3},{5,68},{68,5},{7,70},{70,7},{9,72},{72... | collective-permute-start | bytes 196616 | tf_op jit(solution)/shard_map/ppermute | solution.py:430
  28.4 8.0 %collective-permute-start.1 = (f32[8,32,128]{2,1,0:T(8,128)S(1)}, f32[8,32,128]{2,1,0:T(8,128)S(1)}, u32[]{:S(2)}, u32[]{:S(2)}) collective-permute-start(f32[8,32,128]{2,1,0:T(8,128)S(1)} %unpack_kernel.1.refs_2_), channel_id=1, source_target_pairs={{1,64},{64,1},{3,66},{66,3},{5,68},{68,5},{7,70},{70,7},{9,72},{72... | collective-permute-start | bytes 393224 | tf_op jit(solution)/shard_map/ppermute | solution.py:433
  33.7 3.2 %collective-permute-start.2 = (f32[8,32,128]{2,1,0:T(8,128)S(1)}, f32[8,32,128]{2,1,0:T(8,128)S(1)}, u32[]{:S(2)}, u32[]{:S(2)}) collective-permute-start(f32[8,32,128]{2,1,0:T(8,128)S(1)} %unpack_kernel.1.refs_2_), channel_id=1, source_target_pairs={{0,1},{1,0},{2,3},{3,2},{4,5},{5,4},{6,7},{7,6},{8,9},{9,8},{10,11... | collective-permute-start | bytes 393224 | tf_op jit(solution)/shard_map/ppermute | solution.py:434

commit v8 on v7

--- a/solution.py
+++ b/solution.py
@@ -175,43 +175,16 @@
         )
 
 
-def march_kernel(where_am_i, *refs):
-    (
-        table_ref,
-        outer_ref,
-        own_ref,
-        inner_ref,
-        far_ref,
-        near_ref,
-        faces_ref,
-        out_ref,
-        even_ref,
-        odd_ref,
-        pull_ref,
-        side_ref,
-        done_ref,
-    ) = refs[-13:]
-    here = where_am_i(refs)
-    depth = 3 * HALF
+EARLY = HALF + 1
+EARLY_PLANES = TILE - 2
+
+
+def stepper(load, keep, signs, links, faces_ref):
     lane = iota((ROWS, 128), 1)
     first_y = lane < WIDE
     last_y = lane >= 128 - WIDE
 
-    def start(column, p):
-        base = column * HALF
-        if p < HALF:
-            return outer_ref[base + HALF - 1 - p]
-        if p < 2 * HALF:
-            return own_ref[base + p - HALF]
-        return inner_ref[base + depth - 1 - p]
-
-    def load(step, column, p):
-        if step == 0:
-            return start(column, p)
-        return (odd_ref if step % 2 else even_ref)[column * depth + p]
-
     def one_step(step, column, lo, hi):
-        target_ref = even_ref if step % 2 else odd_ref
         level = load(step, column, lo - 1)
         after = load(step, column, lo)
         ahead_z = after - level
@@ -224,22 +197,22 @@
             ahead_z = after - level
             if p == HALF - 1:
                 ahead_z = ahead_z * faces_ref[column]
-            links = far_ref if p < HALF else near_ref
+            pull_ref, side_ref, at = signs(column, p)
             if step == 0:
                 sign_field = level * lax.rsqrt(level * level + 1.0)
                 pull = TIME_STEP * sign_field
                 up = jnp.where(sign_field > 0, 1.0, -1.0)
-                pull_ref[column * depth + p] = pull
-                side_ref[column * depth + p] = up
+                pull_ref[at] = pull
+                side_ref[at] = up
             else:
-                pull = pull_ref[column * depth + p]
-                up = side_ref[column * depth + p]
+                pull = pull_ref[at]
+                up = side_ref[at]
             down = -up
-            ahead = (shift(level, -1, 1) - level) * links[column]
+            ahead = (shift(level, -1, 1) - level) * links(p)[column]
             back = shift(ahead, 1, 1)
             squares = jnp.square(jnp.maximum(jnp.maximum(up * back, down * ahead), 0.0))
             beyond = jnp.where(first_y, shift(level, -1, 0), level)
-            ahead = (shift(beyond, -WIDE, 1) - level) * links[2 + column]
+            ahead = (shift(beyond, -WIDE, 1) - level) * links(p)[2 + column]
             back = shift(jnp.where(last_y, shift(ahead, 1, 0), ahead), WIDE, 1)
             squares = squares + jnp.square(
                 jnp.maximum(jnp.maximum(up * back, down * ahead), 0.0)
@@ -248,23 +221,90 @@
                 jnp.maximum(jnp.maximum(up * back_z, down * ahead_z), 0.0)
             )
             length = squares + EPSILON
-            target_ref[column * depth + p] = level - pull * (
-                length * lax.rsqrt(length) - 1.0
-            )
-
-    spans = ((1, 11), (2, 10), (3, 9), (4, 8))
-
-    def several(steps, columns):
-        for step in steps:
-            for column in columns:
-                one_step(step, column, *spans[step])
-
-    for block, (steps, columns) in enumerate((((0,), (0,)), ((0,), (1,)), ((1,), (0,)), ((1,), (1,)), ((2,), (0,)), ((2,), (1,)), ((3,), (0, 1)))):
-        pl.when(here > -1 - block)(functools.partial(several, steps, columns))
-    lower = lane % WIDE < TILE
+            keep(step, column, p, level - pull * (length * lax.rsqrt(length) - 1.0))
+
+    return one_step
+
+
+def in_blocks(here, one_step, plan):
+    def several(step, columns, lo, hi):
+        for column in columns:
+            one_step(step, column, lo, hi)
+
+    for block, entry in enumerate(plan):
+        pl.when(here > -1 - block)(functools.partial(several, *entry))
+
+
+def early_kernel(where_am_i, *refs):
+    own_ref, inner_ref, near_ref, odd_ref, even_ref, pull_ref, side_ref = refs[-7:]
+
+    def at(column, p):
+        return column * EARLY_PLANES + p - EARLY
+
+    def load(step, column, p):
+        if step == 0:
+            base = column * HALF
+            return own_ref[base + p - HALF] if p < TILE else inner_ref[base + 3 * HALF - 1 - p]
+        return (odd_ref if step % 2 else even_ref)[at(column, p)]
+
+    def keep(step, column, p, value):
+        (even_ref if step % 2 else odd_ref)[at(column, p)] = value
+
+    one_step = stepper(
+        load, keep, lambda column, p: (pull_ref, side_ref, at(column, p)), lambda p: near_ref, None
+    )
+    plan = ((0, (0,), 5, 11), (0, (1,), 5, 11), (1, (0, 1), 6, 10), (2, (0, 1), 7, 9))
+    in_blocks(where_am_i(refs), one_step, plan)
+
+
+def late_kernel(where_am_i, *refs):
+    (
+        table_ref,
+        outer_ref,
+        own_ref,
+        far_ref,
+        near_ref,
+        faces_ref,
+        early_odd_ref,
+        early_even_ref,
+        early_pull_ref,
+        early_side_ref,
+        out_ref,
+        even_ref,
+        odd_ref,
+        pull_ref,
+        side_ref,
+        done_ref,
+    ) = refs[-16:]
+
+    def early(column, p):
+        return column * EARLY_PLANES + p - EARLY
+
+    def at(column, p):
+        return column * TILE + p
+
+    def load(step, column, p):
+        if step == 0:
+            base = column * HALF
+            return outer_ref[base + HALF - 1 - p] if p < HALF else own_ref[base + p - HALF]
+        if p >= EARLY + step - 1:
+            return (early_odd_ref if step % 2 else early_even_ref)[early(column, p)]
+        return (odd_ref if step % 2 else even_ref)[at(column, p)]
+
+    def keep(step, column, p, value):
+        (even_ref if step % 2 else odd_ref)[at(column, p)] = value
+
+    def signs(column, p):
+        if p >= EARLY:
+            return early_pull_ref, early_side_ref, early(column, p)
+        return pull_ref, side_ref, at(column, p)
+
+    one_step = stepper(load, keep, signs, lambda p: far_ref if p < HALF else near_ref, faces_ref)
+    in_blocks(where_am_i(refs), one_step, [(s, (0, 1), 1 + s, 5 + s) for s in range(STEPS)])
+    lower = iota((ROWS, 128), 1) % WIDE < TILE
     for column in range(2):
         for pair in range(PAIRS):
-            p = column * depth + HALF + pair
+            p = at(column, HALF + pair)
             row = (column * PAIRS + pair) * ROWS
             done_ref[row : row + ROWS, :] = jnp.where(
                 lower, shift(even_ref[p], -4, 1), shift(even_ref[p + PAIRS], 4, 1)
@@ -387,17 +427,34 @@
     return out
 
 
-def march(table, outer, own, inner, far, near, faces, me=None):
+def start_march(own, inner, near, me=None):
+    return run(
+        bind(early_kernel, me),
+        (own, inner, near),
+        [((2 * EARLY_PLANES, ROWS, 128), F32)] * 4,
+        [],
+        me,
+        cost=(1 << 22, 1 << 20),
+    )
+
+
+def end_march(table, outer, own, far, near, faces, early, me=None):
     (out,) = run(
-        bind(march_kernel, me),
-        (pltpu.with_memory_space_constraint(table, pltpu.SMEM), outer, own, inner, far, near, faces),
+        bind(late_kernel, me),
+        (
+            pltpu.with_memory_space_constraint(table, pltpu.SMEM),
+            outer,
+            own,
+            far,
+            near,
+            faces,
+            *early,
+        ),
         [((COLUMNS * BACK // PAIRS, PAIRS, 128), F32)],
-        [pltpu.VMEM((6 * HALF, ROWS, 128), F32)] * 4
-        + [
-            pltpu.VMEM((2 * PAIRS * ROWS, 128), F32),
-        ],
+        [pltpu.VMEM((2 * TILE, ROWS, 128), F32)] * 4
+        + [pltpu.VMEM((2 * PAIRS * ROWS, 128), F32)],
         me,
-        [pltpu.SMEM] + [pltpu.VMEM] * 6,
+        [pltpu.SMEM] + [pltpu.VMEM] * 9,
     )
     return out.reshape(COLUMNS, BACK, 128)
 
@@ -430,9 +487,10 @@
     far = lax.ppermute(near, ("grp", "mem"), across)
     received, far = lax.optimization_barrier((received, far))
     own = unpack(table, received)
+    inner = lax.ppermute(own, "mem", mates)
     outer = lax.ppermute(own, ("grp", "mem"), across)
-    inner = lax.ppermute(own, "mem", mates)
-    returned = exchange(march(table, outer, own, inner, far, near, faces))
+    early = start_march(own, inner, near)
+    returned = exchange(end_march(table, outer, own, far, near, faces, early))
     return deliver(band_counts, returned)
 
 

time: 59.4 us -> 59.8 us (level)
    ppermute x1, waiting for transfers between devices: 0.71 us -> 1.63 us  [on_device(): outer = lax.ppermute(own, ('grp', 'mem'), across)]
    ppermute x1, waiting for transfers between devices: 0.6 us -> 0.01 us  [on_device(): inner = lax.ppermute(own, 'mem', mates)]
    pallas_call x5 -> x6, Pallas kernels: 8.86 us -> 8.96 us  [run(): pl.pallas_call(kernel, out_shape=[(pltpu.SMEM if space == pltpu.SMEM else...]
  transfers between devices with their start and end apart: 4 -> 4, of which waited for: 4 -> 3; matrix products, arithmetic and copies ran while one was open for 0% -> 0% of each run, Pallas kernels for 5% -> 7%
where the time goes in v8:
time: 59.8 us; the launch traced here: 59.5 us
  starting transfers between devices  24 us (40%)
  blocking collectives  18.5 us (31%)
  Pallas kernels  8.96 us (15%)
  waiting for transfers between devices  7.27 us (12%)
  local copies, waits for them, and re-layouts  0.65 us (1%)
    all_to_all x1, blocking collectives, exchange(): return lax.all_to_all(x, 'mem', split_axis=0, concat_axis=0, tiled=True)  18.5 us
    all_to_all x1, starting transfers between devices, exchange(): return lax.all_to_all(x, 'mem', split_axis=0, concat_axis=0, tiled=True)  10.9 us
    pallas_call x6, Pallas kernels, run(): pl.pallas_call(kernel, out_shape=[(pltpu.SMEM if space == pltpu.SMEM else...  8.96 us
    ppermute x1, starting transfers between devices, on_device(): far = lax.ppermute(near, ('grp', 'mem'), across)  5.55 us
    ppermute x1, starting transfers between devices, on_device(): outer = lax.ppermute(own, ('grp', 'mem'), across)  5.33 us
    all_to_all x1, waiting for transfers between devices, exchange(): return lax.all_to_all(x, 'mem', split_axis=0, concat_axis=0, tiled=True)  3.41 us
    ppermute x1, waiting for transfers between devices, on_device(): far = lax.ppermute(near, ('grp', 'mem'), across)  2.23 us
    ppermute x1, starting transfers between devices, on_device(): inner = lax.ppermute(own, 'mem', mates)  2.18 us
  transfers between devices with their start and end apart: 4, of which 3 were waited for; matrix products, arithmetic and copies ran while one was open for 0% of the time, Pallas kernels for 7%

profile of v8, /device:TPU:193, one launch (start us, length us, event | category | flops | bytes accessed | tf_op | source)
XLA Modules:
  0.0 59.5 jit_solution(6177505109442812282)
XLA Ops:
  0.0 2.0 %pack_kernel.1 = f32[768,128]{1,0:T(8,128)} custom-call(s32[1,64]{1,0:T(1,128)} %refs_0_.5, f32[512,128]{1,0:T(8,128)} %bitcast.10), custom_call_target="tpu_custom_call" | custom-call | tf_op jit(solution)/shard_map/pack_kernel/pallas_call | solution.py:359
  2.0 0.0 copy-start.1
  2.0 10.9 %all-to-all-start = ((f32[192,4,128]{2,1,0:T(4,128)}), f32[192,4,128]{2,1,0:T(4,128)S(1)}, u32[]{:S(2)}, u32[]{:S(2)}) async-start(f32[192,4,128]{2,1,0:T(4,128)} %bitcast.9), calls=%async_computation | async-start | bytes 786432 | tf_op jit(solution)/shard_map/all_to_all | solution.py:474
  13.0 0.0 copy-done.1
  13.0 0.0 copy-start
  13.0 0.6 %copy-done = s32[1,64]{1,0:T(1,128)S(1)} copy-done((s32[1,64]{1,0:T(1,128)S(1)}, s32[1,64]{1,0:T(1,128)}, u32[]{:S(2)}) %copy-start) | copy-done | bytes 280
  13.7 3.2 %mask_kernel.1 = (f32[4,32,128]{2,1,0:T(8,128)S(1)}, f32[2,32,128]{2,1,0:T(8,128)S(1)}, s32[6,40]{1,0:T(8,128)S(4)}) custom-call(s32[1,64]{1,0:T(1,128)S(1)} %copy-done, s32[1,6,2048]{2,1,0:T(8,128)S(1)} %copy.4.refs_1_), custom_call_target="tpu_custom_call" | custom-call | flops 4194304 | bytes 131072 | tf_op jit(solution)/shard_map/mask_kernel/pallas_call | solution.py:359
  16.9 5.5 %collective-permute-start = (f32[4,32,128]{2,1,0:T(8,128)S(1)}, f32[4,32,128]{2,1,0:T(8,128)S(1)}, u32[]{:S(2)}, u32[]{:S(2)}) collective-permute-start(f32[4,32,128]{2,1,0:T(8,128)S(1)} %get-tuple-element.15.refs_2_.refs_4_), channel_id=1, source_target_pairs={{1,64},{64,1},{3,66},{66,3},{5,68},{68,5},{7,70},{70,7},{9,72},{72... | collective-permute-start | bytes 196616 | tf_op jit(solution)/shard_map/ppermute | solution.py:487
  22.4 2.2 %collective-permute-done.refs_3_ = f32[4,32,128]{2,1,0:T(8,128)S(1)} collective-permute-done((f32[4,32,128]{2,1,0:T(8,128)S(1)}, f32[4,32,128]{2,1,0:T(8,128)S(1)}, u32[]{:S(2)}, u32[]{:S(2)}) %collective-permute-start) | collective-permute-done | bytes 65568 | tf_op jit(solution)/shard_map/ppermute | solution.py:487
  24.6 3.4 %all-to-all-done = f32[192,4,128]{2,1,0:T(4,128)S(1)} async-done(((f32[192,4,128]{2,1,0:T(4,128)}), f32[192,4,128]{2,1,0:T(4,128)S(1)}, u32[]{:S(2)}, u32[]{:S(2)}) %all-to-all-start) | async-done | bytes 393248 | tf_op jit(solution)/shard_map/all_to_all | solution.py:474
  28.1 0.3 unpack_kernel.1.refs_0_.refs_2_
  28.4 2.2 %collective-permute-start.2 = (f32[8,32,128]{2,1,0:T(8,128)S(1)}, f32[8,32,128]{2,1,0:T(8,128)S(1)}, u32[]{:S(2)}, u32[]{:S(2)}) collective-permute-start(f32[8,32,128]{2,1,0:T(8,128)S(1)} %unpack_kernel.1.refs_0_.refs_2_), channel_id=1, source_target_pairs={{0,1},{1,0},{2,3},{3,2},{4,5},{5,4},{6,7},{7,6},{8,9},{9,8},{10,11... | collective-permute-start | bytes 393224 | tf_op jit(solution)/shard_map/ppermute | solution.py:490
  30.5 5.3 %collective-permute-start.1 = (f32[8,32,128]{2,1,0:T(8,128)S(1)}, f32[8,32,128]{2,1,0:T(8,128)S(1)}, u32[]{:S(2)}, u32[]{:S(2)}) collective-permute-start(f32[8,32,128]{2,1,0:T(8,128)S(1)} %unpack_kernel.1.refs_0_.refs_2_), channel_id=1, source_target_pairs={{1,64},{64,1},{3,66},{66,3},{5,68},{68,5},{7,70},{70,7},{9,72},{72... | collective-permute-start | bytes 393224 | tf_op jit(solution)/shard_map/ppermute | solution.py:491
  35.9 0.0 collective-permute-done.2.refs_1_
  35.9 1.0 %early_kernel.1 = (f32[12,32,128]{2,1,0:T(8,128)S(1)}, f32[12,32,128]{2,1,0:T(8,128)S(1)}, f32[12,32,128]{2,1,0:T(8,128)S(1)}, f32[12,32,128]{2,1,0:T(8,128)S(1)}) custom-call(f32[8,32,128]{2,1,0:T(8,128)S(1)} %unpack_kernel.1.refs_0_.refs_2_, f32[8,32,128]{2,1,0:T(8,128)S(1)} %collective-permute-done.2.refs_1_, ...), custom_call_target="tpu_custom_call" | custom-call | flops 4194304 | bytes 1048576 | tf_op jit(solution)/shard_map/early_kernel/pallas_call | solution.py:359
  36.9 1.6 %collective-permute-done.1.refs_1_ = f32[8,32,128]{2,1,0:T(8,128)S(1)} collective-permute-done((f32[8,32,128]{2,1,0:T(8,128)S(1)}, f32[8,32,128]{2,1,0:T(8,128)S(1)}, u32[]{:S(2)}, u32[]{:S(2)}) %collective-permute-start.1) | collective-permute-done | bytes 131104 | tf_op jit(solution)/shard_map/ppermute | solution.py:491
  38.5 1.3 %late_kernel.1 = f32[256,2,128]{2,1,0:T(2,128)S(1)} custom-call(s32[6,40]{1,0:T(8,128)S(4)} %get-tuple-element.14.table_ref.refs_0_, f32[8,32,128]{2,1,0:T(8,128)S(1)} %collective-permute-done.1.refs_1_, f32[8,32,128]{2,1,0:T(8,128)S(1)} %unpack_kernel.1.refs_0_.refs_2_, f32[4,32,128]{2,1,0:T(8,128)S(1)} %collective-permute-done.refs_3_, ...), custom_call_target="tpu_custom_call" | custom-call | tf_op jit(solution)/shard_map/late_kernel/pallas_call | solution.py:359
  39.8 18.5 %all_to_all.10 = f32[64,8,128]{2,1,0:T(8,128)S(1)} all-to-all(f32[64,8,128]{2,1,0:T(8,128)S(1)} %bitcast.8), channel_id=1, replica_groups=mesh['grp'=8,'mem'=64] {'mem'}, dimensions={0} | all-to-all | bytes 524288 | tf_op jit(solution)/shard_map/all_to_all | solution.py:474
  58.3 1.2 %deliver_kernel.1 = f32[512,128]{1,0:T(8,128)} custom-call(s32[1,64]{1,0:T(1,128)S(1)} %copy-done, f32[512,128]{1,0:T(8,128)S(1)} %bitcast.7), custom_call_target="tpu_custom_call" | custom-call | tf_op jit(solution)/shard_map/deliver_kernel/pallas_call | solution.py:359
  (1 shorter events, 0.0 us)
Async XLA Ops:
  2.0 11.0 %copy-start.1 = (s32[1,6,2048]{2,0,1:T(1,128)S(1)}, s32[1,6,2048]{2,0,1:T(1,128)}, u32[]{:S(2)}) copy-start(s32[1,6,2048]{2,0,1:T(1,128)} %param.5) | copy-start | bytes 147460
  2.0 26.0 %all-to-all-start = ((f32[192,4,128]{2,1,0:T(4,128)}), f32[192,4,128]{2,1,0:T(4,128)S(1)}, u32[]{:S(2)}, u32[]{:S(2)}) async-start(f32[192,4,128]{2,1,0:T(4,128)} %bitcast.9), calls=%async_computation | async-start | bytes 786432 | tf_op jit(solution)/shard_map/all_to_all | solution.py:474
  13.0 0.7 %copy-start = (s32[1,64]{1,0:T(1,128)S(1)}, s32[1,64]{1,0:T(1,128)}, u32[]{:S(2)}) copy-start(s32[1,64]{1,0:T(1,128)} %refs_0_.5) | copy-start | bytes 772
  16.9 7.8 %collective-permute-start = (f32[4,32,128]{2,1,0:T(8,128)S(1)}, f32[4,32,128]{2,1,0:T(8,128)S(1)}, u32[]{:S(2)}, u32[]{:S(2)}) collective-permute-start(f32[4,32,128]{2,1,0:T(8,128)S(1)} %get-tuple-element.15.refs_2_.refs_4_), channel_id=1, source_target_pairs={{1,64},{64,1},{3,66},{66,3},{5,68},{68,5},{7,70},{70,7},{9,72},{72... | collective-permute-start | bytes 196616 | tf_op jit(solution)/shard_map/ppermute | solution.py:487
  28.4 7.5 %collective-permute-start.2 = (f32[8,32,128]{2,1,0:T(8,128)S(1)}, f32[8,32,128]{2,1,0:T(8,128)S(1)}, u32[]{:S(2)}, u32[]{:S(2)}) collective-permute-start(f32[8,32,128]{2,1,0:T(8,128)S(1)} %unpack_kernel.1.refs_0_.refs_2_), channel_id=1, source_target_pairs={{0,1},{1,0},{2,3},{3,2},{4,5},{5,4},{6,7},{7,6},{8,9},{9,8},{10,11... | collective-permute-start | bytes 393224 | tf_op jit(solution)/shard_map/ppermute | solution.py:490
  30.5 8.0 %collective-permute-start.1 = (f32[8,32,128]{2,1,0:T(8,128)S(1)}, f32[8,32,128]{2,1,0:T(8,128)S(1)}, u32[]{:S(2)}, u32[]{:S(2)}) collective-permute-start(f32[8,32,128]{2,1,0:T(8,128)S(1)} %unpack_kernel.1.refs_0_.refs_2_), channel_id=1, source_target_pairs={{1,64},{64,1},{3,66},{66,3},{5,68},{68,5},{7,70},{70,7},{9,72},{72... | collective-permute-start | bytes 393224 | tf_op jit(solution)/shard_map/ppermute | solution.py:491

commit v9 on v8

--- a/solution.py
+++ b/solution.py
@@ -175,7 +175,6 @@
         )
 
 
-EARLY = HALF + 1
 EARLY_PLANES = TILE - 2
 
 
@@ -235,34 +234,35 @@
         pl.when(here > -1 - block)(functools.partial(several, *entry))
 
 
+def early_at(column, p):
+    return column * EARLY_PLANES + p - 1
+
+
 def early_kernel(where_am_i, *refs):
-    own_ref, inner_ref, near_ref, odd_ref, even_ref, pull_ref, side_ref = refs[-7:]
-
-    def at(column, p):
-        return column * EARLY_PLANES + p - EARLY
+    outer_ref, own_ref, far_ref, near_ref, faces_ref, odd_ref, even_ref, pull_ref, side_ref = refs[-9:]
 
     def load(step, column, p):
         if step == 0:
             base = column * HALF
-            return own_ref[base + p - HALF] if p < TILE else inner_ref[base + 3 * HALF - 1 - p]
-        return (odd_ref if step % 2 else even_ref)[at(column, p)]
+            return outer_ref[base + HALF - 1 - p] if p < HALF else own_ref[base + p - HALF]
+        return (odd_ref if step % 2 else even_ref)[early_at(column, p)]
 
     def keep(step, column, p, value):
-        (even_ref if step % 2 else odd_ref)[at(column, p)] = value
-
-    one_step = stepper(
-        load, keep, lambda column, p: (pull_ref, side_ref, at(column, p)), lambda p: near_ref, None
-    )
-    plan = ((0, (0,), 5, 11), (0, (1,), 5, 11), (1, (0, 1), 6, 10), (2, (0, 1), 7, 9))
+        (even_ref if step % 2 else odd_ref)[early_at(column, p)] = value
+
+    def signs(column, p):
+        return pull_ref, side_ref, early_at(column, p)
+
+    one_step = stepper(load, keep, signs, lambda p: far_ref if p < HALF else near_ref, faces_ref)
+    plan = ((0, (0,), 1, 7), (0, (1,), 1, 7), (1, (0, 1), 2, 6), (2, (0, 1), 3, 5))
     in_blocks(where_am_i(refs), one_step, plan)
 
 
 def late_kernel(where_am_i, *refs):
     (
         table_ref,
-        outer_ref,
+        inner_ref,
         own_ref,
-        far_ref,
         near_ref,
         faces_ref,
         early_odd_ref,
@@ -275,32 +275,29 @@
         pull_ref,
         side_ref,
         done_ref,
-    ) = refs[-16:]
-
-    def early(column, p):
-        return column * EARLY_PLANES + p - EARLY
+    ) = refs[-15:]
 
     def at(column, p):
-        return column * TILE + p
+        return column * TILE + p - HALF
 
     def load(step, column, p):
         if step == 0:
             base = column * HALF
-            return outer_ref[base + HALF - 1 - p] if p < HALF else own_ref[base + p - HALF]
-        if p >= EARLY + step - 1:
-            return (early_odd_ref if step % 2 else early_even_ref)[early(column, p)]
+            return own_ref[base + p - HALF] if p < TILE else inner_ref[base + 3 * HALF - 1 - p]
+        if p <= EARLY_PLANES + 1 - step:
+            return (early_odd_ref if step % 2 else early_even_ref)[early_at(column, p)]
         return (odd_ref if step % 2 else even_ref)[at(column, p)]
 
     def keep(step, column, p, value):
         (even_ref if step % 2 else odd_ref)[at(column, p)] = value
 
     def signs(column, p):
-        if p >= EARLY:
-            return early_pull_ref, early_side_ref, early(column, p)
+        if p <= EARLY_PLANES:
+            return early_pull_ref, early_side_ref, early_at(column, p)
         return pull_ref, side_ref, at(column, p)
 
-    one_step = stepper(load, keep, signs, lambda p: far_ref if p < HALF else near_ref, faces_ref)
-    in_blocks(where_am_i(refs), one_step, [(s, (0, 1), 1 + s, 5 + s) for s in range(STEPS)])
+    one_step = stepper(load, keep, signs, lambda p: near_ref, faces_ref)
+    in_blocks(where_am_i(refs), one_step, [(s, (0, 1), 7 - s, 11 - s) for s in range(STEPS)])
     lower = iota((ROWS, 128), 1) % WIDE < TILE
     for column in range(2):
         for pair in range(PAIRS):
@@ -427,10 +424,10 @@
     return out
 
 
-def start_march(own, inner, near, me=None):
+def start_march(outer, own, far, near, faces, me=None):
     return run(
         bind(early_kernel, me),
-        (own, inner, near),
+        (outer, own, far, near, faces),
         [((2 * EARLY_PLANES, ROWS, 128), F32)] * 4,
         [],
         me,
@@ -438,14 +435,13 @@
     )
 
 
-def end_march(table, outer, own, far, near, faces, early, me=None):
+def end_march(table, inner, own, near, faces, early, me=None):
     (out,) = run(
         bind(late_kernel, me),
         (
             pltpu.with_memory_space_constraint(table, pltpu.SMEM),
-            outer,
+            inner,
             own,
-            far,
             near,
             faces,
             *early,
@@ -454,7 +450,7 @@
         [pltpu.VMEM((2 * TILE, ROWS, 128), F32)] * 4
         + [pltpu.VMEM((2 * PAIRS * ROWS, 128), F32)],
         me,
-        [pltpu.SMEM] + [pltpu.VMEM] * 9,
+        [pltpu.SMEM] + [pltpu.VMEM] * 8,
     )
     return out.reshape(COLUMNS, BACK, 128)
 
@@ -487,10 +483,10 @@
     far = lax.ppermute(near, ("grp", "mem"), across)
     received, far = lax.optimization_barrier((received, far))
     own = unpack(table, received)
+    outer = lax.ppermute(own, ("grp", "mem"), across)
     inner = lax.ppermute(own, "mem", mates)
-    outer = lax.ppermute(own, ("grp", "mem"), across)
-    early = start_march(own, inner, near)
-    returned = exchange(end_march(table, outer, own, far, near, faces, early))
+    early = start_march(outer, own, far, near, faces)
+    returned = exchange(end_march(table, inner, own, near, faces, early))
     return deliver(band_counts, returned)
 
 

time: 59.8 us -> 58.9 us (0.985)
  waiting for transfers between devices: 7.27 us -> 6.35 us
    ppermute x1, waiting for transfers between devices: 1.63 us -> 0.71 us  [on_device(): outer = lax.ppermute(own, ('grp', 'mem'), across)]
where the time goes in v9:
time: 58.9 us; the launch traced here: 58.5 us
  starting transfers between devices  23.8 us (40%)
  blocking collectives  18.7 us (32%)
  Pallas kernels  8.96 us (15%)
  waiting for transfers between devices  6.35 us (11%)
  local copies, waits for them, and re-layouts  0.65 us (1%)
    all_to_all x1, blocking collectives, exchange(): return lax.all_to_all(x, 'mem', split_axis=0, concat_axis=0, tiled=True)  18.7 us
    all_to_all x1, starting transfers between devices, exchange(): return lax.all_to_all(x, 'mem', split_axis=0, concat_axis=0, tiled=True)  10.9 us
    pallas_call x6, Pallas kernels, run(): pl.pallas_call(kernel, out_shape=[(pltpu.SMEM if space == pltpu.SMEM else...  8.96 us
    ppermute x1, starting transfers between devices, on_device(): far = lax.ppermute(near, ('grp', 'mem'), across)  5.55 us
    ppermute x1, starting transfers between devices, on_device(): outer = lax.ppermute(own, ('grp', 'mem'), across)  5.37 us
    all_to_all x1, waiting for transfers between devices, exchange(): return lax.all_to_all(x, 'mem', split_axis=0, concat_axis=0, tiled=True)  3.41 us
    ppermute x1, waiting for transfers between devices, on_device(): far = lax.ppermute(near, ('grp', 'mem'), across)  2.23 us
    ppermute x1, starting transfers between devices, on_device(): inner = lax.ppermute(own, 'mem', mates)  1.92 us
  transfers between devices with their start and end apart: 4, of which 3 were waited for; matrix products, arithmetic and copies ran while one was open for 0% of the time, Pallas kernels for 7%

profile of v9, /device:TPU:193, one launch (start us, length us, event | category | flops | bytes accessed | tf_op | source)
XLA Modules:
  0.0 58.5 jit_solution(2942453614364191569)
XLA Ops:
  0.0 2.0 %pack_kernel.1 = f32[768,128]{1,0:T(8,128)} custom-call(s32[1,64]{1,0:T(1,128)} %refs_0_.5, f32[512,128]{1,0:T(8,128)} %bitcast.10), custom_call_target="tpu_custom_call" | custom-call | tf_op jit(solution)/shard_map/pack_kernel/pallas_call | solution.py:356
  2.0 0.0 copy-start.1
  2.0 10.9 %all-to-all-start = ((f32[192,4,128]{2,1,0:T(4,128)}), f32[192,4,128]{2,1,0:T(4,128)S(1)}, u32[]{:S(2)}, u32[]{:S(2)}) async-start(f32[192,4,128]{2,1,0:T(4,128)} %bitcast.9), calls=%async_computation | async-start | bytes 786432 | tf_op jit(solution)/shard_map/all_to_all | solution.py:470
  13.0 0.0 copy-done.1
  13.0 0.0 copy-start
  13.0 0.6 %copy-done = s32[1,64]{1,0:T(1,128)S(1)} copy-done((s32[1,64]{1,0:T(1,128)S(1)}, s32[1,64]{1,0:T(1,128)}, u32[]{:S(2)}) %copy-start) | copy-done | bytes 280
  13.7 3.2 %mask_kernel.1 = (f32[4,32,128]{2,1,0:T(8,128)S(1)}, f32[2,32,128]{2,1,0:T(8,128)S(1)}, s32[6,40]{1,0:T(8,128)S(4)}) custom-call(s32[1,64]{1,0:T(1,128)S(1)} %copy-done, s32[1,6,2048]{2,1,0:T(8,128)S(1)} %copy.4.refs_1_), custom_call_target="tpu_custom_call" | custom-call | flops 4194304 | bytes 131072 | tf_op jit(solution)/shard_map/mask_kernel/pallas_call | solution.py:356
  16.9 5.5 %collective-permute-start = (f32[4,32,128]{2,1,0:T(8,128)S(1)}, f32[4,32,128]{2,1,0:T(8,128)S(1)}, u32[]{:S(2)}, u32[]{:S(2)}) collective-permute-start(f32[4,32,128]{2,1,0:T(8,128)S(1)} %get-tuple-element.15.refs_3_), channel_id=1, source_target_pairs={{1,64},{64,1},{3,66},{66,3},{5,68},{68,5},{7,70},{70,7},{9,72},{72... | collective-permute-start | bytes 196616 | tf_op jit(solution)/shard_map/ppermute | solution.py:483
  22.4 2.2 %collective-permute-done.refs_2_ = f32[4,32,128]{2,1,0:T(8,128)S(1)} collective-permute-done((f32[4,32,128]{2,1,0:T(8,128)S(1)}, f32[4,32,128]{2,1,0:T(8,128)S(1)}, u32[]{:S(2)}, u32[]{:S(2)}) %collective-permute-start) | collective-permute-done | bytes 65568 | tf_op jit(solution)/shard_map/ppermute | solution.py:483
  24.6 3.4 %all-to-all-done = f32[192,4,128]{2,1,0:T(4,128)S(1)} async-done(((f32[192,4,128]{2,1,0:T(4,128)}), f32[192,4,128]{2,1,0:T(4,128)S(1)}, u32[]{:S(2)}, u32[]{:S(2)}) %all-to-all-start) | async-done | bytes 393248 | tf_op jit(solution)/shard_map/all_to_all | solution.py:470
  28.1 0.3 unpack_kernel.1.refs_1_.refs_2_
  28.4 5.4 %collective-permute-start.2 = (f32[8,32,128]{2,1,0:T(8,128)S(1)}, f32[8,32,128]{2,1,0:T(8,128)S(1)}, u32[]{:S(2)}, u32[]{:S(2)}) collective-permute-start(f32[8,32,128]{2,1,0:T(8,128)S(1)} %unpack_kernel.1.refs_1_.refs_2_), channel_id=1, source_target_pairs={{1,64},{64,1},{3,66},{66,3},{5,68},{68,5},{7,70},{70,7},{9,72},{72... | collective-permute-start | bytes 393224 | tf_op jit(solution)/shard_map/ppermute | solution.py:486
  33.7 1.9 %collective-permute-start.1 = (f32[8,32,128]{2,1,0:T(8,128)S(1)}, f32[8,32,128]{2,1,0:T(8,128)S(1)}, u32[]{:S(2)}, u32[]{:S(2)}) collective-permute-start(f32[8,32,128]{2,1,0:T(8,128)S(1)} %unpack_kernel.1.refs_1_.refs_2_), channel_id=1, source_target_pairs={{0,1},{1,0},{2,3},{3,2},{4,5},{5,4},{6,7},{7,6},{8,9},{9,8},{10,11... | collective-permute-start | bytes 393224 | tf_op jit(solution)/shard_map/ppermute | solution.py:487
  35.7 0.7 %collective-permute-done.2.refs_0_ = f32[8,32,128]{2,1,0:T(8,128)S(1)} collective-permute-done((f32[8,32,128]{2,1,0:T(8,128)S(1)}, f32[8,32,128]{2,1,0:T(8,128)S(1)}, u32[]{:S(2)}, u32[]{:S(2)}) %collective-permute-start.2) | collective-permute-done | bytes 131104 | tf_op jit(solution)/shard_map/ppermute | solution.py:486
  36.4 1.0 %early_kernel.1 = (f32[12,32,128]{2,1,0:T(8,128)S(1)}, f32[12,32,128]{2,1,0:T(8,128)S(1)}, f32[12,32,128]{2,1,0:T(8,128)S(1)}, f32[12,32,128]{2,1,0:T(8,128)S(1)}) custom-call(f32[8,32,128]{2,1,0:T(8,128)S(1)} %collective-permute-done.2.refs_0_, f32[8,32,128]{2,1,0:T(8,128)S(1)} %unpack_kernel.1.refs_1_.refs_2_, ...), custom_call_target="tpu_custom_call" | custom-call | flops 4194304 | bytes 1048576 | tf_op jit(solution)/shard_map/early_kernel/pallas_call | solution.py:356
  37.4 0.0 collective-permute-done.1.refs_1_
  37.4 1.3 %late_kernel.1 = f32[256,2,128]{2,1,0:T(2,128)S(1)} custom-call(s32[6,40]{1,0:T(8,128)S(4)} %get-tuple-element.14.table_ref.refs_0_, f32[8,32,128]{2,1,0:T(8,128)S(1)} %collective-permute-done.1.refs_1_, f32[8,32,128]{2,1,0:T(8,128)S(1)} %unpack_kernel.1.refs_1_.refs_2_, f32[4,32,128]{2,1,0:T(8,128)S(1)} %get-tuple-element.15.refs_3_, ...), custom_call_target="tpu_custom_call" | custom-call | tf_op jit(solution)/shard_map/late_kernel/pallas_call | solution.py:356
  38.7 18.7 %all_to_all.10 = f32[64,8,128]{2,1,0:T(8,128)S(1)} all-to-all(f32[64,8,128]{2,1,0:T(8,128)S(1)} %bitcast.8), channel_id=1, replica_groups=mesh['grp'=8,'mem'=64] {'mem'}, dimensions={0} | all-to-all | bytes 524288 | tf_op jit(solution)/shard_map/all_to_all | solution.py:470
  57.4 1.2 %deliver_kernel.1 = f32[512,128]{1,0:T(8,128)} custom-call(s32[1,64]{1,0:T(1,128)S(1)} %copy-done, f32[512,128]{1,0:T(8,128)S(1)} %bitcast.7), custom_call_target="tpu_custom_call" | custom-call | tf_op jit(solution)/shard_map/deliver_kernel/pallas_call | solution.py:356
  (1 shorter events, 0.0 us)
Async XLA Ops:
  2.0 11.0 %copy-start.1 = (s32[1,6,2048]{2,0,1:T(1,128)S(1)}, s32[1,6,2048]{2,0,1:T(1,128)}, u32[]{:S(2)}) copy-start(s32[1,6,2048]{2,0,1:T(1,128)} %param.5) | copy-start | bytes 147460
  2.0 26.0 %all-to-all-start = ((f32[192,4,128]{2,1,0:T(4,128)}), f32[192,4,128]{2,1,0:T(4,128)S(1)}, u32[]{:S(2)}, u32[]{:S(2)}) async-start(f32[192,4,128]{2,1,0:T(4,128)} %bitcast.9), calls=%async_computation | async-start | bytes 786432 | tf_op jit(solution)/shard_map/all_to_all | solution.py:470
  13.0 0.7 %copy-start = (s32[1,64]{1,0:T(1,128)S(1)}, s32[1,64]{1,0:T(1,128)}, u32[]{:S(2)}) copy-start(s32[1,64]{1,0:T(1,128)} %refs_0_.5) | copy-start | bytes 772
  16.9 7.8 %collective-permute-start = (f32[4,32,128]{2,1,0:T(8,128)S(1)}, f32[4,32,128]{2,1,0:T(8,128)S(1)}, u32[]{:S(2)}, u32[]{:S(2)}) collective-permute-start(f32[4,32,128]{2,1,0:T(8,128)S(1)} %get-tuple-element.15.refs_3_), channel_id=1, source_target_pairs={{1,64},{64,1},{3,66},{66,3},{5,68},{68,5},{7,70},{70,7},{9,72},{72... | collective-permute-start | bytes 196616 | tf_op jit(solution)/shard_map/ppermute | solution.py:483
  28.4 8.0 %collective-permute-start.2 = (f32[8,32,128]{2,1,0:T(8,128)S(1)}, f32[8,32,128]{2,1,0:T(8,128)S(1)}, u32[]{:S(2)}, u32[]{:S(2)}) collective-permute-start(f32[8,32,128]{2,1,0:T(8,128)S(1)} %unpack_kernel.1.refs_1_.refs_2_), channel_id=1, source_target_pairs={{1,64},{64,1},{3,66},{66,3},{5,68},{68,5},{7,70},{70,7},{9,72},{72... | collective-permute-start | bytes 393224 | tf_op jit(solution)/shard_map/ppermute | solution.py:486
  33.7 3.6 %collective-permute-start.1 = (f32[8,32,128]{2,1,0:T(8,128)S(1)}, f32[8,32,128]{2,1,0:T(8,128)S(1)}, u32[]{:S(2)}, u32[]{:S(2)}) collective-permute-start(f32[8,32,128]{2,1,0:T(8,128)S(1)} %unpack_kernel.1.refs_1_.refs_2_), channel_id=1, source_target_pairs={{0,1},{1,0},{2,3},{3,2},{4,5},{5,4},{6,7},{7,6},{8,9},{9,8},{10,11... | collective-permute-start | bytes 393224 | tf_op jit(solution)/shard_map/ppermute | solution.py:487

commit v10 on v9

--- a/solution.py
+++ b/solution.py
@@ -147,24 +147,29 @@
         )
 
 
-def unpack_kernel(table_ref, received_ref, planes_ref, packed_ref):
+def unpack_kernel(table_ref, received_ref, packed_ref, sides_ref):
+    span = PAIRS * ROWS
     for r in range(ROWS):
         for entry in range(4):
-            packed_ref[pl.ds(entry * PAIRS * ROWS + r, PAIRS, stride=ROWS), :] = received_ref[
+            rows_ref, first = (packed_ref, entry) if entry < 2 else (sides_ref, entry - 2)
+            rows_ref[pl.ds(first * span + r, PAIRS, stride=ROWS), :] = received_ref[
                 table_ref[entry, r + 1]
             ]
-    lane = iota((ROWS, 128), 1)
-    x16 = lane % WIDE
+    upper_x = iota((span, 128), 1) % TILE >= HALF
+    packed_ref[2 * span :, :] = jnp.where(upper_x, sides_ref[:span, :], sides_ref[span:, :])
+
+
+def join_pairs(packed_ref, planes_ref):
+    x16 = iota((ROWS, 128), 1) % WIDE
+
+    def join(left, here, right):
+        return jnp.where(x16 < 4, left, jnp.where(x16 >= 12, right, here))
+
     for pair in range(PAIRS):
-        first, second, left, right = (
+        first, second, outside = (
             packed_ref[(entry * PAIRS + pair) * ROWS : (entry * PAIRS + pair + 1) * ROWS, :]
-            for entry in range(4)
+            for entry in range(3)
         )
-        outside = jnp.where(lane % TILE >= HALF, left, right)
-
-        def join(left, here, right):
-            return jnp.where(x16 < 4, left, jnp.where(x16 >= 12, right, here))
-
         second_4 = shift(second, 4, 1)
         first_m4 = shift(first, -4, 1)
         planes_ref[pair] = join(shift(outside, -4, 1), shift(first, 4, 1), shift(second, 12, 1))
@@ -239,7 +244,22 @@
 
 
 def early_kernel(where_am_i, *refs):
-    outer_ref, own_ref, far_ref, near_ref, faces_ref, odd_ref, even_ref, pull_ref, side_ref = refs[-9:]
+    (
+        outer_packed_ref,
+        own_packed_ref,
+        far_ref,
+        near_ref,
+        faces_ref,
+        own_ref,
+        odd_ref,
+        even_ref,
+        pull_ref,
+        side_ref,
+        outer_ref,
+    ) = refs[-11:]
+    here = where_am_i(refs)
+    pl.when(here > -65)(functools.partial(join_pairs, own_packed_ref, own_ref))
+    pl.when(here > -66)(functools.partial(join_pairs, outer_packed_ref, outer_ref))
 
     def load(step, column, p):
         if step == 0:
@@ -255,13 +275,13 @@
 
     one_step = stepper(load, keep, signs, lambda p: far_ref if p < HALF else near_ref, faces_ref)
     plan = ((0, (0,), 1, 7), (0, (1,), 1, 7), (1, (0, 1), 2, 6), (2, (0, 1), 3, 5))
-    in_blocks(where_am_i(refs), one_step, plan)
+    in_blocks(here, one_step, plan)
 
 
 def late_kernel(where_am_i, *refs):
     (
         table_ref,
-        inner_ref,
+        inner_packed_ref,
         own_ref,
         near_ref,
         faces_ref,
@@ -275,7 +295,10 @@
         pull_ref,
         side_ref,
         done_ref,
-    ) = refs[-15:]
+        inner_ref,
+    ) = refs[-16:]
+    here = where_am_i(refs)
+    pl.when(here > -65)(functools.partial(join_pairs, inner_packed_ref, inner_ref))
 
     def at(column, p):
         return column * TILE + p - HALF
@@ -297,7 +320,7 @@
         return pull_ref, side_ref, at(column, p)
 
     one_step = stepper(load, keep, signs, lambda p: near_ref, faces_ref)
-    in_blocks(where_am_i(refs), one_step, [(s, (0, 1), 7 - s, 11 - s) for s in range(STEPS)])
+    in_blocks(here, one_step, [(s, (0, 1), 7 - s, 11 - s) for s in range(STEPS)])
     lower = iota((ROWS, 128), 1) % WIDE < TILE
     for column in range(2):
         for pair in range(PAIRS):
@@ -416,8 +439,8 @@
     (out,) = run(
         unpack_kernel,
         (pltpu.with_memory_space_constraint(table, pltpu.SMEM), received.reshape(COLUMNS * SENT // PAIRS, PAIRS, 128)),
-        [((TILE, ROWS, 128), F32)],
-        [pltpu.VMEM((4 * PAIRS * ROWS, 128), F32)],
+        [((3 * PAIRS * ROWS, 128), F32)],
+        [pltpu.VMEM((2 * PAIRS * ROWS, 128), F32)],
         None,
         [pltpu.SMEM, pltpu.VMEM],
     )
@@ -428,8 +451,8 @@
     return run(
         bind(early_kernel, me),
         (outer, own, far, near, faces),
-        [((2 * EARLY_PLANES, ROWS, 128), F32)] * 4,
-        [],
+        [((TILE, ROWS, 128), F32)] + [((2 * EARLY_PLANES, ROWS, 128), F32)] * 4,
+        [pltpu.VMEM((TILE, ROWS, 128), F32)],
         me,
         cost=(1 << 22, 1 << 20),
     )
@@ -448,7 +471,7 @@
         ),
         [((COLUMNS * BACK // PAIRS, PAIRS, 128), F32)],
         [pltpu.VMEM((2 * TILE, ROWS, 128), F32)] * 4
-        + [pltpu.VMEM((2 * PAIRS * ROWS, 128), F32)],
+        + [pltpu.VMEM((2 * PAIRS * ROWS, 128), F32), pltpu.VMEM((TILE, ROWS, 128), F32)],
         me,
         [pltpu.SMEM] + [pltpu.VMEM] * 8,
     )
@@ -482,10 +505,10 @@
     near, faces, table = masks_of(band_counts, neighbours)
     far = lax.ppermute(near, ("grp", "mem"), across)
     received, far = lax.optimization_barrier((received, far))
-    own = unpack(table, received)
-    outer = lax.ppermute(own, ("grp", "mem"), across)
-    inner = lax.ppermute(own, "mem", mates)
-    early = start_march(outer, own, far, near, faces)
+    packed = unpack(table, received)
+    outer = lax.ppermute(packed, ("grp", "mem"), across)
+    inner = lax.ppermute(packed, "mem", mates)
+    own, *early = start_march(outer, packed, far, near, faces)
     returned = exchange(end_march(table, inner, own, near, faces, early))
     return deliver(band_counts, returned)
 

time: 58.9 us -> 58.8 us (level)
  transfers between devices with their start and end apart: 4 -> 4, of which waited for: 3 -> 3; matrix products, arithmetic and copies ran while one was open for 0% -> 0% of each run, Pallas kernels for 7% -> 8%
where the time goes in v10:
time: 58.8 us; the launch traced here: 58.5 us
  starting transfers between devices  23.8 us (40%)
  blocking collectives  18.8 us (32%)
  Pallas kernels  9.23 us (16%)
  waiting for transfers between devices  6 us (10%)
  local copies, waits for them, and re-layouts  0.65 us (1%)
    all_to_all x1, blocking collectives, exchange(): return lax.all_to_all(x, 'mem', split_axis=0, concat_axis=0, tiled=True)  18.8 us
    all_to_all x1, starting transfers between devices, exchange(): return lax.all_to_all(x, 'mem', split_axis=0, concat_axis=0, tiled=True)  10.9 us
    pallas_call x6, Pallas kernels, run(): pl.pallas_call(kernel, out_shape=[(pltpu.SMEM if space == pltpu.SMEM else...  9.23 us
    ppermute x1, starting transfers between devices, on_device(): far = lax.ppermute(near, ('grp', 'mem'), across)  5.55 us
    ppermute x1, starting transfers between devices, on_device(): outer = lax.ppermute(packed, ('grp', 'mem'), across)  5.37 us
    all_to_all x1, waiting for transfers between devices, exchange(): return lax.all_to_all(x, 'mem', split_axis=0, concat_axis=0, tiled=True)  3.41 us
    ppermute x1, waiting for transfers between devices, on_device(): far = lax.ppermute(near, ('grp', 'mem'), across)  2.23 us
    ppermute x1, starting transfers between devices, on_device(): inner = lax.ppermute(packed, 'mem', mates)  1.92 us
  transfers between devices with their start and end apart: 4, of which 3 were waited for; matrix products, arithmetic and copies ran while one was open for 0% of the time, Pallas kernels for 8%

profile of v10, /device:TPU:193, one launch (start us, length us, event | category | flops | bytes accessed | tf_op | source)
XLA Modules:
  0.0 58.5 jit_solution(8697789325818475118)
XLA Ops:
  0.0 2.0 %pack_kernel.1 = f32[768,128]{1,0:T(8,128)} custom-call(s32[1,64]{1,0:T(1,128)} %refs_0_.5, f32[512,128]{1,0:T(8,128)} %bitcast.10), custom_call_target="tpu_custom_call" | custom-call | tf_op jit(solution)/shard_map/pack_kernel/pallas_call | solution.py:379
  2.0 0.0 copy-start.1
  2.0 10.9 %all-to-all-start = ((f32[192,4,128]{2,1,0:T(4,128)}), f32[192,4,128]{2,1,0:T(4,128)S(1)}, u32[]{:S(2)}, u32[]{:S(2)}) async-start(f32[192,4,128]{2,1,0:T(4,128)} %bitcast.9), calls=%async_computation | async-start | bytes 786432 | tf_op jit(solution)/shard_map/all_to_all | solution.py:493
  13.0 0.0 copy-done.1
  13.0 0.0 copy-start
  13.0 0.6 %copy-done = s32[1,64]{1,0:T(1,128)S(1)} copy-done((s32[1,64]{1,0:T(1,128)S(1)}, s32[1,64]{1,0:T(1,128)}, u32[]{:S(2)}) %copy-start) | copy-done | bytes 280
  13.7 3.2 %mask_kernel.1 = (f32[4,32,128]{2,1,0:T(8,128)S(1)}, f32[2,32,128]{2,1,0:T(8,128)S(1)}, s32[6,40]{1,0:T(8,128)S(4)}) custom-call(s32[1,64]{1,0:T(1,128)S(1)} %copy-done, s32[1,6,2048]{2,1,0:T(8,128)S(1)} %copy.4.refs_1_), custom_call_target="tpu_custom_call" | custom-call | flops 4194304 | bytes 131072 | tf_op jit(solution)/shard_map/mask_kernel/pallas_call | solution.py:379
  16.9 5.5 %collective-permute-start = (f32[4,32,128]{2,1,0:T(8,128)S(1)}, f32[4,32,128]{2,1,0:T(8,128)S(1)}, u32[]{:S(2)}, u32[]{:S(2)}) collective-permute-start(f32[4,32,128]{2,1,0:T(8,128)S(1)} %get-tuple-element.16.refs_3_), channel_id=1, source_target_pairs={{1,64},{64,1},{3,66},{66,3},{5,68},{68,5},{7,70},{70,7},{9,72},{72... | collective-permute-start | bytes 196616 | tf_op jit(solution)/shard_map/ppermute | solution.py:506
  22.4 2.2 %collective-permute-done.refs_2_ = f32[4,32,128]{2,1,0:T(8,128)S(1)} collective-permute-done((f32[4,32,128]{2,1,0:T(8,128)S(1)}, f32[4,32,128]{2,1,0:T(8,128)S(1)}, u32[]{:S(2)}, u32[]{:S(2)}) %collective-permute-start) | collective-permute-done | bytes 65568 | tf_op jit(solution)/shard_map/ppermute | solution.py:506
  24.6 3.4 %all-to-all-done = f32[192,4,128]{2,1,0:T(4,128)S(1)} async-done(((f32[192,4,128]{2,1,0:T(4,128)}), f32[192,4,128]{2,1,0:T(4,128)S(1)}, u32[]{:S(2)}, u32[]{:S(2)}) %all-to-all-start) | async-done | bytes 393248 | tf_op jit(solution)/shard_map/all_to_all | solution.py:493
  28.1 0.2 unpack_kernel.1.refs_1_
  28.2 5.4 %collective-permute-start.2 = (f32[192,128]{1,0:T(8,128)S(1)}, f32[192,128]{1,0:T(8,128)S(1)}, u32[]{:S(2)}, u32[]{:S(2)}) collective-permute-start(f32[192,128]{1,0:T(8,128)S(1)} %unpack_kernel.1.refs_1_), channel_id=1, source_target_pairs={{1,64},{64,1},{3,66},{66,3},{5,68},{68,5},{7,70},{70,7},{9,72},{72... | collective-permute-start | bytes 294920 | tf_op jit(solution)/shard_map/ppermute | solution.py:509
  33.6 1.9 %collective-permute-start.1 = (f32[192,128]{1,0:T(8,128)S(1)}, f32[192,128]{1,0:T(8,128)S(1)}, u32[]{:S(2)}, u32[]{:S(2)}) collective-permute-start(f32[192,128]{1,0:T(8,128)S(1)} %unpack_kernel.1.refs_1_), channel_id=1, source_target_pairs={{0,1},{1,0},{2,3},{3,2},{4,5},{5,4},{6,7},{7,6},{8,9},{9,8},{10,11... | collective-permute-start | bytes 294920 | tf_op jit(solution)/shard_map/ppermute | solution.py:510
  35.5 0.4 collective-permute-done.2.refs_0_
  35.9 1.3 %early_kernel.1 = (f32[8,32,128]{2,1,0:T(8,128)S(1)}, f32[12,32,128]{2,1,0:T(8,128)S(1)}, f32[12,32,128]{2,1,0:T(8,128)S(1)}, f32[12,32,128]{2,1,0:T(8,128)S(1)}, f32[12,32,128]{2,1,0:T(8,128)S(1)}) custom-call(f32[192,128]{1,0:T(8,128)S(1)} %collective-permute-done.2.refs_0_, f32[192,128]{1,0:T(8,128)S(1)} %unpack_kernel.1.refs_1_, ...), custom_call_target="tpu_custom_call" | custom-call | flops 4194304 | bytes 1048576 | tf_op jit(solution)/shard_map/early_kernel/pallas_call | solution.py:379
  37.1 0.0 collective-permute-done.1.refs_1_
  37.2 1.4 %late_kernel.1 = f32[256,2,128]{2,1,0:T(2,128)S(1)} custom-call(s32[6,40]{1,0:T(8,128)S(4)} %get-tuple-element.15.table_ref.refs_0_, f32[192,128]{1,0:T(8,128)S(1)} %collective-permute-done.1.refs_1_, f32[8,32,128]{2,1,0:T(8,128)S(1)} %get-tuple-element.20.refs_2_, f32[4,32,128]{2,1,0:T(8,128)S(1)} %get-tuple-element.16.refs_3_, ...), custom_call_target="tpu_custom_call" | custom-call | tf_op jit(solution)/shard_map/late_kernel/pallas_call | solution.py:379
  38.6 18.8 %all_to_all.10 = f32[64,8,128]{2,1,0:T(8,128)S(1)} all-to-all(f32[64,8,128]{2,1,0:T(8,128)S(1)} %bitcast.8), channel_id=1, replica_groups=mesh['grp'=8,'mem'=64] {'mem'}, dimensions={0} | all-to-all | bytes 524288 | tf_op jit(solution)/shard_map/all_to_all | solution.py:493
  57.3 1.2 %deliver_kernel.1 = f32[512,128]{1,0:T(8,128)} custom-call(s32[1,64]{1,0:T(1,128)S(1)} %copy-done, f32[512,128]{1,0:T(8,128)S(1)} %bitcast.7), custom_call_target="tpu_custom_call" | custom-call | tf_op jit(solution)/shard_map/deliver_kernel/pallas_call | solution.py:379
  (1 shorter events, 0.0 us)
Async XLA Ops:
  2.0 11.0 %copy-start.1 = (s32[1,6,2048]{2,0,1:T(1,128)S(1)}, s32[1,6,2048]{2,0,1:T(1,128)}, u32[]{:S(2)}) copy-start(s32[1,6,2048]{2,0,1:T(1,128)} %param.5) | copy-start | bytes 147460
  2.0 26.0 %all-to-all-start = ((f32[192,4,128]{2,1,0:T(4,128)}), f32[192,4,128]{2,1,0:T(4,128)S(1)}, u32[]{:S(2)}, u32[]{:S(2)}) async-start(f32[192,4,128]{2,1,0:T(4,128)} %bitcast.9), calls=%async_computation | async-start | bytes 786432 | tf_op jit(solution)/shard_map/all_to_all | solution.py:493
  13.0 0.7 %copy-start = (s32[1,64]{1,0:T(1,128)S(1)}, s32[1,64]{1,0:T(1,128)}, u32[]{:S(2)}) copy-start(s32[1,64]{1,0:T(1,128)} %refs_0_.5) | copy-start | bytes 772
  16.9 7.8 %collective-permute-start = (f32[4,32,128]{2,1,0:T(8,128)S(1)}, f32[4,32,128]{2,1,0:T(8,128)S(1)}, u32[]{:S(2)}, u32[]{:S(2)}) collective-permute-start(f32[4,32,128]{2,1,0:T(8,128)S(1)} %get-tuple-element.16.refs_3_), channel_id=1, source_target_pairs={{1,64},{64,1},{3,66},{66,3},{5,68},{68,5},{7,70},{70,7},{9,72},{72... | collective-permute-start | bytes 196616 | tf_op jit(solution)/shard_map/ppermute | solution.py:506
  28.2 7.7 %collective-permute-start.2 = (f32[192,128]{1,0:T(8,128)S(1)}, f32[192,128]{1,0:T(8,128)S(1)}, u32[]{:S(2)}, u32[]{:S(2)}) collective-permute-start(f32[192,128]{1,0:T(8,128)S(1)} %unpack_kernel.1.refs_1_), channel_id=1, source_target_pairs={{1,64},{64,1},{3,66},{66,3},{5,68},{68,5},{7,70},{70,7},{9,72},{72... | collective-permute-start | bytes 294920 | tf_op jit(solution)/shard_map/ppermute | solution.py:509
  33.6 3.6 %collective-permute-start.1 = (f32[192,128]{1,0:T(8,128)S(1)}, f32[192,128]{1,0:T(8,128)S(1)}, u32[]{:S(2)}, u32[]{:S(2)}) collective-permute-start(f32[192,128]{1,0:T(8,128)S(1)} %unpack_kernel.1.refs_1_), channel_id=1, source_target_pairs={{0,1},{1,0},{2,3},{3,2},{4,5},{5,4},{6,7},{7,6},{8,9},{9,8},{10,11... | collective-permute-start | bytes 294920 | tf_op jit(solution)/shard_map/ppermute | solution.py:510

commit v11 on v9

--- a/solution.py
+++ b/solution.py
@@ -178,7 +178,7 @@
 EARLY_PLANES = TILE - 2
 
 
-def stepper(load, keep, signs, links, faces_ref):
+def stepper(load, keep, signs, links, lags, faces_ref):
     lane = iota((ROWS, 128), 1)
     first_y = lane < WIDE
     last_y = lane >= 128 - WIDE
@@ -208,7 +208,7 @@
                 up = side_ref[at]
             down = -up
             ahead = (shift(level, -1, 1) - level) * links(p)[column]
-            back = shift(ahead, 1, 1)
+            back = (level - shift(level, 1, 1)) * lags(p, column)
             squares = jnp.square(jnp.maximum(jnp.maximum(up * back, down * ahead), 0.0))
             beyond = jnp.where(first_y, shift(level, -1, 0), level)
             ahead = (shift(beyond, -WIDE, 1) - level) * links(p)[2 + column]
@@ -239,7 +239,21 @@
 
 
 def early_kernel(where_am_i, *refs):
-    outer_ref, own_ref, far_ref, near_ref, faces_ref, odd_ref, even_ref, pull_ref, side_ref = refs[-9:]
+    (
+        outer_ref,
+        own_ref,
+        far_ref,
+        near_ref,
+        faces_ref,
+        odd_ref,
+        even_ref,
+        pull_ref,
+        side_ref,
+        lag_ref,
+    ) = refs[-10:]
+    for column in range(2):
+        lag_ref[column] = shift(far_ref[column], 1, 1)
+        lag_ref[2 + column] = shift(near_ref[column], 1, 1)
 
     def load(step, column, p):
         if step == 0:
@@ -253,7 +267,13 @@
     def signs(column, p):
         return pull_ref, side_ref, early_at(column, p)
 
-    one_step = stepper(load, keep, signs, lambda p: far_ref if p < HALF else near_ref, faces_ref)
+    def links(p):
+        return far_ref if p < HALF else near_ref
+
+    def lags(p, column):
+        return lag_ref[column if p < HALF else 2 + column]
+
+    one_step = stepper(load, keep, signs, links, lags, faces_ref)
     plan = ((0, (0,), 1, 7), (0, (1,), 1, 7), (1, (0, 1), 2, 6), (2, (0, 1), 3, 5))
     in_blocks(where_am_i(refs), one_step, plan)
 
@@ -275,7 +295,10 @@
         pull_ref,
         side_ref,
         done_ref,
-    ) = refs[-15:]
+        lag_ref,
+    ) = refs[-16:]
+    for column in range(2):
+        lag_ref[column] = shift(near_ref[column], 1, 1)
 
     def at(column, p):
         return column * TILE + p - HALF
@@ -296,7 +319,9 @@
             return early_pull_ref, early_side_ref, early_at(column, p)
         return pull_ref, side_ref, at(column, p)
 
-    one_step = stepper(load, keep, signs, lambda p: near_ref, faces_ref)
+    one_step = stepper(
+        load, keep, signs, lambda p: near_ref, lambda p, column: lag_ref[column], faces_ref
+    )
     in_blocks(where_am_i(refs), one_step, [(s, (0, 1), 7 - s, 11 - s) for s in range(STEPS)])
     lower = iota((ROWS, 128), 1) % WIDE < TILE
     for column in range(2):
@@ -314,13 +339,14 @@
 
 
 def deliver_kernel(where_am_i, *refs):
-    counts_ref, returned_ref, out_ref, turned_ref = refs[-4:]
+    counts_ref, returned_ref, out_hbm, turned_ref, planes_ref, sems = refs[-6:]
     me = where_am_i(refs)
     counts = counts_ref[...]
     owner = iota((1, COLUMNS), 1)
     turn = jnp.sum(jnp.where(owner < me, counts, 0)) & (COLUMNS - 1)
     live = iota((SLOTS, SLOTS), 1) < jnp.sum(jnp.where(owner == me, counts, 0))
     chips = COLUMNS // 2
+    sends = []
     for core in range(2):
         for pair in range(PAIRS):
             held_ref = turned_ref.at[core * PAIRS + pair]
@@ -336,9 +362,13 @@
                 for upper in range(2):
                     row = y * WIDE + upper * TILE
                     z = plane_of(core, pair, upper)
-                    out_ref[pl.ds(y * TILE + z, TILE, stride=TILE * TILE), :] = turned[
-                        row : row + TILE
-                    ]
+                    planes_ref[z, pl.ds(y, TILE, stride=TILE), :] = turned[row : row + TILE]
+            for upper in range(2):
+                z = plane_of(core, pair, upper)
+                sends.append(pltpu.make_async_copy(planes_ref.at[z], out_hbm.at[:, z], sems.at[z]))
+                sends[-1].start()
+    for send in sends:
+        send.wait()
 
 
 def spec(space=pltpu.VMEM):
@@ -429,7 +459,7 @@
         bind(early_kernel, me),
         (outer, own, far, near, faces),
         [((2 * EARLY_PLANES, ROWS, 128), F32)] * 4,
-        [],
+        [pltpu.VMEM((4, ROWS, 128), F32)],
         me,
         cost=(1 << 22, 1 << 20),
     )
@@ -448,7 +478,7 @@
         ),
         [((COLUMNS * BACK // PAIRS, PAIRS, 128), F32)],
         [pltpu.VMEM((2 * TILE, ROWS, 128), F32)] * 4
-        + [pltpu.VMEM((2 * PAIRS * ROWS, 128), F32)],
+        + [pltpu.VMEM((2 * PAIRS * ROWS, 128), F32), pltpu.VMEM((2, ROWS, 128), F32)],
         me,
         [pltpu.SMEM] + [pltpu.VMEM] * 8,
     )
@@ -459,9 +489,15 @@
     (out,) = run(
         bind(deliver_kernel, me),
         (counts, returned.reshape(COLUMNS * BACK, 128)),
-        [((CELLS, SLOTS), F32)],
-        [pltpu.VMEM((2 * PAIRS, SLOTS, 128), F32)],
+        [((TILE * TILE, TILE, SLOTS), F32)],
+        [
+            pltpu.VMEM((2 * PAIRS, SLOTS, 128), F32),
+            pltpu.VMEM((TILE, TILE * TILE, SLOTS), F32),
+            pltpu.SemaphoreType.DMA((TILE,)),
+        ],
         me,
+        None,
+        [pltpu.HBM],
     )
     return out.reshape(TILE, TILE, TILE, SLOTS)
 

time: 58.9 us -> 58.8 us (level)
  no operation moved by 1% of the time
where the time goes in v11:
time: 58.8 us; the launch traced here: 58.5 us
  starting transfers between devices  23.8 us (40%)
  blocking collectives  18.7 us (32%)
  Pallas kernels  8.94 us (15%)
  waiting for transfers between devices  6.35 us (11%)
  local copies, waits for them, and re-layouts  0.65 us (1%)
    all_to_all x1, blocking collectives, exchange(): return lax.all_to_all(x, 'mem', split_axis=0, concat_axis=0, tiled=True)  18.7 us
    all_to_all x1, starting transfers between devices, exchange(): return lax.all_to_all(x, 'mem', split_axis=0, concat_axis=0, tiled=True)  10.9 us
    pallas_call x6, Pallas kernels, run(): pl.pallas_call(kernel, out_shape=[(pltpu.SMEM if space == pltpu.SMEM else...  8.94 us
    ppermute x1, starting transfers between devices, on_device(): far = lax.ppermute(near, ('grp', 'mem'), across)  5.55 us
    ppermute x1, starting transfers between devices, on_device(): outer = lax.ppermute(own, ('grp', 'mem'), across)  5.37 us
    all_to_all x1, waiting for transfers between devices, exchange(): return lax.all_to_all(x, 'mem', split_axis=0, concat_axis=0, tiled=True)  3.41 us
    ppermute x1, waiting for transfers between devices, on_device(): far = lax.ppermute(near, ('grp', 'mem'), across)  2.23 us
    ppermute x1, starting transfers between devices, on_device(): inner = lax.ppermute(own, 'mem', mates)  1.92 us
  transfers between devices with their start and end apart: 4, of which 3 were waited for; matrix products, arithmetic and copies ran while one was open for 0% of the time, Pallas kernels for 7%

profile of v11, /device:TPU:193, one launch (start us, length us, event | category | flops | bytes accessed | tf_op | source)
XLA Modules:
  0.0 58.5 jit_solution(1692167609705049369)
XLA Ops:
  0.0 2.0 %pack_kernel.1 = f32[768,128]{1,0:T(8,128)} custom-call(s32[1,64]{1,0:T(1,128)} %refs_0_.5, f32[512,128]{1,0:T(8,128)} %bitcast.10), custom_call_target="tpu_custom_call" | custom-call | tf_op jit(solution)/shard_map/pack_kernel/pallas_call | solution.py:386
  2.0 0.0 copy-start.1
  2.0 10.9 %all-to-all-start = ((f32[192,4,128]{2,1,0:T(4,128)}), f32[192,4,128]{2,1,0:T(4,128)S(1)}, u32[]{:S(2)}, u32[]{:S(2)}) async-start(f32[192,4,128]{2,1,0:T(4,128)} %bitcast.9), calls=%async_computation | async-start | bytes 786432 | tf_op jit(solution)/shard_map/all_to_all | solution.py:506
  13.0 0.0 copy-done.1
  13.0 0.0 copy-start
  13.0 0.6 %copy-done = s32[1,64]{1,0:T(1,128)S(1)} copy-done((s32[1,64]{1,0:T(1,128)S(1)}, s32[1,64]{1,0:T(1,128)}, u32[]{:S(2)}) %copy-start) | copy-done | bytes 280
  13.7 3.2 %mask_kernel.1 = (f32[4,32,128]{2,1,0:T(8,128)S(1)}, f32[2,32,128]{2,1,0:T(8,128)S(1)}, s32[6,40]{1,0:T(8,128)S(4)}) custom-call(s32[1,64]{1,0:T(1,128)S(1)} %copy-done, s32[1,6,2048]{2,1,0:T(8,128)S(1)} %copy.4.refs_1_), custom_call_target="tpu_custom_call" | custom-call | flops 4194304 | bytes 131072 | tf_op jit(solution)/shard_map/mask_kernel/pallas_call | solution.py:386
  16.9 5.5 %collective-permute-start = (f32[4,32,128]{2,1,0:T(8,128)S(1)}, f32[4,32,128]{2,1,0:T(8,128)S(1)}, u32[]{:S(2)}, u32[]{:S(2)}) collective-permute-start(f32[4,32,128]{2,1,0:T(8,128)S(1)} %get-tuple-element.15.refs_3_), channel_id=1, source_target_pairs={{1,64},{64,1},{3,66},{66,3},{5,68},{68,5},{7,70},{70,7},{9,72},{72... | collective-permute-start | bytes 196616 | tf_op jit(solution)/shard_map/ppermute | solution.py:519
  22.4 2.2 %collective-permute-done.refs_2_ = f32[4,32,128]{2,1,0:T(8,128)S(1)} collective-permute-done((f32[4,32,128]{2,1,0:T(8,128)S(1)}, f32[4,32,128]{2,1,0:T(8,128)S(1)}, u32[]{:S(2)}, u32[]{:S(2)}) %collective-permute-start) | collective-permute-done | bytes 65568 | tf_op jit(solution)/shard_map/ppermute | solution.py:519
  24.6 3.4 %all-to-all-done = f32[192,4,128]{2,1,0:T(4,128)S(1)} async-done(((f32[192,4,128]{2,1,0:T(4,128)}), f32[192,4,128]{2,1,0:T(4,128)S(1)}, u32[]{:S(2)}, u32[]{:S(2)}) %all-to-all-start) | async-done | bytes 393248 | tf_op jit(solution)/shard_map/all_to_all | solution.py:506
  28.1 0.3 unpack_kernel.1.refs_1_.refs_2_
  28.4 5.4 %collective-permute-start.2 = (f32[8,32,128]{2,1,0:T(8,128)S(1)}, f32[8,32,128]{2,1,0:T(8,128)S(1)}, u32[]{:S(2)}, u32[]{:S(2)}) collective-permute-start(f32[8,32,128]{2,1,0:T(8,128)S(1)} %unpack_kernel.1.refs_1_.refs_2_), channel_id=1, source_target_pairs={{1,64},{64,1},{3,66},{66,3},{5,68},{68,5},{7,70},{70,7},{9,72},{72... | collective-permute-start | bytes 393224 | tf_op jit(solution)/shard_map/ppermute | solution.py:522
  33.7 1.9 %collective-permute-start.1 = (f32[8,32,128]{2,1,0:T(8,128)S(1)}, f32[8,32,128]{2,1,0:T(8,128)S(1)}, u32[]{:S(2)}, u32[]{:S(2)}) collective-permute-start(f32[8,32,128]{2,1,0:T(8,128)S(1)} %unpack_kernel.1.refs_1_.refs_2_), channel_id=1, source_target_pairs={{0,1},{1,0},{2,3},{3,2},{4,5},{5,4},{6,7},{7,6},{8,9},{9,8},{10,11... | collective-permute-start | bytes 393224 | tf_op jit(solution)/shard_map/ppermute | solution.py:523
  35.7 0.7 %collective-permute-done.2.refs_0_ = f32[8,32,128]{2,1,0:T(8,128)S(1)} collective-permute-done((f32[8,32,128]{2,1,0:T(8,128)S(1)}, f32[8,32,128]{2,1,0:T(8,128)S(1)}, u32[]{:S(2)}, u32[]{:S(2)}) %collective-permute-start.2) | collective-permute-done | bytes 131104 | tf_op jit(solution)/shard_map/ppermute | solution.py:522
  36.4 1.0 %early_kernel.1 = (f32[12,32,128]{2,1,0:T(8,128)S(1)}, f32[12,32,128]{2,1,0:T(8,128)S(1)}, f32[12,32,128]{2,1,0:T(8,128)S(1)}, f32[12,32,128]{2,1,0:T(8,128)S(1)}) custom-call(f32[8,32,128]{2,1,0:T(8,128)S(1)} %collective-permute-done.2.refs_0_, f32[8,32,128]{2,1,0:T(8,128)S(1)} %unpack_kernel.1.refs_1_.refs_2_, ...), custom_call_target="tpu_custom_call" | custom-call | flops 4194304 | bytes 1048576 | tf_op jit(solution)/shard_map/early_kernel/pallas_call | solution.py:386
  37.4 0.0 collective-permute-done.1.refs_1_
  37.4 1.3 %late_kernel.1 = f32[256,2,128]{2,1,0:T(2,128)S(1)} custom-call(s32[6,40]{1,0:T(8,128)S(4)} %get-tuple-element.14.table_ref.refs_0_, f32[8,32,128]{2,1,0:T(8,128)S(1)} %collective-permute-done.1.refs_1_, f32[8,32,128]{2,1,0:T(8,128)S(1)} %unpack_kernel.1.refs_1_.refs_2_, f32[4,32,128]{2,1,0:T(8,128)S(1)} %get-tuple-element.15.refs_3_, ...), custom_call_target="tpu_custom_call" | custom-call | tf_op jit(solution)/shard_map/late_kernel/pallas_call | solution.py:386
  38.7 18.7 %all_to_all.10 = f32[64,8,128]{2,1,0:T(8,128)S(1)} all-to-all(f32[64,8,128]{2,1,0:T(8,128)S(1)} %bitcast.8), channel_id=1, replica_groups=mesh['grp'=8,'mem'=64] {'mem'}, dimensions={0} | all-to-all | bytes 524288 | tf_op jit(solution)/shard_map/all_to_all | solution.py:506
  57.4 1.1 %deliver_kernel.1 = f32[64,8,128]{2,1,0:T(8,128)} custom-call(s32[1,64]{1,0:T(1,128)S(1)} %copy-done, f32[512,128]{1,0:T(8,128)S(1)} %bitcast.7), custom_call_target="tpu_custom_call" | custom-call | tf_op jit(solution)/shard_map/deliver_kernel/pallas_call | solution.py:386
  (1 shorter events, 0.0 us)
Async XLA Ops:
  2.0 11.0 %copy-start.1 = (s32[1,6,2048]{2,0,1:T(1,128)S(1)}, s32[1,6,2048]{2,0,1:T(1,128)}, u32[]{:S(2)}) copy-start(s32[1,6,2048]{2,0,1:T(1,128)} %param.5) | copy-start | bytes 147460
  2.0 26.0 %all-to-all-start = ((f32[192,4,128]{2,1,0:T(4,128)}), f32[192,4,128]{2,1,0:T(4,128)S(1)}, u32[]{:S(2)}, u32[]{:S(2)}) async-start(f32[192,4,128]{2,1,0:T(4,128)} %bitcast.9), calls=%async_computation | async-start | bytes 786432 | tf_op jit(solution)/shard_map/all_to_all | solution.py:506
  13.0 0.7 %copy-start = (s32[1,64]{1,0:T(1,128)S(1)}, s32[1,64]{1,0:T(1,128)}, u32[]{:S(2)}) copy-start(s32[1,64]{1,0:T(1,128)} %refs_0_.5) | copy-start | bytes 772
  16.9 7.8 %collective-permute-start = (f32[4,32,128]{2,1,0:T(8,128)S(1)}, f32[4,32,128]{2,1,0:T(8,128)S(1)}, u32[]{:S(2)}, u32[]{:S(2)}) collective-permute-start(f32[4,32,128]{2,1,0:T(8,128)S(1)} %get-tuple-element.15.refs_3_), channel_id=1, source_target_pairs={{1,64},{64,1},{3,66},{66,3},{5,68},{68,5},{7,70},{70,7},{9,72},{72... | collective-permute-start | bytes 196616 | tf_op jit(solution)/shard_map/ppermute | solution.py:519
  28.4 8.0 %collective-permute-start.2 = (f32[8,32,128]{2,1,0:T(8,128)S(1)}, f32[8,32,128]{2,1,0:T(8,128)S(1)}, u32[]{:S(2)}, u32[]{:S(2)}) collective-permute-start(f32[8,32,128]{2,1,0:T(8,128)S(1)} %unpack_kernel.1.refs_1_.refs_2_), channel_id=1, source_target_pairs={{1,64},{64,1},{3,66},{66,3},{5,68},{68,5},{7,70},{70,7},{9,72},{72... | collective-permute-start | bytes 393224 | tf_op jit(solution)/shard_map/ppermute | solution.py:522
  33.7 3.6 %collective-permute-start.1 = (f32[8,32,128]{2,1,0:T(8,128)S(1)}, f32[8,32,128]{2,1,0:T(8,128)S(1)}, u32[]{:S(2)}, u32[]{:S(2)}) collective-permute-start(f32[8,32,128]{2,1,0:T(8,128)S(1)} %unpack_kernel.1.refs_1_.refs_2_), channel_id=1, source_target_pairs={{0,1},{1,0},{2,3},{3,2},{4,5},{5,4},{6,7},{7,6},{8,9},{9,8},{10,11... | collective-permute-start | bytes 393224 | tf_op jit(solution)/shard_map/ppermute | solution.py:523

commit v12 on v10

--- a/solution.py
+++ b/solution.py
@@ -246,20 +246,18 @@
 def early_kernel(where_am_i, *refs):
     (
         outer_packed_ref,
-        own_packed_ref,
+        own_ref,
         far_ref,
         near_ref,
         faces_ref,
-        own_ref,
         odd_ref,
         even_ref,
         pull_ref,
         side_ref,
         outer_ref,
-    ) = refs[-11:]
+    ) = refs[-10:]
     here = where_am_i(refs)
-    pl.when(here > -65)(functools.partial(join_pairs, own_packed_ref, own_ref))
-    pl.when(here > -66)(functools.partial(join_pairs, outer_packed_ref, outer_ref))
+    pl.when(here > -65)(functools.partial(join_pairs, outer_packed_ref, outer_ref))
 
     def load(step, column, p):
         if step == 0:
@@ -447,11 +445,15 @@
     return out
 
 
+def joined(packed):
+    return run(join_pairs, (packed,), [((TILE, ROWS, 128), F32)], [], cost=(1 << 20, 1 << 18))[0]
+
+
 def start_march(outer, own, far, near, faces, me=None):
     return run(
         bind(early_kernel, me),
         (outer, own, far, near, faces),
-        [((TILE, ROWS, 128), F32)] + [((2 * EARLY_PLANES, ROWS, 128), F32)] * 4,
+        [((2 * EARLY_PLANES, ROWS, 128), F32)] * 4,
         [pltpu.VMEM((TILE, ROWS, 128), F32)],
         me,
         cost=(1 << 22, 1 << 20),
@@ -508,7 +510,8 @@
     packed = unpack(table, received)
     outer = lax.ppermute(packed, ("grp", "mem"), across)
     inner = lax.ppermute(packed, "mem", mates)
-    own, *early = start_march(outer, packed, far, near, faces)
+    own = joined(packed)
+    early = start_march(outer, own, far, near, faces)
     returned = exchange(end_march(table, inner, own, near, faces, early))
     return deliver(band_counts, returned)
 

time: 58.8 us -> 58.8 us (level)
    pallas_call x6 -> x7, Pallas kernels: 9.23 us -> 9.25 us  [run(): pl.pallas_call(kernel, out_shape=[(pltpu.SMEM if space == pltpu.SMEM else...]
where the time goes in v12:
time: 58.8 us; the launch traced here: 58.5 us
  starting transfers between devices  23.8 us (40%)
  blocking collectives  18.9 us (32%)
  Pallas kernels  9.25 us (16%)
  waiting for transfers between devices  5.84 us (10%)
  local copies, waits for them, and re-layouts  0.65 us (1%)
    all_to_all x1, blocking collectives, exchange(): return lax.all_to_all(x, 'mem', split_axis=0, concat_axis=0, tiled=True)  18.9 us
    all_to_all x1, starting transfers between devices, exchange(): return lax.all_to_all(x, 'mem', split_axis=0, concat_axis=0, tiled=True)  10.9 us
    pallas_call x7, Pallas kernels, run(): pl.pallas_call(kernel, out_shape=[(pltpu.SMEM if space == pltpu.SMEM else...  9.25 us
    ppermute x1, starting transfers between devices, on_device(): far = lax.ppermute(near, ('grp', 'mem'), across)  5.55 us
    ppermute x1, starting transfers between devices, on_device(): outer = lax.ppermute(packed, ('grp', 'mem'), across)  5.37 us
    all_to_all x1, waiting for transfers between devices, exchange(): return lax.all_to_all(x, 'mem', split_axis=0, concat_axis=0, tiled=True)  3.41 us
    ppermute x1, waiting for transfers between devices, on_device(): far = lax.ppermute(near, ('grp', 'mem'), across)  2.23 us
    ppermute x1, starting transfers between devices, on_device(): inner = lax.ppermute(packed, 'mem', mates)  1.92 us
  transfers between devices with their start and end apart: 4, of which 3 were waited for; matrix products, arithmetic and copies ran while one was open for 0% of the time, Pallas kernels for 8%

profile of v12, /device:TPU:193, one launch (start us, length us, event | category | flops | bytes accessed | tf_op | source)
XLA Modules:
  0.0 58.5 jit_solution(2761747672712632188)
XLA Ops:
  0.0 2.0 %pack_kernel.1 = f32[768,128]{1,0:T(8,128)} custom-call(s32[1,64]{1,0:T(1,128)} %refs_0_.5, f32[512,128]{1,0:T(8,128)} %bitcast.10), custom_call_target="tpu_custom_call" | custom-call | tf_op jit(solution)/shard_map/pack_kernel/pallas_call | solution.py:377
  2.0 0.0 copy-start.1
  2.0 10.9 %all-to-all-start = ((f32[192,4,128]{2,1,0:T(4,128)}), f32[192,4,128]{2,1,0:T(4,128)S(1)}, u32[]{:S(2)}, u32[]{:S(2)}) async-start(f32[192,4,128]{2,1,0:T(4,128)} %bitcast.9), calls=%async_computation | async-start | bytes 786432 | tf_op jit(solution)/shard_map/all_to_all | solution.py:495
  13.0 0.0 copy-done.1
  13.0 0.0 copy-start
  13.0 0.6 %copy-done = s32[1,64]{1,0:T(1,128)S(1)} copy-done((s32[1,64]{1,0:T(1,128)S(1)}, s32[1,64]{1,0:T(1,128)}, u32[]{:S(2)}) %copy-start) | copy-done | bytes 280
  13.7 3.2 %mask_kernel.1 = (f32[4,32,128]{2,1,0:T(8,128)S(1)}, f32[2,32,128]{2,1,0:T(8,128)S(1)}, s32[6,40]{1,0:T(8,128)S(4)}) custom-call(s32[1,64]{1,0:T(1,128)S(1)} %copy-done, s32[1,6,2048]{2,1,0:T(8,128)S(1)} %copy.4.refs_1_), custom_call_target="tpu_custom_call" | custom-call | flops 4194304 | bytes 131072 | tf_op jit(solution)/shard_map/mask_kernel/pallas_call | solution.py:377
  16.9 5.5 %collective-permute-start = (f32[4,32,128]{2,1,0:T(8,128)S(1)}, f32[4,32,128]{2,1,0:T(8,128)S(1)}, u32[]{:S(2)}, u32[]{:S(2)}) collective-permute-start(f32[4,32,128]{2,1,0:T(8,128)S(1)} %get-tuple-element.15.refs_3_), channel_id=1, source_target_pairs={{1,64},{64,1},{3,66},{66,3},{5,68},{68,5},{7,70},{70,7},{9,72},{72... | collective-permute-start | bytes 196616 | tf_op jit(solution)/shard_map/ppermute | solution.py:508
  22.4 2.2 %collective-permute-done.refs_2_ = f32[4,32,128]{2,1,0:T(8,128)S(1)} collective-permute-done((f32[4,32,128]{2,1,0:T(8,128)S(1)}, f32[4,32,128]{2,1,0:T(8,128)S(1)}, u32[]{:S(2)}, u32[]{:S(2)}) %collective-permute-start) | collective-permute-done | bytes 65568 | tf_op jit(solution)/shard_map/ppermute | solution.py:508
  24.6 3.4 %all-to-all-done = f32[192,4,128]{2,1,0:T(4,128)S(1)} async-done(((f32[192,4,128]{2,1,0:T(4,128)}), f32[192,4,128]{2,1,0:T(4,128)S(1)}, u32[]{:S(2)}, u32[]{:S(2)}) %all-to-all-start) | async-done | bytes 393248 | tf_op jit(solution)/shard_map/all_to_all | solution.py:495
  28.1 0.2 unpack_kernel.1.packed_ref
  28.2 5.4 %collective-permute-start.2 = (f32[192,128]{1,0:T(8,128)S(1)}, f32[192,128]{1,0:T(8,128)S(1)}, u32[]{:S(2)}, u32[]{:S(2)}) collective-permute-start(f32[192,128]{1,0:T(8,128)S(1)} %unpack_kernel.1.packed_ref), channel_id=1, source_target_pairs={{1,64},{64,1},{3,66},{66,3},{5,68},{68,5},{7,70},{70,7},{9,72},{72... | collective-permute-start | bytes 294920 | tf_op jit(solution)/shard_map/ppermute | solution.py:511
  33.6 1.9 %collective-permute-start.1 = (f32[192,128]{1,0:T(8,128)S(1)}, f32[192,128]{1,0:T(8,128)S(1)}, u32[]{:S(2)}, u32[]{:S(2)}) collective-permute-start(f32[192,128]{1,0:T(8,128)S(1)} %unpack_kernel.1.packed_ref), channel_id=1, source_target_pairs={{0,1},{1,0},{2,3},{3,2},{4,5},{5,4},{6,7},{7,6},{8,9},{9,8},{10,11... | collective-permute-start | bytes 294920 | tf_op jit(solution)/shard_map/ppermute | solution.py:512
  35.5 0.1 join_pairs.1.refs_1_.refs_2_
  35.7 0.2 collective-permute-done.2.refs_0_
  35.9 1.1 %early_kernel.1 = (f32[12,32,128]{2,1,0:T(8,128)S(1)}, f32[12,32,128]{2,1,0:T(8,128)S(1)}, f32[12,32,128]{2,1,0:T(8,128)S(1)}, f32[12,32,128]{2,1,0:T(8,128)S(1)}) custom-call(f32[192,128]{1,0:T(8,128)S(1)} %collective-permute-done.2.refs_0_, f32[8,32,128]{2,1,0:T(8,128)S(1)} %join_pairs.1.refs_1_.refs_2_, f32[4,32,128]{2,1,0:T(8,128)S(1)} %collective-permute-done.refs_2_, ...), custom_call_target="tpu_custom_call" | custom-call | flops 4194304 | bytes 1048576 | tf_op jit(solution)/shard_map/early_kernel/pallas_call | solution.py:377
  37.0 0.0 collective-permute-done.1.refs_1_
  37.0 1.4 %late_kernel.1 = f32[256,2,128]{2,1,0:T(2,128)S(1)} custom-call(s32[6,40]{1,0:T(8,128)S(4)} %get-tuple-element.14.table_ref.refs_0_, f32[192,128]{1,0:T(8,128)S(1)} %collective-permute-done.1.refs_1_, f32[8,32,128]{2,1,0:T(8,128)S(1)} %join_pairs.1.refs_1_.refs_2_, f32[4,32,128]{2,1,0:T(8,128)S(1)} %get-tuple-element.15.refs_3_, ...), custom_call_target="tpu_custom_call" | custom-call | tf_op jit(solution)/shard_map/late_kernel/pallas_call | solution.py:377
  38.5 18.9 %all_to_all.10 = f32[64,8,128]{2,1,0:T(8,128)S(1)} all-to-all(f32[64,8,128]{2,1,0:T(8,128)S(1)} %bitcast.8), channel_id=1, replica_groups=mesh['grp'=8,'mem'=64] {'mem'}, dimensions={0} | all-to-all | bytes 524288 | tf_op jit(solution)/shard_map/all_to_all | solution.py:495
  57.4 1.2 %deliver_kernel.1 = f32[512,128]{1,0:T(8,128)} custom-call(s32[1,64]{1,0:T(1,128)S(1)} %copy-done, f32[512,128]{1,0:T(8,128)S(1)} %bitcast.7), custom_call_target="tpu_custom_call" | custom-call | tf_op jit(solution)/shard_map/deliver_kernel/pallas_call | solution.py:377
  (1 shorter events, 0.0 us)
Async XLA Ops:
  2.0 11.0 %copy-start.1 = (s32[1,6,2048]{2,0,1:T(1,128)S(1)}, s32[1,6,2048]{2,0,1:T(1,128)}, u32[]{:S(2)}) copy-start(s32[1,6,2048]{2,0,1:T(1,128)} %param.5) | copy-start | bytes 147460
  2.0 26.0 %all-to-all-start = ((f32[192,4,128]{2,1,0:T(4,128)}), f32[192,4,128]{2,1,0:T(4,128)S(1)}, u32[]{:S(2)}, u32[]{:S(2)}) async-start(f32[192,4,128]{2,1,0:T(4,128)} %bitcast.9), calls=%async_computation | async-start | bytes 786432 | tf_op jit(solution)/shard_map/all_to_all | solution.py:495
  13.0 0.7 %copy-start = (s32[1,64]{1,0:T(1,128)S(1)}, s32[1,64]{1,0:T(1,128)}, u32[]{:S(2)}) copy-start(s32[1,64]{1,0:T(1,128)} %refs_0_.5) | copy-start | bytes 772
  16.9 7.8 %collective-permute-start = (f32[4,32,128]{2,1,0:T(8,128)S(1)}, f32[4,32,128]{2,1,0:T(8,128)S(1)}, u32[]{:S(2)}, u32[]{:S(2)}) collective-permute-start(f32[4,32,128]{2,1,0:T(8,128)S(1)} %get-tuple-element.15.refs_3_), channel_id=1, source_target_pairs={{1,64},{64,1},{3,66},{66,3},{5,68},{68,5},{7,70},{70,7},{9,72},{72... | collective-permute-start | bytes 196616 | tf_op jit(solution)/shard_map/ppermute | solution.py:508
  28.2 7.7 %collective-permute-start.2 = (f32[192,128]{1,0:T(8,128)S(1)}, f32[192,128]{1,0:T(8,128)S(1)}, u32[]{:S(2)}, u32[]{:S(2)}) collective-permute-start(f32[192,128]{1,0:T(8,128)S(1)} %unpack_kernel.1.packed_ref), channel_id=1, source_target_pairs={{1,64},{64,1},{3,66},{66,3},{5,68},{68,5},{7,70},{70,7},{9,72},{72... | collective-permute-start | bytes 294920 | tf_op jit(solution)/shard_map/ppermute | solution.py:511
  33.6 3.4 %collective-permute-start.1 = (f32[192,128]{1,0:T(8,128)S(1)}, f32[192,128]{1,0:T(8,128)S(1)}, u32[]{:S(2)}, u32[]{:S(2)}) collective-permute-start(f32[192,128]{1,0:T(8,128)S(1)} %unpack_kernel.1.packed_ref), channel_id=1, source_target_pairs={{0,1},{1,0},{2,3},{3,2},{4,5},{5,4},{6,7},{7,6},{8,9},{9,8},{10,11... | collective-permute-start | bytes 294920 | tf_op jit(solution)/shard_map/ppermute | solution.py:512

commit v13 on v9

--- a/solution.py
+++ b/solution.py
@@ -314,13 +314,14 @@
 
 
 def deliver_kernel(where_am_i, *refs):
-    counts_ref, returned_ref, out_ref, turned_ref = refs[-4:]
+    counts_ref, returned_ref, out_hbm, turned_ref, planes_ref, sems = refs[-6:]
     me = where_am_i(refs)
     counts = counts_ref[...]
     owner = iota((1, COLUMNS), 1)
     turn = jnp.sum(jnp.where(owner < me, counts, 0)) & (COLUMNS - 1)
     live = iota((SLOTS, SLOTS), 1) < jnp.sum(jnp.where(owner == me, counts, 0))
     chips = COLUMNS // 2
+    sends = []
     for core in range(2):
         for pair in range(PAIRS):
             held_ref = turned_ref.at[core * PAIRS + pair]
@@ -336,9 +337,13 @@
                 for upper in range(2):
                     row = y * WIDE + upper * TILE
                     z = plane_of(core, pair, upper)
-                    out_ref[pl.ds(y * TILE + z, TILE, stride=TILE * TILE), :] = turned[
-                        row : row + TILE
-                    ]
+                    planes_ref[z, pl.ds(y, TILE, stride=TILE), :] = turned[row : row + TILE]
+            for upper in range(2):
+                z = plane_of(core, pair, upper)
+                sends.append(pltpu.make_async_copy(planes_ref.at[z], out_hbm.at[:, z], sems.at[z]))
+                sends[-1].start()
+    for send in sends:
+        send.wait()
 
 
 def spec(space=pltpu.VMEM):
@@ -459,9 +464,15 @@
     (out,) = run(
         bind(deliver_kernel, me),
         (counts, returned.reshape(COLUMNS * BACK, 128)),
-        [((CELLS, SLOTS), F32)],
-        [pltpu.VMEM((2 * PAIRS, SLOTS, 128), F32)],
+        [((TILE * TILE, TILE, SLOTS), F32)],
+        [
+            pltpu.VMEM((2 * PAIRS, SLOTS, 128), F32),
+            pltpu.VMEM((TILE, TILE * TILE, SLOTS), F32),
+            pltpu.SemaphoreType.DMA((TILE,)),
+        ],
         me,
+        None,
+        [pltpu.HBM],
     )
     return out.reshape(TILE, TILE, TILE, SLOTS)
 

time: 58.9 us -> 58.8 us (level)
  no operation moved by 1% of the time
where the time goes in v13:
time: 58.8 us; the launch traced here: 58.5 us
  starting transfers between devices  23.8 us (40%)
  blocking collectives  18.7 us (32%)
  Pallas kernels  8.9 us (15%)
  waiting for transfers between devices  6.35 us (11%)
  local copies, waits for them, and re-layouts  0.65 us (1%)
    all_to_all x1, blocking collectives, exchange(): return lax.all_to_all(x, 'mem', split_axis=0, concat_axis=0, tiled=True)  18.7 us
    all_to_all x1, starting transfers between devices, exchange(): return lax.all_to_all(x, 'mem', split_axis=0, concat_axis=0, tiled=True)  10.9 us
    pallas_call x6, Pallas kernels, run(): pl.pallas_call(kernel, out_shape=[(pltpu.SMEM if space == pltpu.SMEM else...  8.9 us
    ppermute x1, starting transfers between devices, on_device(): far = lax.ppermute(near, ('grp', 'mem'), across)  5.55 us
    ppermute x1, starting transfers between devices, on_device(): outer = lax.ppermute(own, ('grp', 'mem'), across)  5.37 us
    all_to_all x1, waiting for transfers between devices, exchange(): return lax.all_to_all(x, 'mem', split_axis=0, concat_axis=0, tiled=True)  3.41 us
    ppermute x1, waiting for transfers between devices, on_device(): far = lax.ppermute(near, ('grp', 'mem'), across)  2.23 us
    ppermute x1, starting transfers between devices, on_device(): inner = lax.ppermute(own, 'mem', mates)  1.92 us
  transfers between devices with their start and end apart: 4, of which 3 were waited for; matrix products, arithmetic and copies ran while one was open for 0% of the time, Pallas kernels for 7%

profile of v13, /device:TPU:193, one launch (start us, length us, event | category | flops | bytes accessed | tf_op | source)
XLA Modules:
  0.0 58.5 jit_solution(2175157213680005888)
XLA Ops:
  0.0 2.0 %pack_kernel.1 = f32[768,128]{1,0:T(8,128)} custom-call(s32[1,64]{1,0:T(1,128)} %refs_0_.5, f32[512,128]{1,0:T(8,128)} %bitcast.10), custom_call_target="tpu_custom_call" | custom-call | tf_op jit(solution)/shard_map/pack_kernel/pallas_call | solution.py:361
  2.0 0.0 copy-start.1
  2.0 10.9 %all-to-all-start = ((f32[192,4,128]{2,1,0:T(4,128)}), f32[192,4,128]{2,1,0:T(4,128)S(1)}, u32[]{:S(2)}, u32[]{:S(2)}) async-start(f32[192,4,128]{2,1,0:T(4,128)} %bitcast.9), calls=%async_computation | async-start | bytes 786432 | tf_op jit(solution)/shard_map/all_to_all | solution.py:481
  13.0 0.0 copy-done.1
  13.0 0.0 copy-start
  13.0 0.6 %copy-done = s32[1,64]{1,0:T(1,128)S(1)} copy-done((s32[1,64]{1,0:T(1,128)S(1)}, s32[1,64]{1,0:T(1,128)}, u32[]{:S(2)}) %copy-start) | copy-done | bytes 280
  13.7 3.2 %mask_kernel.1 = (f32[4,32,128]{2,1,0:T(8,128)S(1)}, f32[2,32,128]{2,1,0:T(8,128)S(1)}, s32[6,40]{1,0:T(8,128)S(4)}) custom-call(s32[1,64]{1,0:T(1,128)S(1)} %copy-done, s32[1,6,2048]{2,1,0:T(8,128)S(1)} %copy.4.refs_1_), custom_call_target="tpu_custom_call" | custom-call | flops 4194304 | bytes 131072 | tf_op jit(solution)/shard_map/mask_kernel/pallas_call | solution.py:361
  16.9 5.5 %collective-permute-start = (f32[4,32,128]{2,1,0:T(8,128)S(1)}, f32[4,32,128]{2,1,0:T(8,128)S(1)}, u32[]{:S(2)}, u32[]{:S(2)}) collective-permute-start(f32[4,32,128]{2,1,0:T(8,128)S(1)} %get-tuple-element.15.refs_3_), channel_id=1, source_target_pairs={{1,64},{64,1},{3,66},{66,3},{5,68},{68,5},{7,70},{70,7},{9,72},{72... | collective-permute-start | bytes 196616 | tf_op jit(solution)/shard_map/ppermute | solution.py:494
  22.4 2.2 %collective-permute-done.refs_2_ = f32[4,32,128]{2,1,0:T(8,128)S(1)} collective-permute-done((f32[4,32,128]{2,1,0:T(8,128)S(1)}, f32[4,32,128]{2,1,0:T(8,128)S(1)}, u32[]{:S(2)}, u32[]{:S(2)}) %collective-permute-start) | collective-permute-done | bytes 65568 | tf_op jit(solution)/shard_map/ppermute | solution.py:494
  24.6 3.4 %all-to-all-done = f32[192,4,128]{2,1,0:T(4,128)S(1)} async-done(((f32[192,4,128]{2,1,0:T(4,128)}), f32[192,4,128]{2,1,0:T(4,128)S(1)}, u32[]{:S(2)}, u32[]{:S(2)}) %all-to-all-start) | async-done | bytes 393248 | tf_op jit(solution)/shard_map/all_to_all | solution.py:481
  28.1 0.3 unpack_kernel.1.refs_1_.refs_2_
  28.4 5.4 %collective-permute-start.2 = (f32[8,32,128]{2,1,0:T(8,128)S(1)}, f32[8,32,128]{2,1,0:T(8,128)S(1)}, u32[]{:S(2)}, u32[]{:S(2)}) collective-permute-start(f32[8,32,128]{2,1,0:T(8,128)S(1)} %unpack_kernel.1.refs_1_.refs_2_), channel_id=1, source_target_pairs={{1,64},{64,1},{3,66},{66,3},{5,68},{68,5},{7,70},{70,7},{9,72},{72... | collective-permute-start | bytes 393224 | tf_op jit(solution)/shard_map/ppermute | solution.py:497
  33.7 1.9 %collective-permute-start.1 = (f32[8,32,128]{2,1,0:T(8,128)S(1)}, f32[8,32,128]{2,1,0:T(8,128)S(1)}, u32[]{:S(2)}, u32[]{:S(2)}) collective-permute-start(f32[8,32,128]{2,1,0:T(8,128)S(1)} %unpack_kernel.1.refs_1_.refs_2_), channel_id=1, source_target_pairs={{0,1},{1,0},{2,3},{3,2},{4,5},{5,4},{6,7},{7,6},{8,9},{9,8},{10,11... | collective-permute-start | bytes 393224 | tf_op jit(solution)/shard_map/ppermute | solution.py:498
  35.7 0.7 %collective-permute-done.2.refs_0_ = f32[8,32,128]{2,1,0:T(8,128)S(1)} collective-permute-done((f32[8,32,128]{2,1,0:T(8,128)S(1)}, f32[8,32,128]{2,1,0:T(8,128)S(1)}, u32[]{:S(2)}, u32[]{:S(2)}) %collective-permute-start.2) | collective-permute-done | bytes 131104 | tf_op jit(solution)/shard_map/ppermute | solution.py:497
  36.4 1.0 %early_kernel.1 = (f32[12,32,128]{2,1,0:T(8,128)S(1)}, f32[12,32,128]{2,1,0:T(8,128)S(1)}, f32[12,32,128]{2,1,0:T(8,128)S(1)}, f32[12,32,128]{2,1,0:T(8,128)S(1)}) custom-call(f32[8,32,128]{2,1,0:T(8,128)S(1)} %collective-permute-done.2.refs_0_, f32[8,32,128]{2,1,0:T(8,128)S(1)} %unpack_kernel.1.refs_1_.refs_2_, ...), custom_call_target="tpu_custom_call" | custom-call | flops 4194304 | bytes 1048576 | tf_op jit(solution)/shard_map/early_kernel/pallas_call | solution.py:361
  37.4 0.0 collective-permute-done.1.refs_1_
  37.4 1.3 %late_kernel.1 = f32[256,2,128]{2,1,0:T(2,128)S(1)} custom-call(s32[6,40]{1,0:T(8,128)S(4)} %get-tuple-element.14.table_ref.refs_0_, f32[8,32,128]{2,1,0:T(8,128)S(1)} %collective-permute-done.1.refs_1_, f32[8,32,128]{2,1,0:T(8,128)S(1)} %unpack_kernel.1.refs_1_.refs_2_, f32[4,32,128]{2,1,0:T(8,128)S(1)} %get-tuple-element.15.refs_3_, ...), custom_call_target="tpu_custom_call" | custom-call | tf_op jit(solution)/shard_map/late_kernel/pallas_call | solution.py:361
  38.7 18.7 %all_to_all.10 = f32[64,8,128]{2,1,0:T(8,128)S(1)} all-to-all(f32[64,8,128]{2,1,0:T(8,128)S(1)} %bitcast.8), channel_id=1, replica_groups=mesh['grp'=8,'mem'=64] {'mem'}, dimensions={0} | all-to-all | bytes 524288 | tf_op jit(solution)/shard_map/all_to_all | solution.py:481
  57.4 1.1 %deliver_kernel.1 = f32[64,8,128]{2,1,0:T(8,128)} custom-call(s32[1,64]{1,0:T(1,128)S(1)} %copy-done, f32[512,128]{1,0:T(8,128)S(1)} %bitcast.7), custom_call_target="tpu_custom_call" | custom-call | tf_op jit(solution)/shard_map/deliver_kernel/pallas_call | solution.py:361
  (1 shorter events, 0.0 us)
Async XLA Ops:
  2.0 11.0 %copy-start.1 = (s32[1,6,2048]{2,0,1:T(1,128)S(1)}, s32[1,6,2048]{2,0,1:T(1,128)}, u32[]{:S(2)}) copy-start(s32[1,6,2048]{2,0,1:T(1,128)} %param.5) | copy-start | bytes 147460
  2.0 26.0 %all-to-all-start = ((f32[192,4,128]{2,1,0:T(4,128)}), f32[192,4,128]{2,1,0:T(4,128)S(1)}, u32[]{:S(2)}, u32[]{:S(2)}) async-start(f32[192,4,128]{2,1,0:T(4,128)} %bitcast.9), calls=%async_computation | async-start | bytes 786432 | tf_op jit(solution)/shard_map/all_to_all | solution.py:481
  13.0 0.7 %copy-start = (s32[1,64]{1,0:T(1,128)S(1)}, s32[1,64]{1,0:T(1,128)}, u32[]{:S(2)}) copy-start(s32[1,64]{1,0:T(1,128)} %refs_0_.5) | copy-start | bytes 772
  16.9 7.8 %collective-permute-start = (f32[4,32,128]{2,1,0:T(8,128)S(1)}, f32[4,32,128]{2,1,0:T(8,128)S(1)}, u32[]{:S(2)}, u32[]{:S(2)}) collective-permute-start(f32[4,32,128]{2,1,0:T(8,128)S(1)} %get-tuple-element.15.refs_3_), channel_id=1, source_target_pairs={{1,64},{64,1},{3,66},{66,3},{5,68},{68,5},{7,70},{70,7},{9,72},{72... | collective-permute-start | bytes 196616 | tf_op jit(solution)/shard_map/ppermute | solution.py:494
  28.4 8.0 %collective-permute-start.2 = (f32[8,32,128]{2,1,0:T(8,128)S(1)}, f32[8,32,128]{2,1,0:T(8,128)S(1)}, u32[]{:S(2)}, u32[]{:S(2)}) collective-permute-start(f32[8,32,128]{2,1,0:T(8,128)S(1)} %unpack_kernel.1.refs_1_.refs_2_), channel_id=1, source_target_pairs={{1,64},{64,1},{3,66},{66,3},{5,68},{68,5},{7,70},{70,7},{9,72},{72... | collective-permute-start | bytes 393224 | tf_op jit(solution)/shard_map/ppermute | solution.py:497
  33.7 3.6 %collective-permute-start.1 = (f32[8,32,128]{2,1,0:T(8,128)S(1)}, f32[8,32,128]{2,1,0:T(8,128)S(1)}, u32[]{:S(2)}, u32[]{:S(2)}) collective-permute-start(f32[8,32,128]{2,1,0:T(8,128)S(1)} %unpack_kernel.1.refs_1_.refs_2_), channel_id=1, source_target_pairs={{0,1},{1,0},{2,3},{3,2},{4,5},{5,4},{6,7},{7,6},{8,9},{9,8},{10,11... | collective-permute-start | bytes 393224 | tf_op jit(solution)/shard_map/ppermute | solution.py:498
